TPU v7x, 32 devices: a whole 2x2x4 slice. The times are simulated.
32 devices in a mesh: blk: 8 (over y, x, core), feat: 4 (over z).
Axes of the slice: x: 2, y: 2, z: 4, core: 2. Of those that a mesh axis runs over, the one named last changes fastest.
Arguments:
- features: bfloat16 [24576, 512], P('blk', 'feat'), may hold values from -6 to 6
- tile_values: bfloat16 [1024, 128, 128], P('blk'), may hold values from -0.375 to 0.375
- tile_rows: int32 [1024], P('blk'), may hold values from 0 to 23, as said below
- tile_cols: int32 [1024], P('blk'), may hold values from 0 to 23, as said below
- tile_counts: int32 [64], P('blk'), may hold values from 1 to 16, as said below
- weight: bfloat16 [512, 512], replicated, may hold values from -0.25 to 0.25
- bias: float32 [512], P('feat'), may hold values from -3 to 3
Outputs:
- hidden: bfloat16 [24576, 512], P('blk', 'feat')
Inputs may be any that keep to these rules, and one draw needn't show every extreme that they name: `tile_rows`: the live slots of one node block and offset name distinct pairs of row and column tiles. `tile_cols`: paired with tile_rows slot by slot. `tile_counts`: some block and offset has all 16 slots live in every draw.
All inputs are finite; a program needn't handle non-finite values.
Results may differ from a plain program's by a relative error of at most 0.0049.
Values may be sent and summed in bfloat16 or wider, within the bound.
No kernel may reach another device: no remote copies, remote signals or barrier semaphores. Data moves between devices by JAX's collectives and lax.ppermute only.
A program may use at most 64 MiB of HBM per device.

v0:
```python
import jax
import jax.numpy as jnp
from jax import lax
from jax.sharding import PartitionSpec as P


def shifted(shard, axis, by):
    count = lax.axis_size(axis)
    return lax.ppermute(shard, axis, [(i, (i + by) % count) for i in range(count)])


def pick_tiles(current, wanted, row_tiles, tile_size):
    source = current.reshape(row_tiles, tile_size, current.shape[-1])
    return jnp.take(source, wanted, axis=0)


def add_tiles(totals, picked, offset, values_all, row_ids, tile_counts):
    row_tiles = totals.shape[0]
    slot_count = row_ids.shape[1]
    products = jnp.einsum(
        "ktj,kjf->ktf", values_all[offset], picked, preferred_element_type=jnp.float32
    )
    active = jnp.arange(slot_count) < tile_counts[offset]
    one_hot = (
        (row_ids[offset][None, :] == jnp.arange(row_tiles)[:, None]) & active[None, :]
    ).astype(jnp.float32)
    return totals + jnp.einsum("rk,ktf->rtf", one_hot, products, precision=lax.Precision.HIGHEST)


def body(features, tile_values, tile_rows, tile_cols, tile_counts, weight, bias):
    row_count, col_width = features.shape
    tile_size = tile_values.shape[-1]
    row_tiles = row_count // tile_size
    steps_all = tile_counts.shape[0]
    slot_count = tile_rows.shape[0] // steps_all
    values_all = tile_values.reshape(steps_all, slot_count, tile_size, tile_size)
    row_ids = tile_rows.reshape(steps_all, slot_count)
    col_ids = tile_cols.reshape(steps_all, slot_count)
    totals = jnp.zeros((row_tiles, tile_size, col_width), jnp.float32)
    own_picked = pick_tiles(features, col_ids[0], row_tiles, tile_size)
    totals = add_tiles(totals, own_picked, 0, values_all, row_ids, tile_counts)
    current = features
    for offset in range(1, steps_all):
        current = shifted(current, "blk", 1)
        picked = pick_tiles(current, col_ids[offset], row_tiles, tile_size)
        totals = add_tiles(totals, picked, offset, values_all, row_ids, tile_counts)
    aggregate = totals.reshape(row_count, col_width).astype(jnp.bfloat16)
    out_width = bias.shape[0]
    member = lax.axis_index("feat")
    own_cols = lax.dynamic_slice_in_dim(weight, member * out_width, out_width, 1)
    mixed = jnp.dot(
        lax.all_gather(aggregate, "feat", axis=1, tiled=True),
        own_cols,
        preferred_element_type=jnp.float32,
    )
    return jnp.maximum(mixed + bias[None, :], 0.0).astype(jnp.bfloat16)


def solution(mesh):
    in_specs = (
        P("blk", "feat"),
        P("blk", None, None),
        P("blk"),
        P("blk"),
        P("blk"),
        P(),
        P("feat"),
    )
    out_specs = P("blk", "feat")
    return jax.shard_map(body, mesh=mesh, in_specs=in_specs, out_specs=out_specs, check_vma=False)
```

profile of v0, /device:TPU:0, one launch (start us, length us, event | category | flops | bytes accessed | tf_op | source)
XLA Modules:
  0.0 183.8 jit_solution(13651544771678281297)
XLA Ops:
  9.7 1.8 gather_fusion
  15.4 4.4 %collective-permute-done = bf16[3072,128]{1,0:T(8,128)(2,1)S(1)} collective-permute-done((bf16[3072,128]{1,0:T(8,128)(2,1)}, bf16[3072,128]{1,0:T(8,128)(2,1)S(1)}, u32[]{:S(2)}, u32[]{:S(2)}) %collective-permute-start) | collective-permute-done | bytes 786464 | tf_op jit(solution)/shard_map/ppermute | solution.py:9
  22.1 10.1 %collective-permute-done.1 = bf16[3072,128]{1,0:T(8,128)(2,1)} collective-permute-done((bf16[3072,128]{1,0:T(8,128)(2,1)S(1)}, bf16[3072,128]{1,0:T(8,128)(2,1)}, u32[]{:S(2)}, u32[]{:S(2)}) %collective-permute-start.1) | collective-permute-done | bytes 786464 | tf_op jit(solution)/shard_map/ppermute | solution.py:9
  34.4 1.8 gather_fusion.1
  36.2 8.7 %collective-permute-done.2 = bf16[3072,128]{1,0:T(8,128)(2,1)} collective-permute-done((bf16[3072,128]{1,0:T(8,128)(2,1)}, bf16[3072,128]{1,0:T(8,128)(2,1)}, u32[]{:S(2)}, u32[]{:S(2)}) %collective-permute-start.2) | collective-permute-done | bytes 786464 | tf_op jit(solution)/shard_map/ppermute | solution.py:9
  44.8 2.7 %fusion.29 = f32[16,128,128]{2,1,0:T(8,128)} fusion(bf16[16,128,128]{2,1,0:T(8,128)(2,1)S(1)} %gather_fusion.1, bf16[128,128,128]{2,1,0:T(8,128)(2,1)} %param.10, pred[16]{0:T(512)(128)(4,1)S(1)} %get-tuple-element.46), kind=kOutput, calls=%fused_computation.39 | convolution fusion | flops 67371008 | bytes 2097168 | tf_op jit(solution)/shard_map/ktj,kjf->ktf/dot_general | solution.py:20
  47.5 1.7 copy.10
  49.2 2.1 %fusion.13 = f32[24,128,128]{2,0,1:T(8,128)} fusion(f32[16,128,128]{1,0,2:T(8,128)S(1)} %copy.10, s32[16]{0:T(128)S(1)} %get-tuple-element.35, pred[16]{0:T(512)(128)(4,1)S(1)} %iota_compare_fusion.14), kind=kOutput, calls=%fused_computation.23 | convolution fusion | flops 75498240 | bytes 2621520 | tf_op jit(solution)/shard_map/rk,ktf->rtf/dot_general | solution.py:27
  51.3 1.8 gather_fusion.2
  53.1 2.7 %fusion.27 = f32[16,128,128]{2,1,0:T(8,128)} fusion(bf16[16,128,128]{2,1,0:T(8,128)(2,1)S(1)} %gather_fusion.2, bf16[128,128,128]{2,1,0:T(8,128)(2,1)} %param.10, pred[16]{0:T(512)(128)(4,1)S(1)} %get-tuple-element.44), kind=kOutput, calls=%fused_computation.37 | convolution fusion | flops 67371008 | bytes 2097168 | tf_op jit(solution)/shard_map/ktj,kjf->ktf/dot_general | solution.py:20
  55.8 1.7 copy.11
  57.6 2.0 %fusion.11 = f32[24,128,128]{2,0,1:T(8,128)} fusion(f32[16,128,128]{1,0,2:T(8,128)S(1)} %copy.11, s32[16]{0:T(128)S(1)} %get-tuple-element.34, pred[16]{0:T(512)(128)(4,1)S(1)} %iota_compare_fusion.13), kind=kOutput, calls=%fused_computation.21 | convolution fusion | flops 75498240 | bytes 2621520 | tf_op jit(solution)/shard_map/rk,ktf->rtf/dot_general | solution.py:27
  59.7 1.8 gather_fusion.3
  61.5 2.7 %fusion.25 = f32[16,128,128]{2,1,0:T(8,128)} fusion(bf16[16,128,128]{2,1,0:T(8,128)(2,1)S(1)} %gather_fusion.3, bf16[128,128,128]{2,1,0:T(8,128)(2,1)} %param.10, pred[16]{0:T(512)(128)(4,1)S(1)} %get-tuple-element.42), kind=kOutput, calls=%fused_computation.35 | convolution fusion | flops 67371008 | bytes 2097168 | tf_op jit(solution)/shard_map/ktj,kjf->ktf/dot_general | solution.py:20
  66.0 2.1 %fusion.9 = f32[24,128,128]{2,0,1:T(8,128)} fusion(f32[16,128,128]{1,0,2:T(8,128)S(1)} %copy.12, s32[16]{0:T(128)S(1)} %get-tuple-element.33, pred[16]{0:T(512)(128)(4,1)S(1)} %iota_compare_fusion.12), kind=kOutput, calls=%fused_computation.19 | convolution fusion | flops 75498240 | bytes 2621520 | tf_op jit(solution)/shard_map/rk,ktf->rtf/dot_general | solution.py:27
  68.0 1.8 gather_fusion.4
  70.4 2.7 %fusion.23 = f32[16,128,128]{2,1,0:T(8,128)} fusion(bf16[16,128,128]{2,1,0:T(8,128)(2,1)S(1)} %gather_fusion.4, bf16[128,128,128]{2,1,0:T(8,128)(2,1)} %param.10, pred[16]{0:T(512)(128)(4,1)S(1)} %get-tuple-element.40), kind=kOutput, calls=%fused_computation.33 | convolution fusion | flops 67371008 | bytes 2097168 | tf_op jit(solution)/shard_map/ktj,kjf->ktf/dot_general | solution.py:20
  73.1 1.7 copy.13
  74.9 2.1 %fusion.7 = f32[24,128,128]{2,0,1:T(8,128)} fusion(f32[16,128,128]{1,0,2:T(8,128)S(1)} %copy.13, s32[16]{0:T(128)S(1)} %get-tuple-element.32, pred[16]{0:T(512)(128)(4,1)S(1)} %iota_compare_fusion.11), kind=kOutput, calls=%fused_computation.17 | convolution fusion | flops 75498240 | bytes 2621520 | tf_op jit(solution)/shard_map/rk,ktf->rtf/dot_general | solution.py:27
  77.0 1.8 gather_fusion.5
  78.8 2.7 %fusion.21 = f32[16,128,128]{2,1,0:T(8,128)} fusion(bf16[16,128,128]{2,1,0:T(8,128)(2,1)S(1)} %gather_fusion.5, bf16[128,128,128]{2,1,0:T(8,128)(2,1)} %param.10, pred[16]{0:T(512)(128)(4,1)S(1)} %get-tuple-element.38), kind=kOutput, calls=%fused_computation.31 | convolution fusion | flops 67371008 | bytes 2097168 | tf_op jit(solution)/shard_map/ktj,kjf->ktf/dot_general | solution.py:20
  81.5 1.7 copy.14
  83.2 3.6 %collective-permute-start.6 = (bf16[3072,128]{1,0:T(8,128)(2,1)}, bf16[3072,128]{1,0:T(8,128)(2,1)}, u32[]{:S(2)}, u32[]{:S(2)}) collective-permute-start(bf16[3072,128]{1,0:T(8,128)(2,1)} %collective-permute-done.5), channel_id=1, source_target_pairs={{0,4},{4,8},{8,12},{12,16},{16,20},{20,24},{24,28},{28,0},{1,5},{5... | collective-permute-start | bytes 2359304 | tf_op jit(solution)/shard_map/ppermute | solution.py:9
  86.8 2.0 %fusion.5 = f32[24,128,128]{2,0,1:T(8,128)} fusion(f32[16,128,128]{1,0,2:T(8,128)S(1)} %copy.14, s32[16]{0:T(128)S(1)} %get-tuple-element.31, pred[16]{0:T(512)(128)(4,1)S(1)} %iota_compare_fusion.10), kind=kOutput, calls=%fused_computation.15 | convolution fusion | flops 75498240 | bytes 2621520 | tf_op jit(solution)/shard_map/rk,ktf->rtf/dot_general | solution.py:27
  88.9 1.8 gather_fusion.6
  90.7 2.8 %fusion.19 = f32[16,128,128]{2,1,0:T(8,128)} fusion(bf16[16,128,128]{2,1,0:T(8,128)(2,1)S(1)} %gather_fusion.6, bf16[128,128,128]{2,1,0:T(8,128)(2,1)} %param.10, pred[16]{0:T(512)(128)(4,1)S(1)} %get-tuple-element.50), kind=kOutput, calls=%fused_computation.29 | convolution fusion | flops 67371008 | bytes 2097168 | tf_op jit(solution)/shard_map/ktj,kjf->ktf/dot_general | solution.py:20
  95.2 2.1 %fusion.3 = f32[24,128,128]{2,0,1:T(8,128)} fusion(f32[16,128,128]{1,0,2:T(8,128)S(1)} %copy.15, s32[16]{0:T(128)S(1)} %get-tuple-element.37, pred[16]{0:T(512)(128)(4,1)S(1)} %iota_compare_fusion.9), kind=kOutput, calls=%fused_computation.13 | convolution fusion | flops 75498240 | bytes 2621520 | tf_op jit(solution)/shard_map/rk,ktf->rtf/dot_general | solution.py:27
  97.3 1.8 gather_fusion.7
  99.1 2.7 %fusion.17 = f32[16,128,128]{2,1,0:T(8,128)} fusion(bf16[16,128,128]{2,1,0:T(8,128)(2,1)S(1)} %gather_fusion.7, bf16[128,128,128]{2,1,0:T(8,128)(2,1)} %param.10, pred[16]{0:T(512)(128)(4,1)S(1)} %get-tuple-element.6), kind=kOutput, calls=%fused_computation.27 | convolution fusion | flops 67371008 | bytes 2097168 | tf_op jit(solution)/shard_map/ktj,kjf->ktf/dot_general | solution.py:20
  103.5 5.0 %add_convert_fusion = bf16[24,128,128]{2,0,1:T(8,128)(2,1)S(1)} fusion(f32[24,128,128]{2,0,1:T(8,128)} %fusion.3, f32[24,128,128]{2,0,1:T(8,128)} %fusion.5, f32[24,128,128]{2,0,1:T(8,128)} %fusion.7, f32[24,128,128]{2,0,1:T(8,128)} %fusion.9, f32[24,128,128]{2,0,1:T(8,128)} %fusion.11, f32[24,128,128]{2,0,1:T(8,128)S(1)} %fusion.15, ...), kind=kOutput, calls=%fused_computation.11 | convolution fusion | flops 78643968 | bytes 12845136 | tf_op jit(solution)/shard_map/rk,ktf->rtf/dot_general | solution.py:27
  109.7 63.5 %all-gather.2.cloned.1.call-done = bf16[3072,512]{1,0:T(8,128)(2,1)} async-done(((bf16[3072,128]{1,0:T(8,128)(2,1)}), bf16[3072,512]{1,0:T(8,128)(2,1)}) %all-gather.2.cloned.1.call-update) | async-done | bytes 3145744 | tf_op jit(solution)/shard_map/all_gather | solution.py:52
  173.2 3.8 %fusion.1 = bf16[3072,128]{1,0:T(8,128)(2,1)} fusion(bf16[3072,512]{1,0:T(8,128)(2,1)} %all-gather.2.cloned.1.call-done, f32[128]{0:T(128)S(1)} %copy-done.3, bf16[512,512]{1,0:T(8,128)(2,1)S(1)} %copy-done, s32[]{:T(128)S(6)} %select_n.10), kind=kOutput, calls=%fused_computation.10 | convolution fusion | flops 403832832 | bytes 4063748 | tf_op jit(solution)/shard_map/dot_general | solution.py:51
  (46 shorter events, 18.4 us)
Async XLA Ops:
  6.5 166.7 %copy-start = (bf16[512,512]{1,0:T(8,128)(2,1)S(1)}, bf16[512,512]{1,0:T(8,128)(2,1)}, u32[]{:S(2)}) copy-start(bf16[512,512]{1,0:T(8,128)(2,1)} %param.14) | copy-start | bytes 1572868
  6.5 166.7 %all-gather.2.cloned.1.call-start = ((), (), s32[]{:S(2)}) async-start(), calls=%async_computation | async-start | bytes 3932160 | tf_op jit(solution)/shard_map/all_gather | solution.py:52
  6.5 13.2 %collective-permute-start = (bf16[3072,128]{1,0:T(8,128)(2,1)}, bf16[3072,128]{1,0:T(8,128)(2,1)S(1)}, u32[]{:S(2)}, u32[]{:S(2)}) collective-permute-start(bf16[3072,128]{1,0:T(8,128)(2,1)} %param.9), channel_id=1, source_target_pairs={{0,4},{4,8},{8,12},{12,16},{16,20},{20,24},{24,28},{28,0},{1,5},{5... | collective-permute-start | bytes 2359304 | tf_op jit(solution)/shard_map/ppermute | solution.py:9
  19.8 12.4 %copy-start.1 = (bf16[3072,128]{1,0:T(8,128)(2,1)}, bf16[3072,128]{1,0:T(8,128)(2,1)S(1)}, u32[]{:S(2)}) copy-start(bf16[3072,128]{1,0:T(8,128)(2,1)S(1)} %collective-permute-done) | copy-start | bytes 2359300
  19.8 12.4 %collective-permute-start.1 = (bf16[3072,128]{1,0:T(8,128)(2,1)S(1)}, bf16[3072,128]{1,0:T(8,128)(2,1)}, u32[]{:S(2)}, u32[]{:S(2)}) collective-permute-start(bf16[3072,128]{1,0:T(8,128)(2,1)S(1)} %collective-permute-done), channel_id=1, source_target_pairs={{0,4},{4,8},{8,12},{12,16},{16,20},{20,24},{24,28},{28,0},{1,5},{5... | collective-permute-start | bytes 2359304 | tf_op jit(solution)/shard_map/ppermute | solution.py:9
  22.1 11.3 %copy-start.2 = (s32[128]{0:T(128)S(1)}, s32[128]{0:T(128)}, u32[]{:S(2)}) copy-start(s32[128]{0:T(128)} %param.11) | copy-start | bytes 1540
  32.2 12.6 %collective-permute-start.2 = (bf16[3072,128]{1,0:T(8,128)(2,1)}, bf16[3072,128]{1,0:T(8,128)(2,1)}, u32[]{:S(2)}, u32[]{:S(2)}) collective-permute-start(bf16[3072,128]{1,0:T(8,128)(2,1)} %collective-permute-done.1), channel_id=1, source_target_pairs={{0,4},{4,8},{8,12},{12,16},{16,20},{20,24},{24,28},{28,0},{1,5},{5... | collective-permute-start | bytes 2359304 | tf_op jit(solution)/shard_map/ppermute | solution.py:9
  44.8 12.8 %collective-permute-start.3 = (bf16[3072,128]{1,0:T(8,128)(2,1)}, bf16[3072,128]{1,0:T(8,128)(2,1)}, u32[]{:S(2)}, u32[]{:S(2)}) collective-permute-start(bf16[3072,128]{1,0:T(8,128)(2,1)} %collective-permute-done.2), channel_id=1, source_target_pairs={{0,4},{4,8},{8,12},{12,16},{16,20},{20,24},{24,28},{28,0},{1,5},{5... | collective-permute-start | bytes 2359304 | tf_op jit(solution)/shard_map/ppermute | solution.py:9
  57.6 12.7 %collective-permute-start.4 = (bf16[3072,128]{1,0:T(8,128)(2,1)}, bf16[3072,128]{1,0:T(8,128)(2,1)}, u32[]{:S(2)}, u32[]{:S(2)}) collective-permute-start(bf16[3072,128]{1,0:T(8,128)(2,1)} %collective-permute-done.3), channel_id=1, source_target_pairs={{0,4},{4,8},{8,12},{12,16},{16,20},{20,24},{24,28},{28,0},{1,5},{5... | collective-permute-start | bytes 2359304 | tf_op jit(solution)/shard_map/ppermute | solution.py:9
  70.3 13.0 %collective-permute-start.5 = (bf16[3072,128]{1,0:T(8,128)(2,1)}, bf16[3072,128]{1,0:T(8,128)(2,1)}, u32[]{:S(2)}, u32[]{:S(2)}) collective-permute-start(bf16[3072,128]{1,0:T(8,128)(2,1)} %collective-permute-done.4), channel_id=1, source_target_pairs={{0,4},{4,8},{8,12},{12,16},{16,20},{20,24},{24,28},{28,0},{1,5},{5... | collective-permute-start | bytes 2359304 | tf_op jit(solution)/shard_map/ppermute | solution.py:9
  83.2 14.1 %collective-permute-start.6 = (bf16[3072,128]{1,0:T(8,128)(2,1)}, bf16[3072,128]{1,0:T(8,128)(2,1)}, u32[]{:S(2)}, u32[]{:S(2)}) collective-permute-start(bf16[3072,128]{1,0:T(8,128)(2,1)} %collective-permute-done.5), channel_id=1, source_target_pairs={{0,4},{4,8},{8,12},{12,16},{16,20},{20,24},{24,28},{28,0},{1,5},{5... | collective-permute-start | bytes 2359304 | tf_op jit(solution)/shard_map/ppermute | solution.py:9
  108.6 64.7 %copy-start.3 = (f32[128]{0:T(128)S(1)}, f32[128]{0:T(128)}, u32[]{:S(2)}) copy-start(f32[128]{0:T(128)} %param.15) | copy-start | bytes 1540
Sparse Core Ops, SparseCore 0:
  109.8 63.3 all-gather.1
where the time goes:
time: 185 us; the launch traced here: 184 us
  waiting for transfers between devices  87.2 us (47%)
  matrix products  42.9 us (23%)
  local copies, waits for them, and re-layouts  29.6 us (16%)
  between operations  13.7 us (7%)
  other arithmetic  6.13 us (3%)
  starting transfers between devices  4.29 us (2%)
    all_gather x1, waiting for transfers between devices, body(): lax.all_gather(aggregate, 'feat', axis=1, tiled=True)  63.5 us
    ppermute x7, waiting for transfers between devices, shifted(): lax.ppermute(shard, axis, [(i, (i + by) % count) for i in range(count)])  23.6 us
    dot_general x8, matrix products, add_tiles(): jnp.einsum('ktj,kjf->ktf', values_all[offset], picked, preferred_element_...  20.8 us
    dot_general x8, matrix products, add_tiles(): jnp.einsum('rk,ktf->rtf', one_hot, products, precision=lax.Precision.HIGH...  18.4 us
    gather x8, local copies, waits for them, and re-layouts, pick_tiles(): return jnp.take(source, wanted, axis=0)  14.2 us
    dot_general x8, local copies, waits for them, and re-layouts, add_tiles(): jnp.einsum('ktj,kjf->ktf', values_all[offset], picked, preferred_element_...  12.6 us
    lt x8, other arithmetic, add_tiles(): active = jnp.arange(slot_count) < tile_counts[offset]  5.05 us
    ppermute x7, starting transfers between devices, shifted(): lax.ppermute(shard, axis, [(i, (i + by) % count) for i in range(count)])  4.28 us
  transfers between devices with their start and end apart: 8, of which 5 were waited for; matrix products, arithmetic and copies ran while one was open for 34% of the time, Pallas kernels for 0%

commit v1 on v0

--- a/solution.py
+++ b/solution.py
@@ -1,12 +1,24 @@
+import functools
+
 import jax
 import jax.numpy as jnp
 from jax import lax
+from jax.experimental import pallas as pl
+from jax.experimental.pallas import tpu as pltpu
 from jax.sharding import PartitionSpec as P
+
+CHUNKS = (8, 8, 8)
+UNROLL = 16
 
 
 def shifted(shard, axis, by):
     count = lax.axis_size(axis)
     return lax.ppermute(shard, axis, [(i, (i + by) % count) for i in range(count)])
+
+
+def flipped(shard, axis, bits):
+    count = lax.axis_size(axis)
+    return lax.ppermute(shard, axis, [(i, i ^ bits) for i in range(count)])
 
 
 def pick_tiles(current, wanted, row_tiles, tile_size):
@@ -27,7 +39,7 @@
     return totals + jnp.einsum("rk,ktf->rtf", one_hot, products, precision=lax.Precision.HIGHEST)
 
 
-def body(features, tile_values, tile_rows, tile_cols, tile_counts, weight, bias):
+def ring_body(features, tile_values, tile_rows, tile_cols, tile_counts, weight, bias):
     row_count, col_width = features.shape
     tile_size = tile_values.shape[-1]
     row_tiles = row_count // tile_size
@@ -56,6 +68,190 @@
     return jnp.maximum(mixed + bias[None, :], 0.0).astype(jnp.bfloat16)
 
 
+def plan_kernel(edges, row_tiles, rows, cols, counts, place, order):
+    steps = counts.shape[0]
+    slots = rows.shape[0] // steps
+    where = place[0]
+    for part in range(len(edges) - 1):
+        low, high = edges[part], edges[part + 1]
+
+        def offset_loop(offset, found):
+            source = where ^ ((where + steps - offset) & (steps - 1))
+
+            def slot_loop(k, found):
+                slot = offset * slots + k
+                col = cols[slot]
+                order[part, 0, found] = slot
+                order[part, 1, found] = rows[slot]
+                order[part, 2, found] = source * (high - low) + col - low
+                return found + ((col >= low) & (col < high)).astype(jnp.int32)
+
+            return lax.fori_loop(0, counts[offset], slot_loop, found)
+
+        found = lax.fori_loop(0, steps, offset_loop, 0)
+        for u in range(UNROLL):
+            order[part, 0, found + u] = 0
+            order[part, 1, found + u] = row_tiles
+            order[part, 2, found + u] = 0
+        order[part, 3, 0] = (found + UNROLL - 1) // UNROLL
+
+
+def plan(edges, row_tiles, rows, cols, counts, place):
+    parts = len(edges) - 1
+    room = rows.shape[0] + UNROLL
+    return pl.pallas_call(
+        functools.partial(plan_kernel, edges, row_tiles),
+        out_shape=jax.ShapeDtypeStruct((parts, 4, room), jnp.int32),
+        in_specs=[pl.BlockSpec(memory_space=pltpu.SMEM)] * 4,
+        out_specs=pl.BlockSpec(memory_space=pltpu.SMEM),
+        name="plan",
+    )(rows, cols, counts, place)
+
+
+def mix_kernel(own, pair, across, far, weights, mine, other):
+    width = own.shape[1]
+    total = jnp.dot(own[...], weights[0], preferred_element_type=jnp.float32)
+    for index, piece in enumerate((pair, across, far)):
+        total += jnp.dot(piece[...], weights[index + 1], preferred_element_type=jnp.float32)
+    mine[...] = total[:, :width].astype(mine.dtype)
+    other[...] = total[:, width:].astype(other.dtype)
+
+
+def mix(own, pair, across, far, weights):
+    shape = jax.ShapeDtypeStruct(own.shape, own.dtype)
+    return pl.pallas_call(
+        mix_kernel,
+        out_shape=(shape, shape),
+        in_specs=[pl.BlockSpec(memory_space=pltpu.VMEM)] * 5,
+        out_specs=(pl.BlockSpec(memory_space=pltpu.VMEM),) * 2,
+        compiler_params=pltpu.CompilerParams(vmem_limit_bytes=16 << 20),
+        cost_estimate=pl.CostEstimate(
+            flops=16 * own.size * own.shape[1], bytes_accessed=12 * own.size, transcendentals=0
+        ),
+        name="mix",
+    )(own, pair, across, far, weights)
+
+
+def add_kernel(part, first, last, order, values, bias, *rest):
+    pieces = rest[:8]
+    rest = rest[8:]
+    totals_in = None
+    if not first:
+        totals_in, rest = rest[0], rest[1:]
+    out, held, sem, rest = rest[0], rest[1], rest[2], rest[3:]
+    copies = []
+    for index, piece in enumerate(pieces):
+        size = piece.shape[0]
+        copies.append(
+            pltpu.make_async_copy(piece, held.at[pl.ds(index * size, size)], sem.at[index])
+        )
+        copies[-1].start()
+    totals = rest[0] if last else out
+    if first:
+        totals[...] = jnp.zeros_like(totals)
+    elif last:
+        totals[...] = totals_in[...]
+    for copy in copies:
+        copy.wait()
+
+    def group(g, carry):
+        sums = []
+        for u in range(UNROLL):
+            index = g * UNROLL + u
+            product = jnp.dot(
+                values[order[part, 0, index]],
+                held[order[part, 2, index]],
+                preferred_element_type=jnp.float32,
+            )
+            sums.append((order[part, 1, index], product))
+        for row, product in sums:
+            totals[row] += product
+        return carry
+
+    lax.fori_loop(0, order[part, 3, 0], group, 0)
+    if last:
+        count = out.shape[0]
+
+        def finish(r, carry):
+            out[r] = jnp.maximum(totals[r] + bias[...], 0.0).astype(out.dtype)
+            return carry
+
+        lax.fori_loop(0, count, finish, 0)
+
+
+def add_part(part, last, row_tiles, order, values, bias, pieces, totals):
+    tile = values.shape[-1]
+    width = pieces[0].shape[-1]
+    first = totals is None
+    size = pieces[0].shape[0]
+    vmem = pl.BlockSpec(memory_space=pltpu.VMEM)
+    any_space = pl.BlockSpec(memory_space=pl.ANY)
+    operands = [order, values, bias, *pieces] + ([] if first else [totals])
+    specs = [pl.BlockSpec(memory_space=pltpu.SMEM), vmem, vmem] + [any_space] * 8
+    specs += [] if first else [vmem]
+    total_shape = (row_tiles + 1, tile, width)
+    scratch = [pltpu.VMEM((8 * size, tile, width), jnp.bfloat16), pltpu.SemaphoreType.DMA((8,))]
+    if last:
+        out_shape = jax.ShapeDtypeStruct((row_tiles, tile, width), jnp.bfloat16)
+        scratch.append(pltpu.VMEM(total_shape, jnp.float32))
+    else:
+        out_shape = jax.ShapeDtypeStruct(total_shape, jnp.float32)
+    return pl.pallas_call(
+        functools.partial(add_kernel, part, first, last),
+        out_shape=out_shape,
+        in_specs=specs,
+        out_specs=vmem,
+        scratch_shapes=scratch,
+        input_output_aliases={} if first or last else {len(operands) - 1: 0},
+        compiler_params=pltpu.CompilerParams(vmem_limit_bytes=24 << 20),
+        cost_estimate=pl.CostEstimate(
+            flops=10**9, bytes_accessed=8 << 20, transcendentals=0
+        ),
+        name="add_tiles",
+    )(*operands)
+
+
+def body(features, tile_values, tile_rows, tile_cols, tile_counts, weight, bias):
+    row_count, width = features.shape
+    tile = tile_values.shape[-1]
+    row_tiles = row_count // tile
+    members = lax.axis_size("feat")
+    member = lax.axis_index("feat")
+    place = lax.axis_index("blk").reshape(1).astype(jnp.int32)
+    edges = [0]
+    for count in CHUNKS:
+        edges.append(edges[-1] + count)
+    order = plan(tuple(edges), row_tiles, tile_rows, tile_cols, tile_counts, place)
+    blocks = weight.reshape(members, width, members, width)
+    along = member ^ jnp.array([0, 1, 3, 2])
+    across = member ^ jnp.array([0, 1])
+    weights = blocks[along][:, :, across].reshape(members, width, 2 * width)
+    middle = (member == 1) | (member == 2)
+    inward, inner, outward = [(0, 1), (3, 2)], [(1, 2), (2, 1)], [(1, 0), (2, 3)]
+    totals = None
+    for part in range(len(edges) - 1):
+        own = features[edges[part] * tile : edges[part + 1] * tile]
+        pair = lax.ppermute(own, "feat", inward)
+        opposite = lax.ppermute(own, "feat", inner)
+        far = lax.ppermute(pair, "feat", inner)
+        mine, other = mix(own, pair, opposite, far, weights)
+        given = lax.ppermute(other, "feat", outward)
+        mixed = jnp.where(middle, mine, given)
+        beside = flipped(mixed, "blk", 2)
+        above = flipped(mixed, "blk", 4)
+        if part % 2 == 0:
+            corner = flipped(beside, "blk", 4)
+        else:
+            corner = flipped(above, "blk", 2)
+        pieces = []
+        for piece in (mixed, beside, above, corner):
+            pieces += [piece, flipped(piece, "blk", 1)]
+        pieces = [piece.reshape(-1, tile, width) for piece in pieces]
+        last = part == len(edges) - 2
+        totals = add_part(part, last, row_tiles, order, tile_values, bias[None], pieces, totals)
+    return totals.reshape(row_count, width)
+
+
 def solution(mesh):
     in_specs = (
         P("blk", "feat"),
@@ -67,4 +263,5 @@
         P("feat"),
     )
     out_specs = P("blk", "feat")
-    return jax.shard_map(body, mesh=mesh, in_specs=in_specs, out_specs=out_specs, check_vma=False)
+    chosen = body if mesh.shape["blk"] == 8 and mesh.shape["feat"] == 4 else ring_body
+    return jax.shard_map(chosen, mesh=mesh, in_specs=in_specs, out_specs=out_specs, check_vma=False)

time: 185 us -> 97 us (0.52)
  the two profiles are of different devices: /device:TPU:0 before, /device:TPU:9 now
where the time goes in v1:
time: 97 us; the launch traced here: 96.4 us
  starting transfers between devices  49.4 us (51%)
  waiting for transfers between devices  17.9 us (18%)
  Pallas kernels  16.3 us (17%)
  local copies, waits for them, and re-layouts  11.5 us (12%)
    ppermute x21, starting transfers between devices, flipped(): return lax.ppermute(shard, axis, [(i, i ^ bits) for i in range(count)])  24.7 us
    ppermute x3, starting transfers between devices, body(): far = lax.ppermute(pair, 'feat', inner)  9.37 us
    unnamed x36, local copies, waits for them, and re-layouts  8.8 us
    pallas_call x3, Pallas kernels, add_part(): pl.pallas_call(functools.partial(add_kernel, part, first, last), out_shap...  8.6 us
    ppermute x21, waiting for transfers between devices, flipped(): return lax.ppermute(shard, axis, [(i, i ^ bits) for i in range(count)])  7.99 us
    ppermute x3, starting transfers between devices, body(): opposite = lax.ppermute(own, 'feat', inner)  7.47 us
    ppermute x3, waiting for transfers between devices, body(): far = lax.ppermute(pair, 'feat', inner)  5.89 us
    pallas_call x1, Pallas kernels, plan(): pl.pallas_call(functools.partial(plan_kernel, edges, row_tiles), out_shap...  4.93 us
  transfers between devices with their start and end apart: 33, of which 9 were waited for; matrix products, arithmetic and copies ran while one was open for 2% of the time, Pallas kernels for 13%

profile of v1, /device:TPU:9, one launch (start us, length us, event | category | flops | bytes accessed | tf_op | source)
XLA Modules:
  0.0 96.4 jit_solution(12548099240330540861)
XLA Ops:
  1.2 1.3 %collective-permute-start.22 = (bf16[1024,128]{1,0:T(8,128)(2,1)S(1)}, bf16[1024,128]{1,0:T(8,128)(2,1)S(1)}, u32[]{:S(2)}, u32[]{:S(2)}) collective-permute-start(bf16[1024,128]{1,0:T(8,128)(2,1)S(1)} %get-tuple-element.17.own), channel_id=1, source_target_pairs={{0,1},{3,2},{4,5},{7,6},{8,9},{11,10},{12,13},{15,14},{16,17},{19,... | collective-permute-start | bytes 786440 | tf_op jit(solution)/shard_map/ppermute | solution.py:234
  2.5 3.2 %collective-permute-start.23 = (bf16[1024,128]{1,0:T(8,128)(2,1)S(1)}, bf16[1024,128]{1,0:T(8,128)(2,1)S(1)}, u32[]{:S(2)}, u32[]{:S(2)}) collective-permute-start(bf16[1024,128]{1,0:T(8,128)(2,1)S(1)} %get-tuple-element.17.own), channel_id=1, source_target_pairs={{1,2},{2,1},{5,6},{6,5},{9,10},{10,9},{13,14},{14,13},{17,18},{18,... | collective-permute-start | bytes 786440 | tf_op jit(solution)/shard_map/ppermute | solution.py:235
  5.7 1.3 %collective-permute-start.11 = (bf16[1024,128]{1,0:T(8,128)(2,1)S(1)}, bf16[1024,128]{1,0:T(8,128)(2,1)S(1)}, u32[]{:S(2)}, u32[]{:S(2)}) collective-permute-start(bf16[1024,128]{1,0:T(8,128)(2,1)S(1)} %get-tuple-element.19.own), channel_id=1, source_target_pairs={{0,1},{3,2},{4,5},{7,6},{8,9},{11,10},{12,13},{15,14},{16,17},{19,... | collective-permute-start | bytes 786440 | tf_op jit(solution)/shard_map/ppermute | solution.py:234
  7.0 2.1 %collective-permute-start.12 = (bf16[1024,128]{1,0:T(8,128)(2,1)S(1)}, bf16[1024,128]{1,0:T(8,128)(2,1)S(1)}, u32[]{:S(2)}, u32[]{:S(2)}) collective-permute-start(bf16[1024,128]{1,0:T(8,128)(2,1)S(1)} %get-tuple-element.19.own), channel_id=1, source_target_pairs={{1,2},{2,1},{5,6},{6,5},{9,10},{10,9},{13,14},{14,13},{17,18},{18,... | collective-permute-start | bytes 786440 | tf_op jit(solution)/shard_map/ppermute | solution.py:235
  9.1 1.3 %collective-permute-start = (bf16[1024,128]{1,0:T(8,128)(2,1)S(1)}, bf16[1024,128]{1,0:T(8,128)(2,1)S(1)}, u32[]{:S(2)}, u32[]{:S(2)}) collective-permute-start(bf16[1024,128]{1,0:T(8,128)(2,1)S(1)} %get-tuple-element.18.own), channel_id=1, source_target_pairs={{0,1},{3,2},{4,5},{7,6},{8,9},{11,10},{12,13},{15,14},{16,17},{19,... | collective-permute-start | bytes 786440 | tf_op jit(solution)/shard_map/ppermute | solution.py:234
  11.1 3.2 %collective-permute-start.24 = (bf16[1024,128]{1,0:T(8,128)(2,1)S(1)}, bf16[1024,128]{1,0:T(8,128)(2,1)S(1)}, u32[]{:S(2)}, u32[]{:S(2)}) collective-permute-start(bf16[1024,128]{1,0:T(8,128)(2,1)S(1)} %collective-permute-done.22.pair), channel_id=1, source_target_pairs={{1,2},{2,1},{5,6},{6,5},{9,10},{10,9},{13,14},{14,13},{17,18},{18,... | collective-permute-start | bytes 786440 | tf_op jit(solution)/shard_map/ppermute | solution.py:236
  16.0 3.1 %collective-permute-start.13 = (bf16[1024,128]{1,0:T(8,128)(2,1)S(1)}, bf16[1024,128]{1,0:T(8,128)(2,1)S(1)}, u32[]{:S(2)}, u32[]{:S(2)}) collective-permute-start(bf16[1024,128]{1,0:T(8,128)(2,1)S(1)} %collective-permute-done.11.pair), channel_id=1, source_target_pairs={{1,2},{2,1},{5,6},{6,5},{9,10},{10,9},{13,14},{14,13},{17,18},{18,... | collective-permute-start | bytes 786440 | tf_op jit(solution)/shard_map/ppermute | solution.py:236
  19.2 2.2 %collective-permute-start.1 = (bf16[1024,128]{1,0:T(8,128)(2,1)S(1)}, bf16[1024,128]{1,0:T(8,128)(2,1)S(1)}, u32[]{:S(2)}, u32[]{:S(2)}) collective-permute-start(bf16[1024,128]{1,0:T(8,128)(2,1)S(1)} %get-tuple-element.18.own), channel_id=1, source_target_pairs={{1,2},{2,1},{5,6},{6,5},{9,10},{10,9},{13,14},{14,13},{17,18},{18,... | collective-permute-start | bytes 786440 | tf_op jit(solution)/shard_map/ppermute | solution.py:235
  21.6 3.1 %collective-permute-start.2 = (bf16[1024,128]{1,0:T(8,128)(2,1)S(1)}, bf16[1024,128]{1,0:T(8,128)(2,1)S(1)}, u32[]{:S(2)}, u32[]{:S(2)}) collective-permute-start(bf16[1024,128]{1,0:T(8,128)(2,1)S(1)} %collective-permute-done.pair), channel_id=1, source_target_pairs={{1,2},{2,1},{5,6},{6,5},{9,10},{10,9},{13,14},{14,13},{17,18},{18,... | collective-permute-start | bytes 786440 | tf_op jit(solution)/shard_map/ppermute | solution.py:236
  24.7 1.4 %mix.5 = (bf16[1024,128]{1,0:T(8,128)(2,1)S(1)}, bf16[1024,128]{1,0:T(8,128)(2,1)}) custom-call(bf16[1024,128]{1,0:T(8,128)(2,1)S(1)} %get-tuple-element.17.own, bf16[1024,128]{1,0:T(8,128)(2,1)S(1)} %collective-permute-done.22.pair, bf16[1024,128]{1,0:T(8,128)(2,1)S(1)} %collective-permute-done.23.across, ...), custom_call_target="tpu_custom_call" | custom-call | flops 268435456 | bytes 1572864 | tf_op jit(solution)/shard_map/mix/pallas_call | solution.py:122
  26.8 1.4 %collective-permute-start.25 = (bf16[1024,128]{1,0:T(8,128)(2,1)}, bf16[1024,128]{1,0:T(8,128)(2,1)S(1)}, u32[]{:S(2)}, u32[]{:S(2)}) collective-permute-start(bf16[1024,128]{1,0:T(8,128)(2,1)} %get-tuple-element.16), channel_id=1, source_target_pairs={{1,0},{2,3},{5,4},{6,7},{9,8},{10,11},{13,12},{14,15},{17,16},{18,... | collective-permute-start | bytes 786440 | tf_op jit(solution)/shard_map/ppermute | solution.py:238
  29.3 1.3 %collective-permute-start.14 = (bf16[1024,128]{1,0:T(8,128)(2,1)S(1)}, bf16[1024,128]{1,0:T(8,128)(2,1)S(1)}, u32[]{:S(2)}, u32[]{:S(2)}) collective-permute-start(bf16[1024,128]{1,0:T(8,128)(2,1)S(1)} %get-tuple-element.14), channel_id=1, source_target_pairs={{1,0},{2,3},{5,4},{6,7},{9,8},{10,11},{13,12},{14,15},{17,16},{18,... | collective-permute-start | bytes 786440 | tf_op jit(solution)/shard_map/ppermute | solution.py:238
  30.6 3.6 %collective-permute-done.1.across = bf16[1024,128]{1,0:T(8,128)(2,1)S(1)} collective-permute-done((bf16[1024,128]{1,0:T(8,128)(2,1)S(1)}, bf16[1024,128]{1,0:T(8,128)(2,1)S(1)}, u32[]{:S(2)}, u32[]{:S(2)}) %collective-permute-start.1) | collective-permute-done | bytes 262176 | tf_op jit(solution)/shard_map/ppermute | solution.py:235
  34.2 5.6 %collective-permute-done.2.far = bf16[1024,128]{1,0:T(8,128)(2,1)S(1)} collective-permute-done((bf16[1024,128]{1,0:T(8,128)(2,1)S(1)}, bf16[1024,128]{1,0:T(8,128)(2,1)S(1)}, u32[]{:S(2)}, u32[]{:S(2)}) %collective-permute-start.2) | collective-permute-done | bytes 262176 | tf_op jit(solution)/shard_map/ppermute | solution.py:236
  40.5 1.3 %collective-permute-start.3 = (bf16[1024,128]{1,0:T(8,128)(2,1)S(1)}, bf16[1024,128]{1,0:T(8,128)(2,1)S(1)}, u32[]{:S(2)}, u32[]{:S(2)}) collective-permute-start(bf16[1024,128]{1,0:T(8,128)(2,1)S(1)} %get-tuple-element.12), channel_id=1, source_target_pairs={{1,0},{2,3},{5,4},{6,7},{9,8},{10,11},{13,12},{14,15},{17,16},{18,... | collective-permute-start | bytes 786440 | tf_op jit(solution)/shard_map/ppermute | solution.py:238
  41.9 1.3 %collective-permute-start.27 = (bf16[1024,128]{1,0:T(8,128)(2,1)S(1)}, bf16[1024,128]{1,0:T(8,128)(2,1)S(1)}, u32[]{:S(2)}, u32[]{:S(2)}) collective-permute-start(bf16[1024,128]{1,0:T(8,128)(2,1)S(1)} %broadcast_select_fusion), channel_id=1, source_target_pairs={{0,8},{4,12},{8,0},{12,4},{16,24},{20,28},{24,16},{28,20},{1,9},{5... | collective-permute-start | bytes 786440 | tf_op jit(solution)/shard_map/ppermute | solution.py:21
  43.1 1.2 %collective-permute-start.29 = (bf16[1024,128]{1,0:T(8,128)(2,1)S(1)}, bf16[1024,128]{1,0:T(8,128)(2,1)S(1)}, u32[]{:S(2)}, u32[]{:S(2)}) collective-permute-start(bf16[1024,128]{1,0:T(8,128)(2,1)S(1)} %broadcast_select_fusion), channel_id=1, source_target_pairs={{0,16},{4,20},{8,24},{12,28},{16,0},{20,4},{24,8},{28,12},{1,17},{... | collective-permute-start | bytes 786440 | tf_op jit(solution)/shard_map/ppermute | solution.py:21
  44.4 2.0 %collective-permute-start.26 = (bf16[1024,128]{1,0:T(8,128)(2,1)S(1)}, bf16[1024,128]{1,0:T(8,128)(2,1)S(1)}, u32[]{:S(2)}, u32[]{:S(2)}) collective-permute-start(bf16[1024,128]{1,0:T(8,128)(2,1)S(1)} %broadcast_select_fusion), channel_id=1, source_target_pairs={{0,4},{4,0},{8,12},{12,8},{16,20},{20,16},{24,28},{28,24},{1,5},{5... | collective-permute-start | bytes 786440 | tf_op jit(solution)/shard_map/ppermute | solution.py:21
  48.3 3.1 %collective-permute-start.15 = (bf16[1024,128]{1,0:T(8,128)(2,1)S(1)}, bf16[1024,128]{1,0:T(8,128)(2,1)S(1)}, u32[]{:S(2)}, u32[]{:S(2)}) collective-permute-start(bf16[1024,128]{1,0:T(8,128)(2,1)S(1)} %broadcast_select_fusion.1), channel_id=1, source_target_pairs={{0,4},{4,0},{8,12},{12,8},{16,20},{20,16},{24,28},{28,24},{1,5},{5... | collective-permute-start | bytes 786440 | tf_op jit(solution)/shard_map/ppermute | solution.py:21
  51.5 1.8 %collective-permute-start.5 = (bf16[1024,128]{1,0:T(8,128)(2,1)S(1)}, bf16[1024,128]{1,0:T(8,128)(2,1)S(1)}, u32[]{:S(2)}, u32[]{:S(2)}) collective-permute-start(bf16[1024,128]{1,0:T(8,128)(2,1)S(1)} %broadcast_select_fusion.2), channel_id=1, source_target_pairs={{0,8},{4,12},{8,0},{12,4},{16,24},{20,28},{24,16},{28,20},{1,9},{5... | collective-permute-start | bytes 786440 | tf_op jit(solution)/shard_map/ppermute | solution.py:21
  53.2 1.2 %collective-permute-start.7 = (bf16[1024,128]{1,0:T(8,128)(2,1)S(1)}, bf16[1024,128]{1,0:T(8,128)(2,1)S(1)}, u32[]{:S(2)}, u32[]{:S(2)}) collective-permute-start(bf16[1024,128]{1,0:T(8,128)(2,1)S(1)} %broadcast_select_fusion.2), channel_id=1, source_target_pairs={{0,16},{4,20},{8,24},{12,28},{16,0},{20,4},{24,8},{28,12},{1,17},{... | collective-permute-start | bytes 786440 | tf_op jit(solution)/shard_map/ppermute | solution.py:21
  56.1 4.0 %collective-permute-start.28 = (bf16[1024,128]{1,0:T(8,128)(2,1)S(1)}, bf16[1024,128]{1,0:T(8,128)(2,1)S(1)}, u32[]{:S(2)}, u32[]{:S(2)}) collective-permute-start(bf16[1024,128]{1,0:T(8,128)(2,1)S(1)} %collective-permute-done.27), channel_id=1, source_target_pairs={{0,4},{4,0},{8,12},{12,8},{16,20},{20,16},{24,28},{28,24},{1,5},{5... | collective-permute-start | bytes 786440 | tf_op jit(solution)/shard_map/ppermute | solution.py:21
  61.6 2.5 %collective-permute-start.19 = (bf16[1024,128]{1,0:T(8,128)(2,1)S(1)}, bf16[1024,128]{1,0:T(8,128)(2,1)S(1)}, u32[]{:S(2)}, u32[]{:S(2)}) collective-permute-start(bf16[1024,128]{1,0:T(8,128)(2,1)S(1)} %collective-permute-done.18), channel_id=1, source_target_pairs={{0,4},{4,0},{8,12},{12,8},{16,20},{20,16},{24,28},{28,24},{1,5},{5... | collective-permute-start | bytes 786440 | tf_op jit(solution)/shard_map/ppermute | solution.py:21
  64.9 2.5 %collective-permute-done.31 = bf16[1024,128]{1,0:T(8,128)(2,1)S(1)} collective-permute-done((bf16[1024,128]{1,0:T(8,128)(2,1)S(1)}, bf16[1024,128]{1,0:T(8,128)(2,1)S(1)}, u32[]{:S(2)}, u32[]{:S(2)}) %collective-permute-start.31) | collective-permute-done | bytes 262176 | tf_op jit(solution)/shard_map/ppermute | solution.py:21
  67.4 1.4 %collective-permute-start.17 = (bf16[1024,128]{1,0:T(8,128)(2,1)S(1)}, bf16[1024,128]{1,0:T(8,128)(2,1)S(1)}, u32[]{:S(2)}, u32[]{:S(2)}) collective-permute-start(bf16[1024,128]{1,0:T(8,128)(2,1)S(1)} %collective-permute-done.16), channel_id=1, source_target_pairs={{0,4},{4,0},{8,12},{12,8},{16,20},{20,16},{24,28},{28,24},{1,5},{5... | collective-permute-start | bytes 786440 | tf_op jit(solution)/shard_map/ppermute | solution.py:21
  69.4 1.2 %collective-permute-start.9 = (bf16[1024,128]{1,0:T(8,128)(2,1)S(1)}, bf16[1024,128]{1,0:T(8,128)(2,1)S(1)}, u32[]{:S(2)}, u32[]{:S(2)}) collective-permute-start(bf16[1024,128]{1,0:T(8,128)(2,1)S(1)} %collective-permute-done.5), channel_id=1, source_target_pairs={{0,16},{4,20},{8,24},{12,28},{16,0},{20,4},{24,8},{28,12},{1,17},{... | collective-permute-start | bytes 786440 | tf_op jit(solution)/shard_map/ppermute | solution.py:21
  73.1 4.2 %collective-permute-done.9 = bf16[1024,128]{1,0:T(8,128)(2,1)S(1)} collective-permute-done((bf16[1024,128]{1,0:T(8,128)(2,1)S(1)}, bf16[1024,128]{1,0:T(8,128)(2,1)S(1)}, u32[]{:S(2)}, u32[]{:S(2)}) %collective-permute-start.9) | collective-permute-done | bytes 262176 | tf_op jit(solution)/shard_map/ppermute | solution.py:21
  78.8 4.9 %plan.1.order = s32[3,4,144]{2,1,0:T(4,128)} custom-call(s32[128]{0:T(128)} %rows.1, s32[128]{0:T(128)} %cols.1, s32[8]{0:T(128)} %counts.1, s32[1]{0:T(128)} %bitcast.place), custom_call_target="tpu_custom_call" | custom-call | tf_op jit(solution)/shard_map/plan/pallas_call | solution.py:102
  83.8 2.2 %copy-done = bf16[128,128,128]{2,1,0:T(8,128)(2,1)S(1)} copy-done((bf16[128,128,128]{2,1,0:T(8,128)(2,1)S(1)}, bf16[128,128,128]{2,1,0:T(8,128)(2,1)}, u32[]{:S(2)}) %copy-start) | copy-done | bytes 4194328
  87.7 2.0 %add_tiles.3.rest_8_ = f32[25,128,128]{2,1,0:T(8,128)S(1)} custom-call(s32[3,4,144]{2,1,0:T(4,128)S(1)} %copy-done.15, bf16[128,128,128]{2,1,0:T(8,128)(2,1)S(1)} %copy-done, f32[1,128]{1,0:T(1,128)S(1)} %bitcast.52, bf16[8,128,128]{2,1,0:T(8,128)(2,1)S(1)} %bitcast.33, bf16[8,128,128]{2,1,0:T(8,128)(2,1)S(1)} %bitcast.38, ...), custom_call_target="tpu_custom_call" | custom-call | flops 1000000000 | bytes 8388608 | tf_op jit(solution)/shard_map/add_tiles/pallas_call | solution.py:199
  89.7 2.9 %add_tiles.4.rest_8_ = f32[25,128,128]{2,1,0:T(8,128)S(1)} custom-call(s32[3,4,144]{2,1,0:T(4,128)S(1)} %copy-done.15, bf16[128,128,128]{2,1,0:T(8,128)(2,1)S(1)} %copy-done, f32[1,128]{1,0:T(1,128)S(1)} %bitcast.53, bf16[8,128,128]{2,1,0:T(8,128)(2,1)S(1)} %bitcast.35, bf16[8,128,128]{2,1,0:T(8,128)(2,1)S(1)} %bitcast.49, ...), custom_call_target="tpu_custom_call", output_to_operand_aliasing={{}: (11, {})} | custom-call | flops 1000000000 | bytes 8388608 | tf_op jit(solution)/shard_map/add_tiles/pallas_call | solution.py:199
  92.6 3.7 %add_tiles.5 = bf16[24,128,128]{2,1,0:T(8,128)(2,1)} custom-call(s32[3,4,144]{2,1,0:T(4,128)S(1)} %copy-done.15, bf16[128,128,128]{2,1,0:T(8,128)(2,1)S(1)} %copy-done, f32[1,128]{1,0:T(1,128)S(1)} %bitcast.54, bf16[8,128,128]{2,1,0:T(8,128)(2,1)S(1)} %bitcast.34, bf16[8,128,128]{2,1,0:T(8,128)(2,1)S(1)} %bitcast.45, bf16[8,128,128]{2,1,0:T(8,128)(2,1)S(1)} %bitcast.39, ...), custom_call_target="tpu_custom_call" | custom-call | flops 1000000000 | bytes 8388608 | tf_op jit(solution)/shard_map/add_tiles/pallas_call | solution.py:199
  (90 shorter events, 18.4 us)
Async XLA Ops:
  1.2 9.9 %collective-permute-start.22 = (bf16[1024,128]{1,0:T(8,128)(2,1)S(1)}, bf16[1024,128]{1,0:T(8,128)(2,1)S(1)}, u32[]{:S(2)}, u32[]{:S(2)}) collective-permute-start(bf16[1024,128]{1,0:T(8,128)(2,1)S(1)} %get-tuple-element.17.own), channel_id=1, source_target_pairs={{0,1},{3,2},{4,5},{7,6},{8,9},{11,10},{12,13},{15,14},{16,17},{19,... | collective-permute-start | bytes 786440 | tf_op jit(solution)/shard_map/ppermute | solution.py:234
  2.5 16.6 %collective-permute-start.23 = (bf16[1024,128]{1,0:T(8,128)(2,1)S(1)}, bf16[1024,128]{1,0:T(8,128)(2,1)S(1)}, u32[]{:S(2)}, u32[]{:S(2)}) collective-permute-start(bf16[1024,128]{1,0:T(8,128)(2,1)S(1)} %get-tuple-element.17.own), channel_id=1, source_target_pairs={{1,2},{2,1},{5,6},{6,5},{9,10},{10,9},{13,14},{14,13},{17,18},{18,... | collective-permute-start | bytes 786440 | tf_op jit(solution)/shard_map/ppermute | solution.py:235
  5.7 10.3 %collective-permute-start.11 = (bf16[1024,128]{1,0:T(8,128)(2,1)S(1)}, bf16[1024,128]{1,0:T(8,128)(2,1)S(1)}, u32[]{:S(2)}, u32[]{:S(2)}) collective-permute-start(bf16[1024,128]{1,0:T(8,128)(2,1)S(1)} %get-tuple-element.19.own), channel_id=1, source_target_pairs={{0,1},{3,2},{4,5},{7,6},{8,9},{11,10},{12,13},{15,14},{16,17},{19,... | collective-permute-start | bytes 786440 | tf_op jit(solution)/shard_map/ppermute | solution.py:234
  7.0 21.2 %collective-permute-start.12 = (bf16[1024,128]{1,0:T(8,128)(2,1)S(1)}, bf16[1024,128]{1,0:T(8,128)(2,1)S(1)}, u32[]{:S(2)}, u32[]{:S(2)}) collective-permute-start(bf16[1024,128]{1,0:T(8,128)(2,1)S(1)} %get-tuple-element.19.own), channel_id=1, source_target_pairs={{1,2},{2,1},{5,6},{6,5},{9,10},{10,9},{13,14},{14,13},{17,18},{18,... | collective-permute-start | bytes 786440 | tf_op jit(solution)/shard_map/ppermute | solution.py:235
  9.1 12.5 %collective-permute-start = (bf16[1024,128]{1,0:T(8,128)(2,1)S(1)}, bf16[1024,128]{1,0:T(8,128)(2,1)S(1)}, u32[]{:S(2)}, u32[]{:S(2)}) collective-permute-start(bf16[1024,128]{1,0:T(8,128)(2,1)S(1)} %get-tuple-element.18.own), channel_id=1, source_target_pairs={{0,1},{3,2},{4,5},{7,6},{8,9},{11,10},{12,13},{15,14},{16,17},{19,... | collective-permute-start | bytes 786440 | tf_op jit(solution)/shard_map/ppermute | solution.py:234
  11.1 13.6 %collective-permute-start.24 = (bf16[1024,128]{1,0:T(8,128)(2,1)S(1)}, bf16[1024,128]{1,0:T(8,128)(2,1)S(1)}, u32[]{:S(2)}, u32[]{:S(2)}) collective-permute-start(bf16[1024,128]{1,0:T(8,128)(2,1)S(1)} %collective-permute-done.22.pair), channel_id=1, source_target_pairs={{1,2},{2,1},{5,6},{6,5},{9,10},{10,9},{13,14},{14,13},{17,18},{18,... | collective-permute-start | bytes 786440 | tf_op jit(solution)/shard_map/ppermute | solution.py:236
  16.0 12.5 %collective-permute-start.13 = (bf16[1024,128]{1,0:T(8,128)(2,1)S(1)}, bf16[1024,128]{1,0:T(8,128)(2,1)S(1)}, u32[]{:S(2)}, u32[]{:S(2)}) collective-permute-start(bf16[1024,128]{1,0:T(8,128)(2,1)S(1)} %collective-permute-done.11.pair), channel_id=1, source_target_pairs={{1,2},{2,1},{5,6},{6,5},{9,10},{10,9},{13,14},{14,13},{17,18},{18,... | collective-permute-start | bytes 786440 | tf_op jit(solution)/shard_map/ppermute | solution.py:236
  19.2 15.0 %collective-permute-start.1 = (bf16[1024,128]{1,0:T(8,128)(2,1)S(1)}, bf16[1024,128]{1,0:T(8,128)(2,1)S(1)}, u32[]{:S(2)}, u32[]{:S(2)}) collective-permute-start(bf16[1024,128]{1,0:T(8,128)(2,1)S(1)} %get-tuple-element.18.own), channel_id=1, source_target_pairs={{1,2},{2,1},{5,6},{6,5},{9,10},{10,9},{13,14},{14,13},{17,18},{18,... | collective-permute-start | bytes 786440 | tf_op jit(solution)/shard_map/ppermute | solution.py:235
  21.6 18.2 %collective-permute-start.2 = (bf16[1024,128]{1,0:T(8,128)(2,1)S(1)}, bf16[1024,128]{1,0:T(8,128)(2,1)S(1)}, u32[]{:S(2)}, u32[]{:S(2)}) collective-permute-start(bf16[1024,128]{1,0:T(8,128)(2,1)S(1)} %collective-permute-done.pair), channel_id=1, source_target_pairs={{1,2},{2,1},{5,6},{6,5},{9,10},{10,9},{13,14},{14,13},{17,18},{18,... | collective-permute-start | bytes 786440 | tf_op jit(solution)/shard_map/ppermute | solution.py:236
  26.8 15.0 %collective-permute-start.25 = (bf16[1024,128]{1,0:T(8,128)(2,1)}, bf16[1024,128]{1,0:T(8,128)(2,1)S(1)}, u32[]{:S(2)}, u32[]{:S(2)}) collective-permute-start(bf16[1024,128]{1,0:T(8,128)(2,1)} %get-tuple-element.16), channel_id=1, source_target_pairs={{1,0},{2,3},{5,4},{6,7},{9,8},{10,11},{13,12},{14,15},{17,16},{18,... | collective-permute-start | bytes 786440 | tf_op jit(solution)/shard_map/ppermute | solution.py:238
  29.3 17.1 %collective-permute-start.14 = (bf16[1024,128]{1,0:T(8,128)(2,1)S(1)}, bf16[1024,128]{1,0:T(8,128)(2,1)S(1)}, u32[]{:S(2)}, u32[]{:S(2)}) collective-permute-start(bf16[1024,128]{1,0:T(8,128)(2,1)S(1)} %get-tuple-element.14), channel_id=1, source_target_pairs={{1,0},{2,3},{5,4},{6,7},{9,8},{10,11},{13,12},{14,15},{17,16},{18,... | collective-permute-start | bytes 786440 | tf_op jit(solution)/shard_map/ppermute | solution.py:238
  40.5 6.2 %collective-permute-start.3 = (bf16[1024,128]{1,0:T(8,128)(2,1)S(1)}, bf16[1024,128]{1,0:T(8,128)(2,1)S(1)}, u32[]{:S(2)}, u32[]{:S(2)}) collective-permute-start(bf16[1024,128]{1,0:T(8,128)(2,1)S(1)} %get-tuple-element.12), channel_id=1, source_target_pairs={{1,0},{2,3},{5,4},{6,7},{9,8},{10,11},{13,12},{14,15},{17,16},{18,... | collective-permute-start | bytes 786440 | tf_op jit(solution)/shard_map/ppermute | solution.py:238
  41.9 6.4 %collective-permute-start.27 = (bf16[1024,128]{1,0:T(8,128)(2,1)S(1)}, bf16[1024,128]{1,0:T(8,128)(2,1)S(1)}, u32[]{:S(2)}, u32[]{:S(2)}) collective-permute-start(bf16[1024,128]{1,0:T(8,128)(2,1)S(1)} %broadcast_select_fusion), channel_id=1, source_target_pairs={{0,8},{4,12},{8,0},{12,4},{16,24},{20,28},{24,16},{28,20},{1,9},{5... | collective-permute-start | bytes 786440 | tf_op jit(solution)/shard_map/ppermute | solution.py:21
  43.1 8.3 %collective-permute-start.29 = (bf16[1024,128]{1,0:T(8,128)(2,1)S(1)}, bf16[1024,128]{1,0:T(8,128)(2,1)S(1)}, u32[]{:S(2)}, u32[]{:S(2)}) collective-permute-start(bf16[1024,128]{1,0:T(8,128)(2,1)S(1)} %broadcast_select_fusion), channel_id=1, source_target_pairs={{0,16},{4,20},{8,24},{12,28},{16,0},{20,4},{24,8},{28,12},{1,17},{... | collective-permute-start | bytes 786440 | tf_op jit(solution)/shard_map/ppermute | solution.py:21
  44.4 8.9 %collective-permute-start.26 = (bf16[1024,128]{1,0:T(8,128)(2,1)S(1)}, bf16[1024,128]{1,0:T(8,128)(2,1)S(1)}, u32[]{:S(2)}, u32[]{:S(2)}) collective-permute-start(bf16[1024,128]{1,0:T(8,128)(2,1)S(1)} %broadcast_select_fusion), channel_id=1, source_target_pairs={{0,4},{4,0},{8,12},{12,8},{16,20},{20,16},{24,28},{28,24},{1,5},{5... | collective-permute-start | bytes 786440 | tf_op jit(solution)/shard_map/ppermute | solution.py:21
  46.4 8.4 %collective-permute-start.18 = (bf16[1024,128]{1,0:T(8,128)(2,1)S(1)}, bf16[1024,128]{1,0:T(8,128)(2,1)S(1)}, u32[]{:S(2)}, u32[]{:S(2)}) collective-permute-start(bf16[1024,128]{1,0:T(8,128)(2,1)S(1)} %broadcast_select_fusion.1), channel_id=1, source_target_pairs={{0,16},{4,20},{8,24},{12,28},{16,0},{20,4},{24,8},{28,12},{1,17},{... | collective-permute-start | bytes 786440 | tf_op jit(solution)/shard_map/ppermute | solution.py:21
  46.7 9.4 %collective-permute-start.16 = (bf16[1024,128]{1,0:T(8,128)(2,1)S(1)}, bf16[1024,128]{1,0:T(8,128)(2,1)S(1)}, u32[]{:S(2)}, u32[]{:S(2)}) collective-permute-start(bf16[1024,128]{1,0:T(8,128)(2,1)S(1)} %broadcast_select_fusion.1), channel_id=1, source_target_pairs={{0,8},{4,12},{8,0},{12,4},{16,24},{20,28},{24,16},{28,20},{1,9},{5... | collective-permute-start | bytes 786440 | tf_op jit(solution)/shard_map/ppermute | solution.py:21
  48.3 11.8 %collective-permute-start.15 = (bf16[1024,128]{1,0:T(8,128)(2,1)S(1)}, bf16[1024,128]{1,0:T(8,128)(2,1)S(1)}, u32[]{:S(2)}, u32[]{:S(2)}) collective-permute-start(bf16[1024,128]{1,0:T(8,128)(2,1)S(1)} %broadcast_select_fusion.1), channel_id=1, source_target_pairs={{0,4},{4,0},{8,12},{12,8},{16,20},{20,16},{24,28},{28,24},{1,5},{5... | collective-permute-start | bytes 786440 | tf_op jit(solution)/shard_map/ppermute | solution.py:21
  51.5 9.3 %collective-permute-start.5 = (bf16[1024,128]{1,0:T(8,128)(2,1)S(1)}, bf16[1024,128]{1,0:T(8,128)(2,1)S(1)}, u32[]{:S(2)}, u32[]{:S(2)}) collective-permute-start(bf16[1024,128]{1,0:T(8,128)(2,1)S(1)} %broadcast_select_fusion.2), channel_id=1, source_target_pairs={{0,8},{4,12},{8,0},{12,4},{16,24},{20,28},{24,16},{28,20},{1,9},{5... | collective-permute-start | bytes 786440 | tf_op jit(solution)/shard_map/ppermute | solution.py:21
  53.2 8.4 %collective-permute-start.7 = (bf16[1024,128]{1,0:T(8,128)(2,1)S(1)}, bf16[1024,128]{1,0:T(8,128)(2,1)S(1)}, u32[]{:S(2)}, u32[]{:S(2)}) collective-permute-start(bf16[1024,128]{1,0:T(8,128)(2,1)S(1)} %broadcast_select_fusion.2), channel_id=1, source_target_pairs={{0,16},{4,20},{8,24},{12,28},{16,0},{20,4},{24,8},{28,12},{1,17},{... | collective-permute-start | bytes 786440 | tf_op jit(solution)/shard_map/ppermute | solution.py:21
  54.8 12.5 %collective-permute-start.31 = (bf16[1024,128]{1,0:T(8,128)(2,1)S(1)}, bf16[1024,128]{1,0:T(8,128)(2,1)S(1)}, u32[]{:S(2)}, u32[]{:S(2)}) collective-permute-start(bf16[1024,128]{1,0:T(8,128)(2,1)S(1)} %collective-permute-done.27), channel_id=1, source_target_pairs={{0,16},{4,20},{8,24},{12,28},{16,0},{20,4},{24,8},{28,12},{1,17},{... | collective-permute-start | bytes 786440 | tf_op jit(solution)/shard_map/ppermute | solution.py:21
  56.1 13.3 %collective-permute-start.28 = (bf16[1024,128]{1,0:T(8,128)(2,1)S(1)}, bf16[1024,128]{1,0:T(8,128)(2,1)S(1)}, u32[]{:S(2)}, u32[]{:S(2)}) collective-permute-start(bf16[1024,128]{1,0:T(8,128)(2,1)S(1)} %collective-permute-done.27), channel_id=1, source_target_pairs={{0,4},{4,0},{8,12},{12,8},{16,20},{20,16},{24,28},{28,24},{1,5},{5... | collective-permute-start | bytes 786440 | tf_op jit(solution)/shard_map/ppermute | solution.py:21
  60.8 9.9 %collective-permute-start.30 = (bf16[1024,128]{1,0:T(8,128)(2,1)S(1)}, bf16[1024,128]{1,0:T(8,128)(2,1)S(1)}, u32[]{:S(2)}, u32[]{:S(2)}) collective-permute-start(bf16[1024,128]{1,0:T(8,128)(2,1)S(1)} %collective-permute-done.29), channel_id=1, source_target_pairs={{0,4},{4,0},{8,12},{12,8},{16,20},{20,16},{24,28},{28,24},{1,5},{5... | collective-permute-start | bytes 786440 | tf_op jit(solution)/shard_map/ppermute | solution.py:21
  60.8 10.2 %collective-permute-start.20 = (bf16[1024,128]{1,0:T(8,128)(2,1)S(1)}, bf16[1024,128]{1,0:T(8,128)(2,1)}, u32[]{:S(2)}, u32[]{:S(2)}) collective-permute-start(bf16[1024,128]{1,0:T(8,128)(2,1)S(1)} %collective-permute-done.18), channel_id=1, source_target_pairs={{0,8},{4,12},{8,0},{12,4},{16,24},{20,28},{24,16},{28,20},{1,9},{5... | collective-permute-start | bytes 786440 | tf_op jit(solution)/shard_map/ppermute | solution.py:21
  61.6 9.5 %collective-permute-start.19 = (bf16[1024,128]{1,0:T(8,128)(2,1)S(1)}, bf16[1024,128]{1,0:T(8,128)(2,1)S(1)}, u32[]{:S(2)}, u32[]{:S(2)}) collective-permute-start(bf16[1024,128]{1,0:T(8,128)(2,1)S(1)} %collective-permute-done.18), channel_id=1, source_target_pairs={{0,4},{4,0},{8,12},{12,8},{16,20},{20,16},{24,28},{28,24},{1,5},{5... | collective-permute-start | bytes 786440 | tf_op jit(solution)/shard_map/ppermute | solution.py:21
  69.4 7.9 %collective-permute-start.9 = (bf16[1024,128]{1,0:T(8,128)(2,1)S(1)}, bf16[1024,128]{1,0:T(8,128)(2,1)S(1)}, u32[]{:S(2)}, u32[]{:S(2)}) collective-permute-start(bf16[1024,128]{1,0:T(8,128)(2,1)S(1)} %collective-permute-done.5), channel_id=1, source_target_pairs={{0,16},{4,20},{8,24},{12,28},{16,0},{20,4},{24,8},{28,12},{1,17},{... | collective-permute-start | bytes 786440 | tf_op jit(solution)/shard_map/ppermute | solution.py:21
  70.7 7.5 %collective-permute-start.32 = (bf16[1024,128]{1,0:T(8,128)(2,1)S(1)}, bf16[1024,128]{1,0:T(8,128)(2,1)S(1)}, u32[]{:S(2)}, u32[]{:S(2)}) collective-permute-start(bf16[1024,128]{1,0:T(8,128)(2,1)S(1)} %collective-permute-done.31), channel_id=1, source_target_pairs={{0,4},{4,0},{8,12},{12,8},{16,20},{20,16},{24,28},{28,24},{1,5},{5... | collective-permute-start | bytes 786440 | tf_op jit(solution)/shard_map/ppermute | solution.py:21
  70.9 18.7 %collective-permute-start.21 = (bf16[1024,128]{1,0:T(8,128)(2,1)}, bf16[1024,128]{1,0:T(8,128)(2,1)}, u32[]{:S(2)}, u32[]{:S(2)}) collective-permute-start(bf16[1024,128]{1,0:T(8,128)(2,1)} %collective-permute-done.20), channel_id=1, source_target_pairs={{0,4},{4,0},{8,12},{12,8},{16,20},{20,16},{24,28},{28,24},{1,5},{5... | collective-permute-start | bytes 786440 | tf_op jit(solution)/shard_map/ppermute | solution.py:21
  71.9 20.7 %collective-permute-start.4 = (bf16[1024,128]{1,0:T(8,128)(2,1)S(1)}, bf16[1024,128]{1,0:T(8,128)(2,1)S(1)}, u32[]{:S(2)}, u32[]{:S(2)}) collective-permute-start(bf16[1024,128]{1,0:T(8,128)(2,1)S(1)} %broadcast_select_fusion.2), channel_id=1, source_target_pairs={{0,4},{4,0},{8,12},{12,8},{16,20},{20,16},{24,28},{28,24},{1,5},{5... | collective-permute-start | bytes 786440 | tf_op jit(solution)/shard_map/ppermute | solution.py:21
  72.9 19.7 %collective-permute-start.6 = (bf16[1024,128]{1,0:T(8,128)(2,1)S(1)}, bf16[1024,128]{1,0:T(8,128)(2,1)}, u32[]{:S(2)}, u32[]{:S(2)}) collective-permute-start(bf16[1024,128]{1,0:T(8,128)(2,1)S(1)} %collective-permute-done.5), channel_id=1, source_target_pairs={{0,4},{4,0},{8,12},{12,8},{16,20},{20,16},{24,28},{28,24},{1,5},{5... | collective-permute-start | bytes 786440 | tf_op jit(solution)/shard_map/ppermute | solution.py:21
  77.4 15.3 %collective-permute-start.8 = (bf16[1024,128]{1,0:T(8,128)(2,1)S(1)}, bf16[1024,128]{1,0:T(8,128)(2,1)}, u32[]{:S(2)}, u32[]{:S(2)}) collective-permute-start(bf16[1024,128]{1,0:T(8,128)(2,1)S(1)} %collective-permute-done.7), channel_id=1, source_target_pairs={{0,4},{4,0},{8,12},{12,8},{16,20},{20,16},{24,28},{28,24},{1,5},{5... | collective-permute-start | bytes 786440 | tf_op jit(solution)/shard_map/ppermute | solution.py:21
  78.8 13.8 %collective-permute-start.10 = (bf16[1024,128]{1,0:T(8,128)(2,1)S(1)}, bf16[1024,128]{1,0:T(8,128)(2,1)}, u32[]{:S(2)}, u32[]{:S(2)}) collective-permute-start(bf16[1024,128]{1,0:T(8,128)(2,1)S(1)} %collective-permute-done.9), channel_id=1, source_target_pairs={{0,4},{4,0},{8,12},{12,8},{16,20},{20,16},{24,28},{28,24},{1,5},{5... | collective-permute-start | bytes 786440 | tf_op jit(solution)/shard_map/ppermute | solution.py:21
  (19 other events, 107.7 us)

commit v2 on v0

--- a/solution.py
+++ b/solution.py
@@ -1,12 +1,26 @@
+import functools
+
 import jax
 import jax.numpy as jnp
+import numpy as np
 from jax import lax
+from jax.experimental import pallas as pl
+from jax.experimental.pallas import tpu as pltpu
 from jax.sharding import PartitionSpec as P
+
+SPANS = (8, 8, 8)
+FORWARD = (True, True, False)
+UNROLL = 16
 
 
 def shifted(shard, axis, by):
     count = lax.axis_size(axis)
     return lax.ppermute(shard, axis, [(i, (i + by) % count) for i in range(count)])
+
+
+def flipped(shard, axis, bits):
+    count = lax.axis_size(axis)
+    return lax.ppermute(shard, axis, [(i, i ^ bits) for i in range(count)])
 
 
 def pick_tiles(current, wanted, row_tiles, tile_size):
@@ -27,7 +41,7 @@
     return totals + jnp.einsum("rk,ktf->rtf", one_hot, products, precision=lax.Precision.HIGHEST)
 
 
-def body(features, tile_values, tile_rows, tile_cols, tile_counts, weight, bias):
+def ring_body(features, tile_values, tile_rows, tile_cols, tile_counts, weight, bias):
     row_count, col_width = features.shape
     tile_size = tile_values.shape[-1]
     row_tiles = row_count // tile_size
@@ -56,6 +70,268 @@
     return jnp.maximum(mixed + bias[None, :], 0.0).astype(jnp.bfloat16)
 
 
+def layouts():
+    starts, sides = [], []
+    for k, span in enumerate(SPANS):
+        reach = span + (SPANS[k - 1] // 2 if k and FORWARD[k - 1] else 0)
+        begin = [0, span, span + reach]
+        side = span + 2 * reach
+        if not FORWARD[k]:
+            begin.append(side)
+            side += span
+        starts.append(begin)
+        sides.append(side)
+    return starts, sides
+
+
+def spots():
+    starts, sides = layouts()
+    edges = np.cumsum((0,) + SPANS)
+    table = np.zeros((8, int(edges[-1])), np.int32)
+    for away in range(8):
+        for k, span in enumerate(SPANS):
+            for local in range(span):
+                group, spot = k, local
+                if away >> 1 < 3:
+                    spot = starts[k][away >> 1] + local
+                elif not FORWARD[k]:
+                    spot = starts[k][3] + local
+                else:
+                    group = k + 1
+                    piece = 1 if local < span // 2 else 2
+                    spot = starts[group][piece] + SPANS[group] + local % (span // 2)
+                table[away, edges[k] + local] = group * 1024 + (away & 1) * sides[group] + spot
+    return table.reshape(-1)
+
+
+def plan_kernel(row_tiles, rows, cols, counts, place, table, order, found):
+    steps = counts.shape[0]
+    slots = rows.shape[0] // steps
+    where = place[0]
+    for group in range(len(SPANS)):
+        found[group] = 0
+
+    def offset_loop(offset, carry):
+        away = where ^ ((where + steps - offset) & (steps - 1))
+
+        def slot_loop(k, carry):
+            slot = offset * slots + k
+            key = table[away * row_tiles + cols[slot]]
+            group = key >> 10
+            at = found[group]
+            order[group, 0, at] = slot
+            order[group, 1, at] = rows[slot]
+            order[group, 2, at] = key & 1023
+            found[group] = at + 1
+            return carry
+
+        return lax.fori_loop(0, counts[offset], slot_loop, carry)
+
+    lax.fori_loop(0, steps, offset_loop, 0)
+    for group in range(len(SPANS)):
+        at = found[group]
+        for u in range(UNROLL):
+            order[group, 0, at + u] = 0
+            order[group, 1, at + u] = row_tiles
+            order[group, 2, at + u] = 0
+        order[group, 3, 0] = (at + UNROLL - 1) // UNROLL
+
+
+def plan(row_tiles, rows, cols, counts, place):
+    room = rows.shape[0] + UNROLL
+    return pl.pallas_call(
+        functools.partial(plan_kernel, row_tiles),
+        out_shape=jax.ShapeDtypeStruct((len(SPANS), 4, room), jnp.int32),
+        in_specs=[pl.BlockSpec(memory_space=pltpu.SMEM)] * 5,
+        out_specs=pl.BlockSpec(memory_space=pltpu.SMEM),
+        scratch_shapes=[pltpu.SMEM((len(SPANS),), jnp.int32)],
+        cost_estimate=pl.CostEstimate(flops=1000000000, bytes_accessed=1000, transcendentals=0),
+        name="plan",
+    )(rows, cols, counts, place, jnp.asarray(spots()))
+
+
+def mix_kernel(members, count, member, own, pair, *rest):
+    *received, weight, _, mine, other = rest
+    width = own.shape[1]
+    pieces = [own[...], pair[...]]
+    for piece in received:
+        pieces += [piece[k * count : (k + 1) * count] for k in range(piece.shape[0] // count)]
+    me = member[0]
+
+    def block(row, col):
+        row = pl.multiple_of(row * width, width)
+        col = pl.multiple_of(col * width, width)
+        return weight[pl.ds(row, width), pl.ds(col, width)]
+
+    rows = [me, me ^ 1, me ^ 3, me ^ 2]
+    sides = [
+        jnp.concatenate([block(row, me), block(row, me ^ 1)], axis=1) for row in rows
+    ]
+    total = jnp.dot(
+        jnp.concatenate(pieces, axis=1),
+        jnp.concatenate(sides, axis=0),
+        preferred_element_type=jnp.float32,
+    )
+    mine[...] = total[:, :width].astype(mine.dtype)
+    other[...] = total[:, width:].astype(other.dtype)
+
+
+def mix(member, own, pair, received, weight, event):
+    shape = jax.ShapeDtypeStruct(own.shape, own.dtype)
+    vmem = pl.BlockSpec(memory_space=pltpu.VMEM)
+    return pl.pallas_call(
+        functools.partial(mix_kernel, 4, own.shape[0]),
+        out_shape=(shape, shape),
+        in_specs=[pl.BlockSpec(memory_space=pltpu.SMEM)]
+        + [vmem] * (3 + len(received))
+        + [pl.BlockSpec(memory_space=pl.ANY)],
+        out_specs=(vmem, vmem),
+        compiler_params=pltpu.CompilerParams(vmem_limit_bytes=16 << 20),
+        cost_estimate=pl.CostEstimate(flops=1000, bytes_accessed=1000, transcendentals=0),
+        name="mix",
+    )(member, own, pair, *received, weight, event)
+
+
+def add_kernel(group, first, last, starts, order, values, bias, *rest):
+    pieces = rest[: len(starts)]
+    rest = rest[len(starts) :]
+    if not first:
+        rest = rest[1:]
+    if last:
+        out, rest = rest[0], rest[1:]
+    totals, token, held, sem = rest
+    token[...] = jnp.zeros_like(token)
+    copies = []
+    for index, piece in enumerate(pieces):
+        spot = held.at[pl.ds(starts[index], piece.shape[0])]
+        copies.append(pltpu.make_async_copy(piece, spot, sem.at[index]))
+        copies[-1].start()
+    if first:
+        totals[...] = jnp.zeros_like(totals)
+    for copy in copies:
+        copy.wait()
+
+    def add(g, carry):
+        sums = []
+        for u in range(UNROLL):
+            index = g * UNROLL + u
+            product = jnp.dot(
+                values[order[group, 0, index]],
+                held[order[group, 2, index]],
+                preferred_element_type=jnp.float32,
+            )
+            sums.append((order[group, 1, index], product))
+        for row, product in sums:
+            totals[row] += product
+        return carry
+
+    lax.fori_loop(0, order[group, 3, 0], add, 0)
+    if last:
+
+        def finish(r, carry):
+            out[r] = jnp.maximum(totals[r] + bias[...], 0.0).astype(out.dtype)
+            return carry
+
+        lax.fori_loop(0, out.shape[0], finish, 0)
+
+
+def add_group(group, row_tiles, order, values, bias, pieces, totals):
+    tile = values.shape[-1]
+    pieces = [piece.reshape(-1, tile, piece.shape[-1]) for piece in pieces]
+    width = pieces[0].shape[-1]
+    starts, sides = layouts()
+    side = sides[group]
+    starts = tuple(starts[group]) + tuple(start + side for start in starts[group])
+    first, last = group == 0, group == len(SPANS) - 1
+    vmem = pl.BlockSpec(memory_space=pltpu.VMEM)
+    any_space = pl.BlockSpec(memory_space=pl.ANY)
+    operands = [order, values, bias, *pieces] + ([] if first else [totals])
+    specs = [pl.BlockSpec(memory_space=pltpu.SMEM), vmem, vmem] + [any_space] * len(pieces)
+    specs += [] if first else [vmem]
+    shapes = [
+        jax.ShapeDtypeStruct((row_tiles + 1, tile, width), jnp.float32),
+        jax.ShapeDtypeStruct((8, width), jnp.float32),
+    ]
+    if last:
+        shapes = [jax.ShapeDtypeStruct((row_tiles, tile, width), jnp.bfloat16)] + shapes
+    return pl.pallas_call(
+        functools.partial(add_kernel, group, first, last, starts),
+        out_shape=tuple(shapes),
+        in_specs=specs,
+        out_specs=(vmem,) * len(shapes),
+        scratch_shapes=[
+            pltpu.VMEM((2 * side, tile, width), jnp.bfloat16),
+            pltpu.SemaphoreType.DMA((len(pieces),)),
+        ],
+        input_output_aliases={} if first else {len(operands) - 1: int(last)},
+        compiler_params=pltpu.CompilerParams(vmem_limit_bytes=24 << 20),
+        cost_estimate=pl.CostEstimate(flops=15000000000, bytes_accessed=1000, transcendentals=0),
+        name="add_tiles",
+    )(*operands)
+
+
+def swap_inner(shard):
+    blocks, members = lax.axis_size("blk"), lax.axis_size("feat")
+    pairs = []
+    for block in range(blocks):
+        for member in range(members):
+            if member in (1, 2):
+                target = block * members + 3 - member
+            else:
+                target = (block ^ 1) * members + member
+            pairs.append((block * members + member, target))
+    return lax.ppermute(shard, ("blk", "feat"), pairs)
+
+
+def swap_outer(shard):
+    return lax.ppermute(shard, "feat", [(0, 1), (1, 0), (2, 3), (3, 2)])
+
+
+def body(features, tile_values, tile_rows, tile_cols, tile_counts, weight, bias):
+    row_count, width = features.shape
+    tile = tile_values.shape[-1]
+    row_tiles = row_count // tile
+    member = lax.axis_index("feat").reshape(1).astype(jnp.int32)
+    place = lax.axis_index("blk").reshape(1).astype(jnp.int32)
+    middle = (member[0] == 1) | (member[0] == 2)
+    count = len(SPANS)
+    edges = [int(edge) * tile for edge in np.cumsum((0,) + SPANS)]
+    order = plan(row_tiles, tile_rows, tile_cols, tile_counts, place)
+    own = [features[edges[k] : edges[k + 1]] for k in range(count)]
+    pairs = [swap_outer(own[0])]
+    first = [swap_inner(own[0])]
+    pairs.append(swap_outer(own[1]))
+    later = swap_outer(features[edges[2] :])
+    for k in range(2, count):
+        pairs.append(later[edges[k] - edges[2] : edges[k + 1] - edges[2]])
+    first.append(swap_inner(pairs[0]))
+    received = [first]
+    for k in range(1, count):
+        received.append([swap_inner(jnp.concatenate([own[k], pairs[k]]))])
+    totals = None
+    events = [None] * (count + 2)
+    steps = []
+    for k in range(count):
+        mine, other = mix(member, own[k], pairs[k], received[k], weight, order)
+        mixed = jnp.where(middle, mine, swap_outer(other))
+        to_beside = to_above = mixed
+        if k and FORWARD[k - 1]:
+            half = SPANS[k - 1] * tile // 2
+            _, beside, above = steps[k - 1][:3]
+            to_beside = jnp.concatenate([mixed, above[:half]])
+            to_above = jnp.concatenate([mixed, beside[half : 2 * half]])
+        step = [mixed, flipped(to_beside, "blk", 2), flipped(to_above, "blk", 4)]
+        if not FORWARD[k]:
+            step.append(flipped(mixed, "blk", 6))
+        steps.append(step)
+        pieces = step + [flipped(piece, "blk", 1) for piece in step]
+        *out, totals, event = add_group(
+            k, row_tiles, order, tile_values, bias[None], pieces, totals
+        )
+        events[k + 2] = event
+    return out[0].reshape(row_count, width)
+
+
 def solution(mesh):
     in_specs = (
         P("blk", "feat"),
@@ -67,4 +343,5 @@
         P("feat"),
     )
     out_specs = P("blk", "feat")
-    return jax.shard_map(body, mesh=mesh, in_specs=in_specs, out_specs=out_specs, check_vma=False)
+    chosen = body if mesh.shape["blk"] == 8 and mesh.shape["feat"] == 4 else ring_body
+    return jax.shard_map(chosen, mesh=mesh, in_specs=in_specs, out_specs=out_specs, check_vma=False)

time: 185 us -> 77.5 us (0.42)
  waiting for transfers between devices: 87.2 us -> 29 us
  matrix products: 42.9 us -> 0 us
  local copies, waits for them, and re-layouts: 29.6 us -> 1.92 us
  starting transfers between devices: 4.29 us -> 28.7 us
  Pallas kernels: 0 us -> 15.6 us
  between operations: 13.7 us -> 0.25 us
  other arithmetic: 6.13 us -> 1.86 us
    all_gather x1 -> x0, waiting for transfers between devices: 63.5 us -> none  [body(): lax.all_gather(aggregate, 'feat', axis=1, tiled=True)]
    dot_general x17 -> x0, matrix products: 42.9 us -> none  [the longest x8 20.8 us: add_tiles(): jnp.einsum('ktj,kjf->ktf', values_all[offset], picked, preferred_element_...]
    ppermute x7 -> x27, starting transfers between devices: 4.28 us -> 28.7 us  [the longest x6 16.8 us: swap_outer(): return lax.ppermute(shard, 'feat', [(0, 1), (1, 0), (2, 3), (3, 2)])]
    pallas_call x0 -> x7, Pallas kernels: none -> 15.6 us  [the longest x3 9.73 us: add_group(): pl.pallas_call(functools.partial(add_kernel, group, first, last, starts),...]
    gather x8 -> x0, local copies, waits for them, and re-layouts: 14.2 us -> none  [pick_tiles(): return jnp.take(source, wanted, axis=0)]
    dot_general x8 -> x0, local copies, waits for them, and re-layouts: 12.6 us -> none  [add_tiles(): jnp.einsum('ktj,kjf->ktf', values_all[offset], picked, preferred_element_...]
    ppermute x7 -> x27, waiting for transfers between devices: 23.6 us -> 29 us  [the longest x6 15.6 us: swap_outer(): return lax.ppermute(shard, 'feat', [(0, 1), (1, 0), (2, 3), (3, 2)])]
    lt x8 -> x0, other arithmetic: 5.05 us -> none  [add_tiles(): active = jnp.arange(slot_count) < tile_counts[offset]]
  transfers between devices with their start and end apart: 8 -> 27, of which waited for: 5 -> 7; matrix products, arithmetic and copies ran while one was open for 34% -> 2% of each run, Pallas kernels for 0% -> 15%
where the time goes in v2:
time: 77.5 us; the launch traced here: 77.3 us
  waiting for transfers between devices  29 us (37%)
  starting transfers between devices  28.7 us (37%)
  Pallas kernels  15.6 us (20%)
  local copies, waits for them, and re-layouts  1.92 us (2%)
  other arithmetic  1.86 us (2%)
    ppermute x6, starting transfers between devices, swap_outer(): return lax.ppermute(shard, 'feat', [(0, 1), (1, 0), (2, 3), (3, 2)])  16.8 us
    ppermute x6, waiting for transfers between devices, swap_outer(): return lax.ppermute(shard, 'feat', [(0, 1), (1, 0), (2, 3), (3, 2)])  15.6 us
    ppermute x17, waiting for transfers between devices, flipped(): return lax.ppermute(shard, axis, [(i, i ^ bits) for i in range(count)])  13.3 us
    ppermute x17, starting transfers between devices, flipped(): return lax.ppermute(shard, axis, [(i, i ^ bits) for i in range(count)])  11.9 us
    pallas_call x3, Pallas kernels, add_group(): pl.pallas_call(functools.partial(add_kernel, group, first, last, starts),...  9.73 us
    pallas_call x1, Pallas kernels, plan(): pl.pallas_call(functools.partial(plan_kernel, row_tiles), out_shape=jax.S...  3.8 us
    pallas_call x3, Pallas kernels, mix(): pl.pallas_call(functools.partial(mix_kernel, 4, own.shape[0]), out_shape=...  2.03 us
    concatenate x2, other arithmetic, body(): received.append([swap_inner(jnp.concatenate([own[k], pairs[k]]))])  1.66 us
  transfers between devices with their start and end apart: 27, of which 7 were waited for; matrix products, arithmetic and copies ran while one was open for 2% of the time, Pallas kernels for 15%

profile of v2, /device:TPU:0, one launch (start us, length us, event | category | flops | bytes accessed | tf_op | source)
XLA Modules:
  0.0 77.3 jit_solution(3885977977843537194)
XLA Ops:
  0.0 1.2 %fusion = (bf16[1024,128]{1,0:T(8,128)(2,1)S(1)}, bf16[1024,128]{1,0:T(8,128)(2,1)S(1)}, bf16[1024,128]{1,0:T(8,128)(2,1)S(1)}) fusion(bf16[3072,128]{1,0:T(8,128)(2,1)} %param.8), kind=kLoop, calls=%fused_computation.9 | loop fusion | bytes 1572864 | tf_op jit(solution)/shard_map/slice | solution.py:300
  1.2 3.1 %collective-permute-start.6 = (bf16[1024,128]{1,0:T(8,128)(2,1)S(1)}, bf16[1024,128]{1,0:T(8,128)(2,1)S(1)}, u32[]{:S(2)}, u32[]{:S(2)}) collective-permute-start(bf16[1024,128]{1,0:T(8,128)(2,1)S(1)} %get-tuple-element.23.own), channel_id=1, source_target_pairs={{0,1},{1,0},{2,3},{3,2},{4,5},{5,4},{6,7},{7,6},{8,9},{9,8},{10,11... | collective-permute-start | bytes 786440 | tf_op jit(solution)/shard_map/ppermute | solution.py:287
  4.3 3.5 %collective-permute-start = (bf16[1024,128]{1,0:T(8,128)(2,1)S(1)}, bf16[1024,128]{1,0:T(8,128)(2,1)S(1)}, u32[]{:S(2)}, u32[]{:S(2)}) collective-permute-start(bf16[1024,128]{1,0:T(8,128)(2,1)S(1)} %get-tuple-element.24.own), channel_id=1, source_target_pairs={{0,1},{1,0},{2,3},{3,2},{4,5},{5,4},{6,7},{7,6},{8,9},{9,8},{10,11... | collective-permute-start | bytes 786440 | tf_op jit(solution)/shard_map/ppermute | solution.py:287
  7.9 3.5 %collective-permute-done.6.pair = bf16[1024,128]{1,0:T(8,128)(2,1)S(1)} collective-permute-done((bf16[1024,128]{1,0:T(8,128)(2,1)S(1)}, bf16[1024,128]{1,0:T(8,128)(2,1)S(1)}, u32[]{:S(2)}, u32[]{:S(2)}) %collective-permute-start.6) | collective-permute-done | bytes 262176 | tf_op jit(solution)/shard_map/ppermute | solution.py:287
  11.4 5.6 %collective-permute-done.3.pair = bf16[1024,128]{1,0:T(8,128)(2,1)S(1)} collective-permute-done((bf16[1024,128]{1,0:T(8,128)(2,1)S(1)}, bf16[1024,128]{1,0:T(8,128)(2,1)S(1)}, u32[]{:S(2)}, u32[]{:S(2)}) %collective-permute-start.3) | collective-permute-done | bytes 262176 | tf_op jit(solution)/shard_map/ppermute | solution.py:287
  17.0 0.8 %pad_maximum_fusion.1 = bf16[2048,128]{1,0:T(8,128)(2,1)} fusion(bf16[1024,128]{1,0:T(8,128)(2,1)S(1)} %collective-permute-done.3.pair, bf16[1024,128]{1,0:T(8,128)(2,1)S(1)} %get-tuple-element.25.own), kind=kLoop, calls=%fused_computation.1 | loop fusion | flops 1048576 | bytes 1048576 | tf_op jit(solution)/shard_map/concatenate | solution.py:310
  17.8 3.8 %plan.1.rest_2_.rest_3_.order = s32[3,4,144]{2,1,0:T(4,128)} custom-call(s32[128]{0:T(128)} %rows.1, s32[128]{0:T(128)} %cols.1, s32[8]{0:T(128)} %counts.1, s32[1]{0:T(128)} %bitcast.place, s32[192]{0:T(256)} %constant.15.clone.table), custom_call_target="tpu_custom_call" | custom-call | flops 1000000000 | bytes 1000 | tf_op jit(solution)/shard_map/plan/pallas_call | solution.py:142
  21.7 0.7 copy-done.1
  22.4 1.2 %mix.5 = (bf16[1024,128]{1,0:T(8,128)(2,1)S(1)}, bf16[1024,128]{1,0:T(8,128)(2,1)}) custom-call(s32[1]{0:T(128)} %bitcast.2.member, bf16[1024,128]{1,0:T(8,128)(2,1)S(1)} %get-tuple-element.23.own, bf16[1024,128]{1,0:T(8,128)(2,1)S(1)} %collective-permute-done.6.pair, bf16[1024,128]{1,0:T(8,128)(2,1)S(1)} %collective-permute-done.7.rest_0_, ...), custom_call_target="tpu_custom_call" | custom-call | flops 1000 | bytes 1000 | tf_op jit(solution)/shard_map/mix/pallas_call | solution.py:182
  23.5 3.6 %collective-permute-start.9 = (bf16[1024,128]{1,0:T(8,128)(2,1)}, bf16[1024,128]{1,0:T(8,128)(2,1)S(1)}, u32[]{:S(2)}, u32[]{:S(2)}) collective-permute-start(bf16[1024,128]{1,0:T(8,128)(2,1)} %get-tuple-element.19), channel_id=1, source_target_pairs={{0,1},{1,0},{2,3},{3,2},{4,5},{5,4},{6,7},{7,6},{8,9},{9,8},{10,11... | collective-permute-start | bytes 786440 | tf_op jit(solution)/shard_map/ppermute | solution.py:287
  27.2 0.8 %pad_maximum_fusion = bf16[2048,128]{1,0:T(8,128)(2,1)} fusion(bf16[1024,128]{1,0:T(8,128)(2,1)S(1)} %collective-permute-done.pair, bf16[1024,128]{1,0:T(8,128)(2,1)S(1)} %get-tuple-element.24.own), kind=kLoop, calls=%fused_computation | loop fusion | flops 1048576 | bytes 1048576 | tf_op jit(solution)/shard_map/concatenate | solution.py:310
  28.0 4.5 %collective-permute-done.9 = bf16[1024,128]{1,0:T(8,128)(2,1)S(1)} collective-permute-done((bf16[1024,128]{1,0:T(8,128)(2,1)}, bf16[1024,128]{1,0:T(8,128)(2,1)S(1)}, u32[]{:S(2)}, u32[]{:S(2)}) %collective-permute-start.9) | collective-permute-done | bytes 262176 | tf_op jit(solution)/shard_map/ppermute | solution.py:287
  32.5 1.8 %collective-permute-start.13 = (bf16[1024,128]{1,0:T(8,128)(2,1)S(1)}, bf16[1024,128]{1,0:T(8,128)(2,1)S(1)}, u32[]{:S(2)}, u32[]{:S(2)}) collective-permute-start(bf16[1024,128]{1,0:T(8,128)(2,1)S(1)} %broadcast_select_fusion), channel_id=1, source_target_pairs={{0,16},{4,20},{8,24},{12,28},{16,0},{20,4},{24,8},{28,12},{1,17},{... | collective-permute-start | bytes 786440 | tf_op jit(solution)/shard_map/ppermute | solution.py:23
  34.3 1.8 %collective-permute-start.10 = (bf16[1024,128]{1,0:T(8,128)(2,1)S(1)}, bf16[1024,128]{1,0:T(8,128)(2,1)S(1)}, u32[]{:S(2)}, u32[]{:S(2)}) collective-permute-start(bf16[1024,128]{1,0:T(8,128)(2,1)S(1)} %broadcast_select_fusion), channel_id=1, source_target_pairs={{0,8},{4,12},{8,0},{12,4},{16,24},{20,28},{24,16},{28,20},{1,9},{5... | collective-permute-start | bytes 786440 | tf_op jit(solution)/shard_map/ppermute | solution.py:23
  36.1 0.4 mix.4
  36.5 0.8 %collective-permute-start.5 = (bf16[1024,128]{1,0:T(8,128)(2,1)S(1)}, bf16[1024,128]{1,0:T(8,128)(2,1)S(1)}, u32[]{:S(2)}, u32[]{:S(2)}) collective-permute-start(bf16[1024,128]{1,0:T(8,128)(2,1)S(1)} %get-tuple-element.17), channel_id=1, source_target_pairs={{0,1},{1,0},{2,3},{3,2},{4,5},{5,4},{6,7},{7,6},{8,9},{9,8},{10,11... | collective-permute-start | bytes 786440 | tf_op jit(solution)/shard_map/ppermute | solution.py:287
  37.4 0.4 mix.3
  37.8 5.7 %collective-permute-start.2 = (bf16[1024,128]{1,0:T(8,128)(2,1)S(1)}, bf16[1024,128]{1,0:T(8,128)(2,1)S(1)}, u32[]{:S(2)}, u32[]{:S(2)}) collective-permute-start(bf16[1024,128]{1,0:T(8,128)(2,1)S(1)} %get-tuple-element.15), channel_id=1, source_target_pairs={{0,1},{1,0},{2,3},{3,2},{4,5},{5,4},{6,7},{7,6},{8,9},{9,8},{10,11... | collective-permute-start | bytes 786440 | tf_op jit(solution)/shard_map/ppermute | solution.py:287
  43.7 1.6 %collective-permute-start.14 = (bf16[1536,128]{1,0:T(8,128)(2,1)S(1)}, bf16[1536,128]{1,0:T(8,128)(2,1)S(1)}, u32[]{:S(2)}, u32[]{:S(2)}) collective-permute-start(bf16[1536,128]{1,0:T(8,128)(2,1)S(1)} %get-tuple-element.28), channel_id=1, source_target_pairs={{0,8},{4,12},{8,0},{12,4},{16,24},{20,28},{24,16},{28,20},{1,9},{5... | collective-permute-start | bytes 1179656 | tf_op jit(solution)/shard_map/ppermute | solution.py:23
  45.2 1.5 %collective-permute-start.11 = (bf16[1536,128]{1,0:T(8,128)(2,1)S(1)}, bf16[1536,128]{1,0:T(8,128)(2,1)S(1)}, u32[]{:S(2)}, u32[]{:S(2)}) collective-permute-start(bf16[1536,128]{1,0:T(8,128)(2,1)S(1)} %get-tuple-element.29), channel_id=1, source_target_pairs={{0,16},{4,20},{8,24},{12,28},{16,0},{20,4},{24,8},{28,12},{1,17},{... | collective-permute-start | bytes 1179656 | tf_op jit(solution)/shard_map/ppermute | solution.py:23
  46.8 0.5 collective-permute-start.26
  47.3 2.0 %collective-permute-done.2 = bf16[1024,128]{1,0:T(8,128)(2,1)S(1)} collective-permute-done((bf16[1024,128]{1,0:T(8,128)(2,1)S(1)}, bf16[1024,128]{1,0:T(8,128)(2,1)S(1)}, u32[]{:S(2)}, u32[]{:S(2)}) %collective-permute-start.2) | collective-permute-done | bytes 262176 | tf_op jit(solution)/shard_map/ppermute | solution.py:287
  49.3 4.5 %collective-permute-done.14 = bf16[1536,128]{1,0:T(8,128)(2,1)S(1)} collective-permute-done((bf16[1536,128]{1,0:T(8,128)(2,1)S(1)}, bf16[1536,128]{1,0:T(8,128)(2,1)S(1)}, u32[]{:S(2)}, u32[]{:S(2)}) %collective-permute-start.14) | collective-permute-done | bytes 393248 | tf_op jit(solution)/shard_map/ppermute | solution.py:23
  53.8 2.5 %collective-permute-start.16 = (bf16[1024,128]{1,0:T(8,128)(2,1)S(1)}, bf16[1024,128]{1,0:T(8,128)(2,1)S(1)}, u32[]{:S(2)}, u32[]{:S(2)}) collective-permute-start(bf16[1024,128]{1,0:T(8,128)(2,1)S(1)} %broadcast_select_fusion.2), channel_id=1, source_target_pairs={{0,24},{4,28},{8,16},{12,20},{16,8},{20,12},{24,0},{28,4},{1,25},{... | collective-permute-start | bytes 786440 | tf_op jit(solution)/shard_map/ppermute | solution.py:23
  56.5 0.4 collective-permute-start.15
  56.9 0.7 collective-permute-start.12
  57.6 4.9 %collective-permute-done.16 = bf16[1024,128]{1,0:T(8,128)(2,1)S(1)} collective-permute-done((bf16[1024,128]{1,0:T(8,128)(2,1)S(1)}, bf16[1024,128]{1,0:T(8,128)(2,1)S(1)}, u32[]{:S(2)}, u32[]{:S(2)}) %collective-permute-start.16) | collective-permute-done | bytes 262176 | tf_op jit(solution)/shard_map/ppermute | solution.py:23
  62.5 2.5 %add_tiles.3 = (f32[25,128,128]{2,1,0:T(8,128)S(1)}, f32[8,128]{1,0:T(8,128)}) custom-call(s32[3,4,144]{2,1,0:T(4,128)S(1)} %copy-done.2, bf16[128,128,128]{2,1,0:T(8,128)(2,1)S(1)} %copy-done.3, f32[1,128]{1,0:T(1,128)S(1)} %bitcast.44, bf16[8,128,128]{2,1,0:T(8,128)(2,1)S(1)} %bitcast.26, bf16[8,128,128]{2,1,0:T(8,128)(2,1)S(1)} %bitcast.28, ...), custom_call_target="tpu_custom_call" | custom-call | flops 15000000512 | bytes 1000 | tf_op jit(solution)/shard_map/add_tiles/pallas_call | solution.py:257
  65.6 3.9 %collective-permute-done.15 = bf16[1536,128]{1,0:T(8,128)(2,1)S(1)} collective-permute-done((bf16[1536,128]{1,0:T(8,128)(2,1)S(1)}, bf16[1536,128]{1,0:T(8,128)(2,1)S(1)}, u32[]{:S(2)}, u32[]{:S(2)}) %collective-permute-start.15) | collective-permute-done | bytes 393248 | tf_op jit(solution)/shard_map/ppermute | solution.py:23
  69.6 0.4 collective-permute-start.18
  70.0 3.1 %add_tiles.4 = (f32[25,128,128]{2,1,0:T(8,128)S(1)}, f32[8,128]{1,0:T(8,128)}) custom-call(s32[3,4,144]{2,1,0:T(4,128)S(1)} %copy-done.2, bf16[128,128,128]{2,1,0:T(8,128)(2,1)S(1)} %copy-done.3, f32[1,128]{1,0:T(1,128)S(1)} %bitcast.45, bf16[8,128,128]{2,1,0:T(8,128)(2,1)S(1)} %bitcast.24, ...), custom_call_target="tpu_custom_call", output_to_operand_aliasing={{0}: (9, {})} | custom-call | flops 15000000512 | bytes 1000 | tf_op jit(solution)/shard_map/add_tiles/pallas_call | solution.py:257
  73.2 4.1 %add_tiles.5 = (bf16[24,128,128]{2,1,0:T(8,128)(2,1)}, f32[25,128,128]{2,1,0:T(8,128)S(1)}, f32[8,128]{1,0:T(8,128)}) custom-call(s32[3,4,144]{2,1,0:T(4,128)S(1)} %copy-done.2, bf16[128,128,128]{2,1,0:T(8,128)(2,1)S(1)} %copy-done.3, f32[1,128]{1,0:T(1,128)S(1)} %bitcast.46, bf16[8,128,128]{2,1,0:T(8,128)(2,1)S(1)} %bitcast.25, ...), custom_call_target="tpu_custom_call", output_to_operand_aliasing={{1}: (11, {})} | custom-call | flops 15000000512 | bytes 1000 | tf_op jit(solution)/shard_map/add_tiles/pallas_call | solution.py:257
  (51 shorter events, 1.1 us)
Async XLA Ops:
  1.2 10.2 %collective-permute-start.6 = (bf16[1024,128]{1,0:T(8,128)(2,1)S(1)}, bf16[1024,128]{1,0:T(8,128)(2,1)S(1)}, u32[]{:S(2)}, u32[]{:S(2)}) collective-permute-start(bf16[1024,128]{1,0:T(8,128)(2,1)S(1)} %get-tuple-element.23.own), channel_id=1, source_target_pairs={{0,1},{1,0},{2,3},{3,2},{4,5},{5,4},{6,7},{7,6},{8,9},{9,8},{10,11... | collective-permute-start | bytes 786440 | tf_op jit(solution)/shard_map/ppermute | solution.py:287
  4.3 12.8 %collective-permute-start.3 = (bf16[1024,128]{1,0:T(8,128)(2,1)S(1)}, bf16[1024,128]{1,0:T(8,128)(2,1)S(1)}, u32[]{:S(2)}, u32[]{:S(2)}) collective-permute-start(bf16[1024,128]{1,0:T(8,128)(2,1)S(1)} %get-tuple-element.25.own), channel_id=1, source_target_pairs={{0,1},{1,0},{2,3},{3,2},{4,5},{5,4},{6,7},{7,6},{8,9},{9,8},{10,11... | collective-permute-start | bytes 786440 | tf_op jit(solution)/shard_map/ppermute | solution.py:287
  4.3 17.3 %collective-permute-start.7 = (bf16[1024,128]{1,0:T(8,128)(2,1)S(1)}, bf16[1024,128]{1,0:T(8,128)(2,1)S(1)}, u32[]{:S(2)}, u32[]{:S(2)}) collective-permute-start(bf16[1024,128]{1,0:T(8,128)(2,1)S(1)} %get-tuple-element.23.own), channel_id=1, source_target_pairs={{0,4},{1,2},{2,1},{3,7},{4,0},{5,6},{6,5},{7,3},{8,12},{9,10},{10,... | collective-permute-start | bytes 786440 | tf_op jit(solution)/shard_map/ppermute | solution.py:283
  4.3 22.8 %collective-permute-start = (bf16[1024,128]{1,0:T(8,128)(2,1)S(1)}, bf16[1024,128]{1,0:T(8,128)(2,1)S(1)}, u32[]{:S(2)}, u32[]{:S(2)}) collective-permute-start(bf16[1024,128]{1,0:T(8,128)(2,1)S(1)} %get-tuple-element.24.own), channel_id=1, source_target_pairs={{0,1},{1,0},{2,3},{3,2},{4,5},{5,4},{6,7},{7,6},{8,9},{9,8},{10,11... | collective-permute-start | bytes 786440 | tf_op jit(solution)/shard_map/ppermute | solution.py:287
  11.4 10.3 %collective-permute-start.8 = (bf16[1024,128]{1,0:T(8,128)(2,1)S(1)}, bf16[1024,128]{1,0:T(8,128)(2,1)S(1)}, u32[]{:S(2)}, u32[]{:S(2)}) collective-permute-start(bf16[1024,128]{1,0:T(8,128)(2,1)S(1)} %collective-permute-done.6.pair), channel_id=1, source_target_pairs={{0,4},{1,2},{2,1},{3,7},{4,0},{5,6},{6,5},{7,3},{8,12},{9,10},{10,... | collective-permute-start | bytes 786440 | tf_op jit(solution)/shard_map/ppermute | solution.py:283
  17.8 18.2 %collective-permute-start.4 = (bf16[2048,128]{1,0:T(8,128)(2,1)}, bf16[2048,128]{1,0:T(8,128)(2,1)S(1)}, u32[]{:S(2)}, u32[]{:S(2)}) collective-permute-start(bf16[2048,128]{1,0:T(8,128)(2,1)} %pad_maximum_fusion.1), channel_id=1, source_target_pairs={{0,4},{1,2},{2,1},{3,7},{4,0},{5,6},{6,5},{7,3},{8,12},{9,10},{10,... | collective-permute-start | bytes 1572872 | tf_op jit(solution)/shard_map/ppermute | solution.py:283
  17.8 3.8 %copy-start = (bf16[512,512]{1,0:T(8,128)(2,1)S(1)}, bf16[512,512]{1,0:T(8,128)(2,1)}, u32[]{:S(2)}) copy-start(bf16[512,512]{1,0:T(8,128)(2,1)} %rest_2_.1) | copy-start | bytes 1572868
  21.7 0.7 copy-start.1
  22.4 13.7 %copy-start.2 = (s32[3,4,144]{2,1,0:T(4,128)S(1)}, s32[3,4,144]{2,1,0:T(4,128)}, u32[]{:S(2)}) copy-start(s32[3,4,144]{2,1,0:T(4,128)} %plan.1.rest_2_.rest_3_.order) | copy-start | bytes 20740
  23.5 8.9 %collective-permute-start.9 = (bf16[1024,128]{1,0:T(8,128)(2,1)}, bf16[1024,128]{1,0:T(8,128)(2,1)S(1)}, u32[]{:S(2)}, u32[]{:S(2)}) collective-permute-start(bf16[1024,128]{1,0:T(8,128)(2,1)} %get-tuple-element.19), channel_id=1, source_target_pairs={{0,1},{1,0},{2,3},{3,2},{4,5},{5,4},{6,7},{7,6},{8,9},{9,8},{10,11... | collective-permute-start | bytes 786440 | tf_op jit(solution)/shard_map/ppermute | solution.py:287
  28.0 9.4 %collective-permute-start.1 = (bf16[2048,128]{1,0:T(8,128)(2,1)}, bf16[2048,128]{1,0:T(8,128)(2,1)S(1)}, u32[]{:S(2)}, u32[]{:S(2)}) collective-permute-start(bf16[2048,128]{1,0:T(8,128)(2,1)} %pad_maximum_fusion), channel_id=1, source_target_pairs={{0,4},{1,2},{2,1},{3,7},{4,0},{5,6},{6,5},{7,3},{8,12},{9,10},{10,... | collective-permute-start | bytes 1572872 | tf_op jit(solution)/shard_map/ppermute | solution.py:283
  32.5 11.0 %collective-permute-start.13 = (bf16[1024,128]{1,0:T(8,128)(2,1)S(1)}, bf16[1024,128]{1,0:T(8,128)(2,1)S(1)}, u32[]{:S(2)}, u32[]{:S(2)}) collective-permute-start(bf16[1024,128]{1,0:T(8,128)(2,1)S(1)} %broadcast_select_fusion), channel_id=1, source_target_pairs={{0,16},{4,20},{8,24},{12,28},{16,0},{20,4},{24,8},{28,12},{1,17},{... | collective-permute-start | bytes 786440 | tf_op jit(solution)/shard_map/ppermute | solution.py:23
  34.3 9.2 %collective-permute-start.10 = (bf16[1024,128]{1,0:T(8,128)(2,1)S(1)}, bf16[1024,128]{1,0:T(8,128)(2,1)S(1)}, u32[]{:S(2)}, u32[]{:S(2)}) collective-permute-start(bf16[1024,128]{1,0:T(8,128)(2,1)S(1)} %broadcast_select_fusion), channel_id=1, source_target_pairs={{0,8},{4,12},{8,0},{12,4},{16,24},{20,28},{24,16},{28,20},{1,9},{5... | collective-permute-start | bytes 786440 | tf_op jit(solution)/shard_map/ppermute | solution.py:23
  36.5 7.0 %collective-permute-start.5 = (bf16[1024,128]{1,0:T(8,128)(2,1)S(1)}, bf16[1024,128]{1,0:T(8,128)(2,1)S(1)}, u32[]{:S(2)}, u32[]{:S(2)}) collective-permute-start(bf16[1024,128]{1,0:T(8,128)(2,1)S(1)} %get-tuple-element.17), channel_id=1, source_target_pairs={{0,1},{1,0},{2,3},{3,2},{4,5},{5,4},{6,7},{7,6},{8,9},{9,8},{10,11... | collective-permute-start | bytes 786440 | tf_op jit(solution)/shard_map/ppermute | solution.py:287
  37.8 11.5 %collective-permute-start.2 = (bf16[1024,128]{1,0:T(8,128)(2,1)S(1)}, bf16[1024,128]{1,0:T(8,128)(2,1)S(1)}, u32[]{:S(2)}, u32[]{:S(2)}) collective-permute-start(bf16[1024,128]{1,0:T(8,128)(2,1)S(1)} %get-tuple-element.15), channel_id=1, source_target_pairs={{0,1},{1,0},{2,3},{3,2},{4,5},{5,4},{6,7},{7,6},{8,9},{9,8},{10,11... | collective-permute-start | bytes 786440 | tf_op jit(solution)/shard_map/ppermute | solution.py:287
  43.6 19.0 %copy-start.3 = (bf16[128,128,128]{2,1,0:T(8,128)(2,1)S(1)}, bf16[128,128,128]{2,1,0:T(8,128)(2,1)}, u32[]{:S(2)}) copy-start(bf16[128,128,128]{2,1,0:T(8,128)(2,1)} %values.5) | copy-start | bytes 12582916
  43.7 18.8 %copy-start.4 = (f32[128]{0:T(128)S(1)}, f32[128]{0:T(128)}, u32[]{:S(2)}) copy-start(f32[128]{0:T(128)} %param.14) | copy-start | bytes 1540
  43.7 10.1 %collective-permute-start.14 = (bf16[1536,128]{1,0:T(8,128)(2,1)S(1)}, bf16[1536,128]{1,0:T(8,128)(2,1)S(1)}, u32[]{:S(2)}, u32[]{:S(2)}) collective-permute-start(bf16[1536,128]{1,0:T(8,128)(2,1)S(1)} %get-tuple-element.28), channel_id=1, source_target_pairs={{0,8},{4,12},{8,0},{12,4},{16,24},{20,28},{24,16},{28,20},{1,9},{5... | collective-permute-start | bytes 1179656 | tf_op jit(solution)/shard_map/ppermute | solution.py:23
  45.2 11.0 %collective-permute-start.11 = (bf16[1536,128]{1,0:T(8,128)(2,1)S(1)}, bf16[1536,128]{1,0:T(8,128)(2,1)S(1)}, u32[]{:S(2)}, u32[]{:S(2)}) collective-permute-start(bf16[1536,128]{1,0:T(8,128)(2,1)S(1)} %get-tuple-element.29), channel_id=1, source_target_pairs={{0,16},{4,20},{8,24},{12,28},{16,0},{20,4},{24,8},{28,12},{1,17},{... | collective-permute-start | bytes 1179656 | tf_op jit(solution)/shard_map/ppermute | solution.py:23
  46.8 9.7 %collective-permute-start.24 = (bf16[1024,128]{1,0:T(8,128)(2,1)S(1)}, bf16[1024,128]{1,0:T(8,128)(2,1)S(1)}, u32[]{:S(2)}, u32[]{:S(2)}) collective-permute-start(bf16[1024,128]{1,0:T(8,128)(2,1)S(1)} %broadcast_select_fusion), channel_id=1, source_target_pairs={{0,4},{4,0},{8,12},{12,8},{16,20},{20,16},{24,28},{28,24},{1,5},{5... | collective-permute-start | bytes 786440 | tf_op jit(solution)/shard_map/ppermute | solution.py:23
  46.8 10.1 %collective-permute-start.26 = (bf16[1024,128]{1,0:T(8,128)(2,1)S(1)}, bf16[1024,128]{1,0:T(8,128)(2,1)S(1)}, u32[]{:S(2)}, u32[]{:S(2)}) collective-permute-start(bf16[1024,128]{1,0:T(8,128)(2,1)S(1)} %collective-permute-done.13), channel_id=1, source_target_pairs={{0,4},{4,0},{8,12},{12,8},{16,20},{20,16},{24,28},{28,24},{1,5},{5... | collective-permute-start | bytes 786440 | tf_op jit(solution)/shard_map/ppermute | solution.py:23
  49.3 8.3 %collective-permute-start.25 = (bf16[1024,128]{1,0:T(8,128)(2,1)S(1)}, bf16[1024,128]{1,0:T(8,128)(2,1)S(1)}, u32[]{:S(2)}, u32[]{:S(2)}) collective-permute-start(bf16[1024,128]{1,0:T(8,128)(2,1)S(1)} %collective-permute-done.10), channel_id=1, source_target_pairs={{0,4},{4,0},{8,12},{12,8},{16,20},{20,16},{24,28},{28,24},{1,5},{5... | collective-permute-start | bytes 786440 | tf_op jit(solution)/shard_map/ppermute | solution.py:23
  53.8 8.7 %collective-permute-start.16 = (bf16[1024,128]{1,0:T(8,128)(2,1)S(1)}, bf16[1024,128]{1,0:T(8,128)(2,1)S(1)}, u32[]{:S(2)}, u32[]{:S(2)}) collective-permute-start(bf16[1024,128]{1,0:T(8,128)(2,1)S(1)} %broadcast_select_fusion.2), channel_id=1, source_target_pairs={{0,24},{4,28},{8,16},{12,20},{16,8},{20,12},{24,0},{28,4},{1,25},{... | collective-permute-start | bytes 786440 | tf_op jit(solution)/shard_map/ppermute | solution.py:23
  56.3 8.8 %collective-permute-start.21 = (bf16[1024,128]{1,0:T(8,128)(2,1)S(1)}, bf16[1024,128]{1,0:T(8,128)(2,1)S(1)}, u32[]{:S(2)}, u32[]{:S(2)}) collective-permute-start(bf16[1024,128]{1,0:T(8,128)(2,1)S(1)} %broadcast_select_fusion.1), channel_id=1, source_target_pairs={{0,4},{4,0},{8,12},{12,8},{16,20},{20,16},{24,28},{28,24},{1,5},{5... | collective-permute-start | bytes 786440 | tf_op jit(solution)/shard_map/ppermute | solution.py:23
  56.5 13.0 %collective-permute-start.15 = (bf16[1536,128]{1,0:T(8,128)(2,1)S(1)}, bf16[1536,128]{1,0:T(8,128)(2,1)S(1)}, u32[]{:S(2)}, u32[]{:S(2)}) collective-permute-start(bf16[1536,128]{1,0:T(8,128)(2,1)S(1)} %get-tuple-element.26), channel_id=1, source_target_pairs={{0,16},{4,20},{8,24},{12,28},{16,0},{20,4},{24,8},{28,12},{1,17},{... | collective-permute-start | bytes 1179656 | tf_op jit(solution)/shard_map/ppermute | solution.py:23
  56.9 12.7 %collective-permute-start.12 = (bf16[1536,128]{1,0:T(8,128)(2,1)S(1)}, bf16[1536,128]{1,0:T(8,128)(2,1)S(1)}, u32[]{:S(2)}, u32[]{:S(2)}) collective-permute-start(bf16[1536,128]{1,0:T(8,128)(2,1)S(1)} %get-tuple-element.27), channel_id=1, source_target_pairs={{0,8},{4,12},{8,0},{12,4},{16,24},{20,28},{24,16},{28,20},{1,9},{5... | collective-permute-start | bytes 1179656 | tf_op jit(solution)/shard_map/ppermute | solution.py:23
  57.6 7.8 %collective-permute-start.22 = (bf16[1536,128]{1,0:T(8,128)(2,1)S(1)}, bf16[1536,128]{1,0:T(8,128)(2,1)S(1)}, u32[]{:S(2)}, u32[]{:S(2)}) collective-permute-start(bf16[1536,128]{1,0:T(8,128)(2,1)S(1)} %collective-permute-done.14), channel_id=1, source_target_pairs={{0,4},{4,0},{8,12},{12,8},{16,20},{20,16},{24,28},{28,24},{1,5},{5... | collective-permute-start | bytes 1179656 | tf_op jit(solution)/shard_map/ppermute | solution.py:23
  62.5 7.5 %collective-permute-start.23 = (bf16[1536,128]{1,0:T(8,128)(2,1)S(1)}, bf16[1536,128]{1,0:T(8,128)(2,1)S(1)}, u32[]{:S(2)}, u32[]{:S(2)}) collective-permute-start(bf16[1536,128]{1,0:T(8,128)(2,1)S(1)} %collective-permute-done.11), channel_id=1, source_target_pairs={{0,4},{4,0},{8,12},{12,8},{16,20},{20,16},{24,28},{28,24},{1,5},{5... | collective-permute-start | bytes 1179656 | tf_op jit(solution)/shard_map/ppermute | solution.py:23
  65.1 8.1 %collective-permute-start.17 = (bf16[1024,128]{1,0:T(8,128)(2,1)S(1)}, bf16[1024,128]{1,0:T(8,128)(2,1)S(1)}, u32[]{:S(2)}, u32[]{:S(2)}) collective-permute-start(bf16[1024,128]{1,0:T(8,128)(2,1)S(1)} %broadcast_select_fusion.2), channel_id=1, source_target_pairs={{0,4},{4,0},{8,12},{12,8},{16,20},{20,16},{24,28},{28,24},{1,5},{5... | collective-permute-start | bytes 786440 | tf_op jit(solution)/shard_map/ppermute | solution.py:23
  65.3 7.9 %collective-permute-start.20 = (bf16[1024,128]{1,0:T(8,128)(2,1)S(1)}, bf16[1024,128]{1,0:T(8,128)(2,1)S(1)}, u32[]{:S(2)}, u32[]{:S(2)}) collective-permute-start(bf16[1024,128]{1,0:T(8,128)(2,1)S(1)} %collective-permute-done.16), channel_id=1, source_target_pairs={{0,4},{4,0},{8,12},{12,8},{16,20},{20,16},{24,28},{28,24},{1,5},{5... | collective-permute-start | bytes 786440 | tf_op jit(solution)/shard_map/ppermute | solution.py:23
  69.5 3.7 %collective-permute-start.19 = (bf16[1536,128]{1,0:T(8,128)(2,1)S(1)}, bf16[1536,128]{1,0:T(8,128)(2,1)S(1)}, u32[]{:S(2)}, u32[]{:S(2)}) collective-permute-start(bf16[1536,128]{1,0:T(8,128)(2,1)S(1)} %collective-permute-done.15), channel_id=1, source_target_pairs={{0,4},{4,0},{8,12},{12,8},{16,20},{20,16},{24,28},{28,24},{1,5},{5... | collective-permute-start | bytes 1179656 | tf_op jit(solution)/shard_map/ppermute | solution.py:23
  69.6 3.6 %collective-permute-start.18 = (bf16[1536,128]{1,0:T(8,128)(2,1)S(1)}, bf16[1536,128]{1,0:T(8,128)(2,1)S(1)}, u32[]{:S(2)}, u32[]{:S(2)}) collective-permute-start(bf16[1536,128]{1,0:T(8,128)(2,1)S(1)} %collective-permute-done.12), channel_id=1, source_target_pairs={{0,4},{4,0},{8,12},{12,8},{16,20},{20,16},{24,28},{28,24},{1,5},{5... | collective-permute-start | bytes 1179656 | tf_op jit(solution)/shard_map/ppermute | solution.py:23

commit v3 on v0

--- a/solution.py
+++ b/solution.py
@@ -1,12 +1,26 @@
+import functools
+
 import jax
 import jax.numpy as jnp
+import numpy as np
 from jax import lax
+from jax.experimental import pallas as pl
+from jax.experimental.pallas import tpu as pltpu
 from jax.sharding import PartitionSpec as P
+
+CHUNKS = 2
+UNROLL = 16
+TURNS = (2, 3, 1)
 
 
 def shifted(shard, axis, by):
     count = lax.axis_size(axis)
     return lax.ppermute(shard, axis, [(i, (i + by) % count) for i in range(count)])
+
+
+def flipped(shard, axis, bits):
+    count = lax.axis_size(axis)
+    return lax.ppermute(shard, axis, [(i, i ^ bits) for i in range(count)])
 
 
 def pick_tiles(current, wanted, row_tiles, tile_size):
@@ -27,7 +41,7 @@
     return totals + jnp.einsum("rk,ktf->rtf", one_hot, products, precision=lax.Precision.HIGHEST)
 
 
-def body(features, tile_values, tile_rows, tile_cols, tile_counts, weight, bias):
+def ring_body(features, tile_values, tile_rows, tile_cols, tile_counts, weight, bias):
     row_count, col_width = features.shape
     tile_size = tile_values.shape[-1]
     row_tiles = row_count // tile_size
@@ -56,6 +70,233 @@
     return jnp.maximum(mixed + bias[None, :], 0.0).astype(jnp.bfloat16)
 
 
+def tie(*arrays):
+    return lax.optimization_barrier(arrays)
+
+
+def spots(row_tiles):
+    table = np.zeros((8, row_tiles), np.int32)
+    for away in range(8):
+        side, way = away & 1, away >> 1
+        group = (0, 1, 1, 2)[way]
+        start = (side, 2 * side, 2 * side + 1, side)[way] * row_tiles
+        table[away] = group * 1024 + start + np.arange(row_tiles)
+    return table.reshape(-1)
+
+
+def plan_kernel(row_tiles, rows, cols, counts, place, table, order, found):
+    steps = counts.shape[0]
+    slots = rows.shape[0] // steps
+    where = place[0]
+    for group in range(3):
+        found[group] = 0
+
+    def offset_loop(offset, carry):
+        away = where ^ ((where + steps - offset) & (steps - 1))
+
+        def slot_loop(k, carry):
+            slot = offset * slots + k
+            key = table[away * row_tiles + cols[slot]]
+            group = key >> 10
+            at = found[group]
+            order[group, 0, at] = slot
+            order[group, 1, at] = rows[slot]
+            order[group, 2, at] = key & 1023
+            found[group] = at + 1
+            return carry
+
+        return lax.fori_loop(0, counts[offset], slot_loop, carry)
+
+    lax.fori_loop(0, steps, offset_loop, 0)
+    for group in range(3):
+        at = found[group]
+        for u in range(UNROLL):
+            order[group, 0, at + u] = 0
+            order[group, 1, at + u] = row_tiles
+            order[group, 2, at + u] = 0
+        order[group, 3, 0] = (at + UNROLL - 1) // UNROLL
+
+
+def plan(row_tiles, rows, cols, counts, place):
+    room = rows.shape[0] + UNROLL
+    return pl.pallas_call(
+        functools.partial(plan_kernel, row_tiles),
+        out_shape=jax.ShapeDtypeStruct((3, 4, room), jnp.int32),
+        in_specs=[pl.BlockSpec(memory_space=pltpu.SMEM)] * 5,
+        out_specs=pl.BlockSpec(memory_space=pltpu.SMEM),
+        scratch_shapes=[pltpu.SMEM((3,), jnp.int32)],
+        cost_estimate=pl.CostEstimate(flops=10**9, bytes_accessed=1000, transcendentals=0),
+        name="plan",
+    )(rows, cols, counts, place, jnp.asarray(spots(row_tiles)))
+
+
+def add_kernel(group, first, last, count, order, member, values, *rest):
+    pieces, rest = rest[:count], rest[count:]
+    if not first:
+        rest = rest[1:]
+    if last:
+        outs, totals, held, sem = rest[:-3], rest[-3], rest[-2], rest[-1]
+    else:
+        totals, held, sem = rest
+    copies = []
+    start = 0
+    for index, piece in enumerate(pieces):
+        spot = held.at[pl.ds(start, piece.shape[0])]
+        copies.append(pltpu.make_async_copy(piece, spot, sem.at[index]))
+        copies[-1].start()
+        start += piece.shape[0]
+    if first:
+        totals[...] = jnp.zeros_like(totals)
+    for copy in copies:
+        copy.wait()
+
+    def add(g, carry):
+        sums = []
+        for u in range(UNROLL):
+            index = g * UNROLL + u
+            product = jnp.dot(
+                values[order[group, 0, index]],
+                held[order[group, 2, index]],
+                preferred_element_type=jnp.float32,
+            )
+            sums.append((order[group, 1, index], product))
+        for row, product in sums:
+            totals[row] += product
+        return carry
+
+    lax.fori_loop(0, order[group, 3, 0], add, 0)
+    if last:
+        members = len(outs) // CHUNKS
+        size = outs[0].shape[0]
+        for index, out in enumerate(outs):
+            chunk, turn = index // members, index % members
+            begin = (chunk * members + (member[0] ^ turn)) * size
+            for tile in range(size):
+                out[tile] = totals[begin + tile].astype(out.dtype)
+
+
+def add_group(group, row_tiles, order, member, values, pieces, totals):
+    tile = values.shape[-1]
+    pieces = [piece.reshape(-1, tile, piece.shape[-1]) for piece in pieces]
+    width = pieces[0].shape[-1]
+    room = sum(piece.shape[0] for piece in pieces)
+    first, last = group == 0, group == 2
+    vmem = pl.BlockSpec(memory_space=pltpu.VMEM)
+    smem = pl.BlockSpec(memory_space=pltpu.SMEM)
+    any_space = pl.BlockSpec(memory_space=pl.ANY)
+    operands = [order, member, values, *pieces] + ([] if first else [totals])
+    specs = [smem, smem, vmem] + [any_space] * len(pieces) + ([] if first else [vmem])
+    total = jax.ShapeDtypeStruct((row_tiles + 1, tile, width), jnp.float32)
+    shapes = [total]
+    if last:
+        size = row_tiles // (4 * CHUNKS)
+        shapes = [jax.ShapeDtypeStruct((size, tile, width), jnp.bfloat16)] * (4 * CHUNKS) + [total]
+    return pl.pallas_call(
+        functools.partial(add_kernel, group, first, last, len(pieces)),
+        out_shape=tuple(shapes),
+        in_specs=specs,
+        out_specs=(vmem,) * len(shapes),
+        scratch_shapes=[
+            pltpu.VMEM((room, tile, width), jnp.bfloat16),
+            pltpu.SemaphoreType.DMA((len(pieces),)),
+        ],
+        input_output_aliases={} if first else {len(operands) - 1: len(shapes) - 1},
+        compiler_params=pltpu.CompilerParams(vmem_limit_bytes=24 << 20),
+        cost_estimate=pl.CostEstimate(flops=1000, bytes_accessed=1000, transcendentals=0),
+        name="add_tiles",
+    )(*operands)
+
+
+def mix_kernel(member, *rest):
+    members = 4
+    pieces, weight, bias, outs = rest[:members], rest[members], rest[members + 1], rest[members + 2 :]
+    me = member[0]
+    width = pieces[0].shape[1]
+    left = jnp.concatenate([piece[...] for piece in pieces], axis=1)
+    for turn, out in enumerate(outs):
+        col = pl.multiple_of((me ^ turn) * width, width)
+        right = jnp.concatenate(
+            [
+                weight[pl.ds(pl.multiple_of((me ^ other) * width, width), width), pl.ds(col, width)]
+                for other in range(members)
+            ],
+            axis=0,
+        )
+        total = jnp.dot(left, right, preferred_element_type=jnp.float32)
+        total = total + bias[turn : turn + 1]
+        out[...] = jnp.maximum(total, 0.0).astype(out.dtype)
+
+
+def mix(member, pieces, weight, bias):
+    shape = jax.ShapeDtypeStruct(pieces[0].shape, pieces[0].dtype)
+    vmem = pl.BlockSpec(memory_space=pltpu.VMEM)
+    return pl.pallas_call(
+        mix_kernel,
+        out_shape=(shape,) * 4,
+        in_specs=[pl.BlockSpec(memory_space=pltpu.SMEM)] + [vmem] * 6,
+        out_specs=(vmem,) * 4,
+        compiler_params=pltpu.CompilerParams(vmem_limit_bytes=16 << 20),
+        cost_estimate=pl.CostEstimate(flops=1000, bytes_accessed=1000, transcendentals=0),
+        name="mix",
+    )(member, *pieces, weight, bias)
+
+
+def join_kernel(member, *rest):
+    pieces, out = rest[:-1], rest[-1]
+    for index, piece in enumerate(pieces):
+        size = piece.shape[0]
+        begin = ((index // 4) * 4 + (member[0] ^ (index % 4))) * size
+        out[pl.ds(pl.multiple_of(begin, size), size)] = piece[...]
+
+
+def join(member, pieces):
+    rows = sum(piece.shape[0] for piece in pieces)
+    vmem = pl.BlockSpec(memory_space=pltpu.VMEM)
+    return pl.pallas_call(
+        join_kernel,
+        out_shape=jax.ShapeDtypeStruct((rows, pieces[0].shape[1]), pieces[0].dtype),
+        in_specs=[pl.BlockSpec(memory_space=pltpu.SMEM)] + [vmem] * len(pieces),
+        out_specs=vmem,
+        compiler_params=pltpu.CompilerParams(vmem_limit_bytes=16 << 20),
+        cost_estimate=pl.CostEstimate(flops=1000, bytes_accessed=1000, transcendentals=0),
+        name="join",
+    )(member, *pieces)
+
+
+def body(features, tile_values, tile_rows, tile_cols, tile_counts, weight, bias):
+    row_count, width = features.shape
+    tile = tile_values.shape[-1]
+    row_tiles = row_count // tile
+    half = row_count // 2
+    member = lax.axis_index("feat").reshape(1).astype(jnp.int32)
+    place = lax.axis_index("blk").reshape(1).astype(jnp.int32)
+    order = plan(row_tiles, tile_rows, tile_cols, tile_counts, place)
+    sibling = flipped(features, "blk", 1)
+    beside = flipped(features, "blk", 2)
+    above = flipped(features, "blk", 4)
+    (totals,) = add_group(0, row_tiles, order, member, tile_values, [features, sibling], None)
+    own_bias, totals = tie(bias[None], totals)
+    biases = [flipped(own_bias, "feat", turn) for turn in (1, 2, 3)]
+    beside, above, *biases = tie(beside, above, *biases)
+    biases = [own_bias, *biases]
+    corner = [flipped(above[:half], "blk", 2), flipped(beside[half:], "blk", 4)]
+    near = [beside, above, flipped(beside, "blk", 1), flipped(above, "blk", 1)]
+    (totals,) = add_group(1, row_tiles, order, member, tile_values, near, totals)
+    *corner, totals = tie(*corner, totals)
+    corner += [flipped(piece, "blk", 1) for piece in corner]
+    *parts, totals = add_group(2, row_tiles, order, member, tile_values, corner, totals)
+    every_bias = jnp.concatenate(biases)
+    parts = [part.reshape(-1, width) for part in parts]
+    done = []
+    for chunk in range(CHUNKS):
+        own = parts[4 * chunk : 4 * chunk + 4]
+        came = {turn: flipped(own[turn], "feat", turn) for turn in TURNS}
+        outs = mix(member, [own[0], came[1], came[2], came[3]], weight, every_bias)
+        came = {turn: flipped(outs[turn], "feat", turn) for turn in TURNS}
+        done += [outs[0], came[1], came[2], came[3]]
+    return join(member, done)
+
+
 def solution(mesh):
     in_specs = (
         P("blk", "feat"),
@@ -67,4 +308,5 @@
         P("feat"),
     )
     out_specs = P("blk", "feat")
-    return jax.shard_map(body, mesh=mesh, in_specs=in_specs, out_specs=out_specs, check_vma=False)
+    chosen = body if mesh.shape["blk"] == 8 and mesh.shape["feat"] == 4 else ring_body
+    return jax.shard_map(chosen, mesh=mesh, in_specs=in_specs, out_specs=out_specs, check_vma=False)

time: 185 us -> 78.1 us (0.42)
  waiting for transfers between devices: 87.2 us -> 26.6 us
  matrix products: 42.9 us -> 0 us
  starting transfers between devices: 4.29 us -> 37.4 us
  local copies, waits for them, and re-layouts: 29.6 us -> 2.95 us
  between operations: 13.7 us -> 0.13 us
  Pallas kernels: 0 us -> 10.6 us
  other arithmetic: 6.13 us -> 0.01 us
    all_gather x1 -> x0, waiting for transfers between devices: 63.5 us -> none  [body(): lax.all_gather(aggregate, 'feat', axis=1, tiled=True)]
    dot_general x17 -> x0, matrix products: 42.9 us -> none  [the longest x8 20.8 us: add_tiles(): jnp.einsum('ktj,kjf->ktf', values_all[offset], picked, preferred_element_...]
    ppermute x7 -> x24, starting transfers between devices: 4.28 us -> 37.4 us  [flipped(): return lax.ppermute(shard, axis, [(i, i ^ bits) for i in range(count)])]
    gather x8 -> x0, local copies, waits for them, and re-layouts: 14.2 us -> none  [pick_tiles(): return jnp.take(source, wanted, axis=0)]
    dot_general x8 -> x0, local copies, waits for them, and re-layouts: 12.6 us -> none  [add_tiles(): jnp.einsum('ktj,kjf->ktf', values_all[offset], picked, preferred_element_...]
    pallas_call x0 -> x7, Pallas kernels: none -> 10.6 us  [the longest x3 5.41 us: add_group(): pl.pallas_call(functools.partial(add_kernel, group, first, last, len(piec...]
    lt x8 -> x0, other arithmetic: 5.05 us -> none  [add_tiles(): active = jnp.arange(slot_count) < tile_counts[offset]]
    ppermute x7 -> x24, waiting for transfers between devices: 23.6 us -> 26.6 us  [flipped(): return lax.ppermute(shard, axis, [(i, i ^ bits) for i in range(count)])]
  transfers between devices with their start and end apart: 8 -> 24, of which waited for: 5 -> 10; matrix products, arithmetic and copies ran while one was open for 34% -> 0% of each run, Pallas kernels for 0% -> 10%
where the time goes in v3:
time: 78.1 us; the launch traced here: 77.7 us
  starting transfers between devices  37.4 us (48%)
  waiting for transfers between devices  26.6 us (34%)
  Pallas kernels  10.6 us (14%)
  local copies, waits for them, and re-layouts  2.95 us (4%)
    ppermute x24, starting transfers between devices, flipped(): return lax.ppermute(shard, axis, [(i, i ^ bits) for i in range(count)])  37.4 us
    ppermute x24, waiting for transfers between devices, flipped(): return lax.ppermute(shard, axis, [(i, i ^ bits) for i in range(count)])  26.6 us
    pallas_call x3, Pallas kernels, add_group(): pl.pallas_call(functools.partial(add_kernel, group, first, last, len(piec...  5.41 us
    pallas_call x1, Pallas kernels, plan(): pl.pallas_call(functools.partial(plan_kernel, row_tiles), out_shape=jax.S...  3.09 us
    unnamed x10, local copies, waits for them, and re-layouts  2.9 us
  transfers between devices with their start and end apart: 24, of which 10 were waited for; matrix products, arithmetic and copies ran while one was open for 0% of the time, Pallas kernels for 10%

profile of v3, /device:TPU:0, one launch (start us, length us, event | category | flops | bytes accessed | tf_op | source)
XLA Modules:
  0.0 77.7 jit_solution(16361760072674955205)
XLA Ops:
  0.5 2.5 %collective-permute-start = (bf16[3072,128]{1,0:T(8,128)(2,1)}, bf16[3072,128]{1,0:T(8,128)(2,1)S(1)}, u32[]{:S(2)}, u32[]{:S(2)}) collective-permute-start(bf16[3072,128]{1,0:T(8,128)(2,1)} %param.8), channel_id=1, source_target_pairs={{0,8},{4,12},{8,0},{12,4},{16,24},{20,28},{24,16},{28,20},{1,9},{5... | collective-permute-start | bytes 2359304 | tf_op jit(solution)/shard_map/ppermute | solution.py:23
  2.9 1.5 %collective-permute-start.1 = (bf16[3072,128]{1,0:T(8,128)(2,1)}, bf16[3072,128]{1,0:T(8,128)(2,1)S(1)}, u32[]{:S(2)}, u32[]{:S(2)}) collective-permute-start(bf16[3072,128]{1,0:T(8,128)(2,1)} %param.8), channel_id=1, source_target_pairs={{0,16},{4,20},{8,24},{12,28},{16,0},{20,4},{24,8},{28,12},{1,17},{... | collective-permute-start | bytes 2359304 | tf_op jit(solution)/shard_map/ppermute | solution.py:23
  4.5 3.1 %plan.1.order = s32[3,4,144]{2,1,0:T(4,128)} custom-call(s32[128]{0:T(128)} %rows.1, s32[128]{0:T(128)} %cols.1, s32[8]{0:T(128)} %counts.1, s32[1]{0:T(128)} %bitcast.1.place, s32[192]{0:T(256)} %constant.11.clone.table), custom_call_target="tpu_custom_call" | custom-call | flops 1000000000 | bytes 1000 | tf_op jit(solution)/shard_map/plan/pallas_call | solution.py:122
  7.6 2.2 %copy-done = bf16[128,128,128]{2,1,0:T(8,128)(2,1)S(1)} copy-done((bf16[128,128,128]{2,1,0:T(8,128)(2,1)S(1)}, bf16[128,128,128]{2,1,0:T(8,128)(2,1)}, u32[]{:S(2)}) %copy-start) | copy-done | bytes 4194328
  9.8 0.7 copy-done.3
  10.5 1.6 %add_tiles.3.rest_4_ = f32[25,128,128]{2,1,0:T(8,128)S(1)} custom-call(s32[3,4,144]{2,1,0:T(4,128)S(1)} %copy-done.3, s32[1]{0:T(128)} %bitcast.member, bf16[128,128,128]{2,1,0:T(8,128)(2,1)S(1)} %copy-done, bf16[24,128,128]{2,1,0:T(8,128)(2,1)S(1)} %bitcast.25, bf16[24,128,128]{2,1,0:T(8,128)(2,1)S(1)} %bitcast.26), custom_call_target="tpu_custom_call" | custom-call | flops 1000 | bytes 1000 | tf_op jit(solution)/shard_map/add_tiles/pallas_call | solution.py:194
  12.1 1.6 %collective-permute-start.3 = (f32[1,128]{1,0:T(1,128)S(1)}, f32[1,128]{1,0:T(1,128)S(1)}, u32[]{:S(2)}, u32[]{:S(2)}) collective-permute-start(f32[1,128]{1,0:T(1,128)S(1)} %bitcast.39), channel_id=1, source_target_pairs={{0,1},{1,0},{2,3},{3,2},{4,5},{5,4},{6,7},{7,6},{8,9},{9,8},{10,11... | collective-permute-start | bytes 1544 | tf_op jit(solution)/shard_map/ppermute | solution.py:23
  13.7 2.6 %collective-permute-start.4 = (f32[1,128]{1,0:T(1,128)S(1)}, f32[1,128]{1,0:T(1,128)S(1)}, u32[]{:S(2)}, u32[]{:S(2)}) collective-permute-start(f32[1,128]{1,0:T(1,128)S(1)} %bitcast.40), channel_id=1, source_target_pairs={{0,2},{1,3},{2,0},{3,1},{4,6},{5,7},{6,4},{7,5},{8,10},{9,11},{10,... | collective-permute-start | bytes 1544 | tf_op jit(solution)/shard_map/ppermute | solution.py:23
  16.5 4.8 %collective-permute-done = bf16[3072,128]{1,0:T(8,128)(2,1)S(1)} collective-permute-done((bf16[3072,128]{1,0:T(8,128)(2,1)}, bf16[3072,128]{1,0:T(8,128)(2,1)S(1)}, u32[]{:S(2)}, u32[]{:S(2)}) %collective-permute-start) | collective-permute-done | bytes 786464 | tf_op jit(solution)/shard_map/ppermute | solution.py:23
  21.4 1.5 %collective-permute-done.1 = bf16[3072,128]{1,0:T(8,128)(2,1)S(1)} collective-permute-done((bf16[3072,128]{1,0:T(8,128)(2,1)}, bf16[3072,128]{1,0:T(8,128)(2,1)S(1)}, u32[]{:S(2)}, u32[]{:S(2)}) %collective-permute-start.1) | collective-permute-done | bytes 786464 | tf_op jit(solution)/shard_map/ppermute | solution.py:23
  23.9 1.7 %collective-permute-start.7 = (bf16[1536,128]{1,0:T(8,128)(2,1)S(1)}, bf16[1536,128]{1,0:T(8,128)(2,1)S(1)}, u32[]{:S(2)}, u32[]{:S(2)}) collective-permute-start(bf16[1536,128]{1,0:T(8,128)(2,1)S(1)} %slice.7), channel_id=1, source_target_pairs={{0,16},{4,20},{8,24},{12,28},{16,0},{20,4},{24,8},{28,12},{1,17},{... | collective-permute-start | bytes 1179656 | tf_op jit(solution)/shard_map/ppermute | solution.py:23
  25.6 0.7 collective-permute-done.9
  26.3 1.6 %add_tiles.4.rest_4_ = f32[25,128,128]{2,1,0:T(8,128)S(1)} custom-call(s32[3,4,144]{2,1,0:T(4,128)S(1)} %copy-done.3, s32[1]{0:T(128)} %bitcast.member, bf16[128,128,128]{2,1,0:T(8,128)(2,1)S(1)} %copy-done, bf16[24,128,128]{2,1,0:T(8,128)(2,1)S(1)} %bitcast.21, bf16[24,128,128]{2,1,0:T(8,128)(2,1)S(1)} %bitcast.22, ...), custom_call_target="tpu_custom_call", output_to_operand_aliasing={{}: (7, {})} | custom-call | flops 1000 | bytes 1000 | tf_op jit(solution)/shard_map/add_tiles/pallas_call | solution.py:194
  27.9 6.7 %collective-permute-done.6 = bf16[1536,128]{1,0:T(8,128)(2,1)S(1)} collective-permute-done((bf16[1536,128]{1,0:T(8,128)(2,1)S(1)}, bf16[1536,128]{1,0:T(8,128)(2,1)S(1)}, u32[]{:S(2)}, u32[]{:S(2)}) %collective-permute-start.6) | collective-permute-done | bytes 393248 | tf_op jit(solution)/shard_map/ppermute | solution.py:23
  35.2 1.2 %collective-permute-done.10 = bf16[1536,128]{1,0:T(8,128)(2,1)S(1)} collective-permute-done((bf16[1536,128]{1,0:T(8,128)(2,1)S(1)}, bf16[1536,128]{1,0:T(8,128)(2,1)S(1)}, u32[]{:S(2)}, u32[]{:S(2)}) %collective-permute-start.10) | collective-permute-done | bytes 393248 | tf_op jit(solution)/shard_map/ppermute | solution.py:23
  37.0 2.2 %add_tiles.5 = (bf16[3,128,128]{2,1,0:T(8,128)(2,1)S(1)}, bf16[3,128,128]{2,1,0:T(8,128)(2,1)S(1)}, bf16[3,128,128]{2,1,0:T(8,128)(2,1)S(1)}, bf16[3,128,128]{2,...) custom-call(s32[3,4,144]{2,1,0:T(4,128)S(1)} %copy-done.3, ...), custom_call_target="tpu_custom_call", output_to_operand_aliasing={{8}: (7, {})} | custom-call | flops 1000 | bytes 1000 | tf_op jit(solution)/shard_map/add_tiles/pallas_call | solution.py:194
  39.2 1.8 %collective-permute-start.18 = (bf16[384,128]{1,0:T(8,128)(2,1)S(1)}, bf16[384,128]{1,0:T(8,128)(2,1)S(1)}, u32[]{:S(2)}, u32[]{:S(2)}) collective-permute-start(bf16[384,128]{1,0:T(8,128)(2,1)S(1)} %bitcast.38), channel_id=1, source_target_pairs={{0,1},{1,0},{2,3},{3,2},{4,5},{5,4},{6,7},{7,6},{8,9},{9,8},{10,11... | collective-permute-start | bytes 294920 | tf_op jit(solution)/shard_map/ppermute | solution.py:23
  41.1 2.6 %collective-permute-start.19 = (bf16[384,128]{1,0:T(8,128)(2,1)S(1)}, bf16[384,128]{1,0:T(8,128)(2,1)S(1)}, u32[]{:S(2)}, u32[]{:S(2)}) collective-permute-start(bf16[384,128]{1,0:T(8,128)(2,1)S(1)} %bitcast.37), channel_id=1, source_target_pairs={{0,2},{1,3},{2,0},{3,1},{4,6},{5,7},{6,4},{7,5},{8,10},{9,11},{10,... | collective-permute-start | bytes 294920 | tf_op jit(solution)/shard_map/ppermute | solution.py:23
  43.7 0.9 %collective-permute-start.12 = (bf16[384,128]{1,0:T(8,128)(2,1)S(1)}, bf16[384,128]{1,0:T(8,128)(2,1)S(1)}, u32[]{:S(2)}, u32[]{:S(2)}) collective-permute-start(bf16[384,128]{1,0:T(8,128)(2,1)S(1)} %bitcast.35), channel_id=1, source_target_pairs={{0,1},{1,0},{2,3},{3,2},{4,5},{5,4},{6,7},{7,6},{8,9},{9,8},{10,11... | collective-permute-start | bytes 294920 | tf_op jit(solution)/shard_map/ppermute | solution.py:23
  44.6 3.5 %collective-permute-start.13 = (bf16[384,128]{1,0:T(8,128)(2,1)S(1)}, bf16[384,128]{1,0:T(8,128)(2,1)S(1)}, u32[]{:S(2)}, u32[]{:S(2)}) collective-permute-start(bf16[384,128]{1,0:T(8,128)(2,1)S(1)} %bitcast.34), channel_id=1, source_target_pairs={{0,2},{1,3},{2,0},{3,1},{4,6},{5,7},{6,4},{7,5},{8,10},{9,11},{10,... | collective-permute-start | bytes 294920 | tf_op jit(solution)/shard_map/ppermute | solution.py:23
  48.7 3.0 %collective-permute-done.19.rest_2_ = bf16[384,128]{1,0:T(8,128)(2,1)S(1)} collective-permute-done((bf16[384,128]{1,0:T(8,128)(2,1)S(1)}, bf16[384,128]{1,0:T(8,128)(2,1)S(1)}, u32[]{:S(2)}, u32[]{:S(2)}) %collective-permute-start.19) | collective-permute-done | bytes 98336 | tf_op jit(solution)/shard_map/ppermute | solution.py:23
  51.7 0.6 mix.3
  52.3 8.0 %collective-permute-start.21 = (bf16[384,128]{1,0:T(8,128)(2,1)S(1)}, bf16[384,128]{1,0:T(8,128)(2,1)S(1)}, u32[]{:S(2)}, u32[]{:S(2)}) collective-permute-start(bf16[384,128]{1,0:T(8,128)(2,1)S(1)} %get-tuple-element.54), channel_id=1, source_target_pairs={{0,1},{1,0},{2,3},{3,2},{4,5},{5,4},{6,7},{7,6},{8,9},{9,8},{10,11... | collective-permute-start | bytes 294920 | tf_op jit(solution)/shard_map/ppermute | solution.py:23
  60.3 2.0 %collective-permute-start.22 = (bf16[384,128]{1,0:T(8,128)(2,1)S(1)}, bf16[384,128]{1,0:T(8,128)(2,1)S(1)}, u32[]{:S(2)}, u32[]{:S(2)}) collective-permute-start(bf16[384,128]{1,0:T(8,128)(2,1)S(1)} %get-tuple-element.55), channel_id=1, source_target_pairs={{0,2},{1,3},{2,0},{3,1},{4,6},{5,7},{6,4},{7,5},{8,10},{9,11},{10,... | collective-permute-start | bytes 294920 | tf_op jit(solution)/shard_map/ppermute | solution.py:23
  62.3 1.4 %collective-permute-start.23 = (bf16[384,128]{1,0:T(8,128)(2,1)S(1)}, bf16[384,128]{1,0:T(8,128)(2,1)S(1)}, u32[]{:S(2)}, u32[]{:S(2)}) collective-permute-start(bf16[384,128]{1,0:T(8,128)(2,1)S(1)} %get-tuple-element.56), channel_id=1, source_target_pairs={{0,3},{1,2},{2,1},{3,0},{4,7},{5,6},{6,5},{7,4},{8,11},{9,10},{10,... | collective-permute-start | bytes 294920 | tf_op jit(solution)/shard_map/ppermute | solution.py:23
  63.7 0.6 mix.2
  64.3 1.1 %collective-permute-start.15 = (bf16[384,128]{1,0:T(8,128)(2,1)S(1)}, bf16[384,128]{1,0:T(8,128)(2,1)S(1)}, u32[]{:S(2)}, u32[]{:S(2)}) collective-permute-start(bf16[384,128]{1,0:T(8,128)(2,1)S(1)} %get-tuple-element.46), channel_id=1, source_target_pairs={{0,1},{1,0},{2,3},{3,2},{4,5},{5,4},{6,7},{7,6},{8,9},{9,8},{10,11... | collective-permute-start | bytes 294920 | tf_op jit(solution)/shard_map/ppermute | solution.py:23
  65.4 2.0 %collective-permute-start.16 = (bf16[384,128]{1,0:T(8,128)(2,1)S(1)}, bf16[384,128]{1,0:T(8,128)(2,1)S(1)}, u32[]{:S(2)}, u32[]{:S(2)}) collective-permute-start(bf16[384,128]{1,0:T(8,128)(2,1)S(1)} %get-tuple-element.47), channel_id=1, source_target_pairs={{0,2},{1,3},{2,0},{3,1},{4,6},{5,7},{6,4},{7,5},{8,10},{9,11},{10,... | collective-permute-start | bytes 294920 | tf_op jit(solution)/shard_map/ppermute | solution.py:23
  67.4 1.4 %collective-permute-start.17 = (bf16[384,128]{1,0:T(8,128)(2,1)S(1)}, bf16[384,128]{1,0:T(8,128)(2,1)S(1)}, u32[]{:S(2)}, u32[]{:S(2)}) collective-permute-start(bf16[384,128]{1,0:T(8,128)(2,1)S(1)} %get-tuple-element.48), channel_id=1, source_target_pairs={{0,3},{1,2},{2,1},{3,0},{4,7},{5,6},{6,5},{7,4},{8,11},{9,10},{10,... | collective-permute-start | bytes 294920 | tf_op jit(solution)/shard_map/ppermute | solution.py:23
  68.8 2.2 %collective-permute-done.23.rest_7_ = bf16[384,128]{1,0:T(8,128)(2,1)S(1)} collective-permute-done((bf16[384,128]{1,0:T(8,128)(2,1)S(1)}, bf16[384,128]{1,0:T(8,128)(2,1)S(1)}, u32[]{:S(2)}, u32[]{:S(2)}) %collective-permute-start.23) | collective-permute-done | bytes 98336 | tf_op jit(solution)/shard_map/ppermute | solution.py:23
  71.0 5.8 %collective-permute-done.16.rest_2_ = bf16[384,128]{1,0:T(8,128)(2,1)S(1)} collective-permute-done((bf16[384,128]{1,0:T(8,128)(2,1)S(1)}, bf16[384,128]{1,0:T(8,128)(2,1)S(1)}, u32[]{:S(2)}, u32[]{:S(2)}) %collective-permute-start.16) | collective-permute-done | bytes 98336 | tf_op jit(solution)/shard_map/ppermute | solution.py:23
  76.8 0.9 %join.1 = bf16[3072,128]{1,0:T(8,128)(2,1)} custom-call(s32[1]{0:T(128)} %bitcast.member, bf16[384,128]{1,0:T(8,128)(2,1)S(1)} %get-tuple-element.45.rest_0_, bf16[384,128]{1,0:T(8,128)(2,1)S(1)} %collective-permute-done.15.rest_1_, bf16[384,128]{1,0:T(8,128)(2,1)S(1)} %collective-permute-done.16.rest_2_, ...), custom_call_target="tpu_custom_call" | custom-call | flops 1000 | bytes 1000 | tf_op jit(solution)/shard_map/join/pallas_call | solution.py:255
  (36 shorter events, 3.5 us)
Async XLA Ops:
  0.0 7.6 %collective-permute-start.2 = (bf16[3072,128]{1,0:T(8,128)(2,1)}, bf16[3072,128]{1,0:T(8,128)(2,1)S(1)}, u32[]{:S(2)}, u32[]{:S(2)}) collective-permute-start(bf16[3072,128]{1,0:T(8,128)(2,1)} %param.8), channel_id=1, source_target_pairs={{0,4},{4,0},{8,12},{12,8},{16,20},{20,16},{24,28},{28,24},{1,5},{5... | collective-permute-start | bytes 2359304 | tf_op jit(solution)/shard_map/ppermute | solution.py:23
  0.5 20.9 %collective-permute-start = (bf16[3072,128]{1,0:T(8,128)(2,1)}, bf16[3072,128]{1,0:T(8,128)(2,1)S(1)}, u32[]{:S(2)}, u32[]{:S(2)}) collective-permute-start(bf16[3072,128]{1,0:T(8,128)(2,1)} %param.8), channel_id=1, source_target_pairs={{0,8},{4,12},{8,0},{12,4},{16,24},{20,28},{24,16},{28,20},{1,9},{5... | collective-permute-start | bytes 2359304 | tf_op jit(solution)/shard_map/ppermute | solution.py:23
  2.9 19.9 %collective-permute-start.1 = (bf16[3072,128]{1,0:T(8,128)(2,1)}, bf16[3072,128]{1,0:T(8,128)(2,1)S(1)}, u32[]{:S(2)}, u32[]{:S(2)}) collective-permute-start(bf16[3072,128]{1,0:T(8,128)(2,1)} %param.8), channel_id=1, source_target_pairs={{0,16},{4,20},{8,24},{12,28},{16,0},{20,4},{24,8},{28,12},{1,17},{... | collective-permute-start | bytes 2359304 | tf_op jit(solution)/shard_map/ppermute | solution.py:23
  4.5 3.1 %copy-start.2 = (bf16[3072,128]{1,0:T(8,128)(2,1)S(1)}, bf16[3072,128]{1,0:T(8,128)(2,1)}, u32[]{:S(2)}) copy-start(bf16[3072,128]{1,0:T(8,128)(2,1)} %param.8) | copy-start | bytes 2359300
  7.6 2.2 %copy-start = (bf16[128,128,128]{2,1,0:T(8,128)(2,1)S(1)}, bf16[128,128,128]{2,1,0:T(8,128)(2,1)}, u32[]{:S(2)}) copy-start(bf16[128,128,128]{2,1,0:T(8,128)(2,1)} %values.5) | copy-start | bytes 12582916
  9.8 0.7 copy-start.3
  10.5 1.6 %copy-start.4 = (f32[128]{0:T(128)S(1)}, f32[128]{0:T(128)}, u32[]{:S(2)}) copy-start(f32[128]{0:T(128)} %param.14) | copy-start | bytes 1540
  12.1 10.7 %collective-permute-start.3 = (f32[1,128]{1,0:T(1,128)S(1)}, f32[1,128]{1,0:T(1,128)S(1)}, u32[]{:S(2)}, u32[]{:S(2)}) collective-permute-start(f32[1,128]{1,0:T(1,128)S(1)} %bitcast.39), channel_id=1, source_target_pairs={{0,1},{1,0},{2,3},{3,2},{4,5},{5,4},{6,7},{7,6},{8,9},{9,8},{10,11... | collective-permute-start | bytes 1544 | tf_op jit(solution)/shard_map/ppermute | solution.py:23
  13.7 9.1 %collective-permute-start.4 = (f32[1,128]{1,0:T(1,128)S(1)}, f32[1,128]{1,0:T(1,128)S(1)}, u32[]{:S(2)}, u32[]{:S(2)}) collective-permute-start(f32[1,128]{1,0:T(1,128)S(1)} %bitcast.40), channel_id=1, source_target_pairs={{0,2},{1,3},{2,0},{3,1},{4,6},{5,7},{6,4},{7,5},{8,10},{9,11},{10,... | collective-permute-start | bytes 1544 | tf_op jit(solution)/shard_map/ppermute | solution.py:23
  16.3 6.5 %collective-permute-start.5 = (f32[1,128]{1,0:T(1,128)S(1)}, f32[1,128]{1,0:T(1,128)S(1)}, u32[]{:S(2)}, u32[]{:S(2)}) collective-permute-start(f32[1,128]{1,0:T(1,128)S(1)} %bitcast.41), channel_id=1, source_target_pairs={{0,3},{1,2},{2,1},{3,0},{4,7},{5,6},{6,5},{7,4},{8,11},{9,10},{10,... | collective-permute-start | bytes 1544 | tf_op jit(solution)/shard_map/ppermute | solution.py:23
  22.8 2.8 %collective-permute-start.8 = (bf16[3072,128]{1,0:T(8,128)(2,1)S(1)}, bf16[3072,128]{1,0:T(8,128)(2,1)S(1)}, u32[]{:S(2)}, u32[]{:S(2)}) collective-permute-start(bf16[3072,128]{1,0:T(8,128)(2,1)S(1)} %collective-permute-done), channel_id=1, source_target_pairs={{0,4},{4,0},{8,12},{12,8},{16,20},{20,16},{24,28},{28,24},{1,5},{5... | collective-permute-start | bytes 2359304 | tf_op jit(solution)/shard_map/ppermute | solution.py:23
  22.9 3.4 %collective-permute-start.9 = (bf16[3072,128]{1,0:T(8,128)(2,1)S(1)}, bf16[3072,128]{1,0:T(8,128)(2,1)S(1)}, u32[]{:S(2)}, u32[]{:S(2)}) collective-permute-start(bf16[3072,128]{1,0:T(8,128)(2,1)S(1)} %collective-permute-done.1), channel_id=1, source_target_pairs={{0,4},{4,0},{8,12},{12,8},{16,20},{20,16},{24,28},{28,24},{1,5},{5... | collective-permute-start | bytes 2359304 | tf_op jit(solution)/shard_map/ppermute | solution.py:23
  23.5 11.2 %collective-permute-start.6 = (bf16[1536,128]{1,0:T(8,128)(2,1)S(1)}, bf16[1536,128]{1,0:T(8,128)(2,1)S(1)}, u32[]{:S(2)}, u32[]{:S(2)}) collective-permute-start(bf16[1536,128]{1,0:T(8,128)(2,1)S(1)} %slice.6), channel_id=1, source_target_pairs={{0,8},{4,12},{8,0},{12,4},{16,24},{20,28},{24,16},{28,20},{1,9},{5... | collective-permute-start | bytes 1179656 | tf_op jit(solution)/shard_map/ppermute | solution.py:23
  23.9 10.8 %collective-permute-start.7 = (bf16[1536,128]{1,0:T(8,128)(2,1)S(1)}, bf16[1536,128]{1,0:T(8,128)(2,1)S(1)}, u32[]{:S(2)}, u32[]{:S(2)}) collective-permute-start(bf16[1536,128]{1,0:T(8,128)(2,1)S(1)} %slice.7), channel_id=1, source_target_pairs={{0,16},{4,20},{8,24},{12,28},{16,0},{20,4},{24,8},{28,12},{1,17},{... | collective-permute-start | bytes 1179656 | tf_op jit(solution)/shard_map/ppermute | solution.py:23
  34.7 1.7 %collective-permute-start.10 = (bf16[1536,128]{1,0:T(8,128)(2,1)S(1)}, bf16[1536,128]{1,0:T(8,128)(2,1)S(1)}, u32[]{:S(2)}, u32[]{:S(2)}) collective-permute-start(bf16[1536,128]{1,0:T(8,128)(2,1)S(1)} %collective-permute-done.6), channel_id=1, source_target_pairs={{0,4},{4,0},{8,12},{12,8},{16,20},{20,16},{24,28},{28,24},{1,5},{5... | collective-permute-start | bytes 1179656 | tf_op jit(solution)/shard_map/ppermute | solution.py:23
  34.7 2.3 %collective-permute-start.11 = (bf16[1536,128]{1,0:T(8,128)(2,1)S(1)}, bf16[1536,128]{1,0:T(8,128)(2,1)S(1)}, u32[]{:S(2)}, u32[]{:S(2)}) collective-permute-start(bf16[1536,128]{1,0:T(8,128)(2,1)S(1)} %collective-permute-done.7), channel_id=1, source_target_pairs={{0,4},{4,0},{8,12},{12,8},{16,20},{20,16},{24,28},{28,24},{1,5},{5... | collective-permute-start | bytes 1179656 | tf_op jit(solution)/shard_map/ppermute | solution.py:23
  37.0 14.7 %copy-start.1 = (bf16[512,512]{1,0:T(8,128)(2,1)S(1)}, bf16[512,512]{1,0:T(8,128)(2,1)}, u32[]{:S(2)}) copy-start(bf16[512,512]{1,0:T(8,128)(2,1)} %rest_4_.3) | copy-start | bytes 1572868
  39.2 8.9 %collective-permute-start.18 = (bf16[384,128]{1,0:T(8,128)(2,1)S(1)}, bf16[384,128]{1,0:T(8,128)(2,1)S(1)}, u32[]{:S(2)}, u32[]{:S(2)}) collective-permute-start(bf16[384,128]{1,0:T(8,128)(2,1)S(1)} %bitcast.38), channel_id=1, source_target_pairs={{0,1},{1,0},{2,3},{3,2},{4,5},{5,4},{6,7},{7,6},{8,9},{9,8},{10,11... | collective-permute-start | bytes 294920 | tf_op jit(solution)/shard_map/ppermute | solution.py:23
  41.1 10.7 %collective-permute-start.19 = (bf16[384,128]{1,0:T(8,128)(2,1)S(1)}, bf16[384,128]{1,0:T(8,128)(2,1)S(1)}, u32[]{:S(2)}, u32[]{:S(2)}) collective-permute-start(bf16[384,128]{1,0:T(8,128)(2,1)S(1)} %bitcast.37), channel_id=1, source_target_pairs={{0,2},{1,3},{2,0},{3,1},{4,6},{5,7},{6,4},{7,5},{8,10},{9,11},{10,... | collective-permute-start | bytes 294920 | tf_op jit(solution)/shard_map/ppermute | solution.py:23
  43.6 8.1 %collective-permute-start.20 = (bf16[384,128]{1,0:T(8,128)(2,1)S(1)}, bf16[384,128]{1,0:T(8,128)(2,1)S(1)}, u32[]{:S(2)}, u32[]{:S(2)}) collective-permute-start(bf16[384,128]{1,0:T(8,128)(2,1)S(1)} %bitcast.36), channel_id=1, source_target_pairs={{0,3},{1,2},{2,1},{3,0},{4,7},{5,6},{6,5},{7,4},{8,11},{9,10},{10,... | collective-permute-start | bytes 294920 | tf_op jit(solution)/shard_map/ppermute | solution.py:23
  43.7 18.6 %collective-permute-start.12 = (bf16[384,128]{1,0:T(8,128)(2,1)S(1)}, bf16[384,128]{1,0:T(8,128)(2,1)S(1)}, u32[]{:S(2)}, u32[]{:S(2)}) collective-permute-start(bf16[384,128]{1,0:T(8,128)(2,1)S(1)} %bitcast.35), channel_id=1, source_target_pairs={{0,1},{1,0},{2,3},{3,2},{4,5},{5,4},{6,7},{7,6},{8,9},{9,8},{10,11... | collective-permute-start | bytes 294920 | tf_op jit(solution)/shard_map/ppermute | solution.py:23
  44.6 19.1 %collective-permute-start.13 = (bf16[384,128]{1,0:T(8,128)(2,1)S(1)}, bf16[384,128]{1,0:T(8,128)(2,1)S(1)}, u32[]{:S(2)}, u32[]{:S(2)}) collective-permute-start(bf16[384,128]{1,0:T(8,128)(2,1)S(1)} %bitcast.34), channel_id=1, source_target_pairs={{0,2},{1,3},{2,0},{3,1},{4,6},{5,7},{6,4},{7,5},{8,10},{9,11},{10,... | collective-permute-start | bytes 294920 | tf_op jit(solution)/shard_map/ppermute | solution.py:23
  48.1 15.6 %collective-permute-start.14 = (bf16[384,128]{1,0:T(8,128)(2,1)S(1)}, bf16[384,128]{1,0:T(8,128)(2,1)S(1)}, u32[]{:S(2)}, u32[]{:S(2)}) collective-permute-start(bf16[384,128]{1,0:T(8,128)(2,1)S(1)} %bitcast.33), channel_id=1, source_target_pairs={{0,3},{1,2},{2,1},{3,0},{4,7},{5,6},{6,5},{7,4},{8,11},{9,10},{10,... | collective-permute-start | bytes 294920 | tf_op jit(solution)/shard_map/ppermute | solution.py:23
  52.3 15.1 %collective-permute-start.21 = (bf16[384,128]{1,0:T(8,128)(2,1)S(1)}, bf16[384,128]{1,0:T(8,128)(2,1)S(1)}, u32[]{:S(2)}, u32[]{:S(2)}) collective-permute-start(bf16[384,128]{1,0:T(8,128)(2,1)S(1)} %get-tuple-element.54), channel_id=1, source_target_pairs={{0,1},{1,0},{2,3},{3,2},{4,5},{5,4},{6,7},{7,6},{8,9},{9,8},{10,11... | collective-permute-start | bytes 294920 | tf_op jit(solution)/shard_map/ppermute | solution.py:23
  60.3 8.5 %collective-permute-start.22 = (bf16[384,128]{1,0:T(8,128)(2,1)S(1)}, bf16[384,128]{1,0:T(8,128)(2,1)S(1)}, u32[]{:S(2)}, u32[]{:S(2)}) collective-permute-start(bf16[384,128]{1,0:T(8,128)(2,1)S(1)} %get-tuple-element.55), channel_id=1, source_target_pairs={{0,2},{1,3},{2,0},{3,1},{4,6},{5,7},{6,4},{7,5},{8,10},{9,11},{10,... | collective-permute-start | bytes 294920 | tf_op jit(solution)/shard_map/ppermute | solution.py:23
  62.3 8.6 %collective-permute-start.23 = (bf16[384,128]{1,0:T(8,128)(2,1)S(1)}, bf16[384,128]{1,0:T(8,128)(2,1)S(1)}, u32[]{:S(2)}, u32[]{:S(2)}) collective-permute-start(bf16[384,128]{1,0:T(8,128)(2,1)S(1)} %get-tuple-element.56), channel_id=1, source_target_pairs={{0,3},{1,2},{2,1},{3,0},{4,7},{5,6},{6,5},{7,4},{8,11},{9,10},{10,... | collective-permute-start | bytes 294920 | tf_op jit(solution)/shard_map/ppermute | solution.py:23
  64.3 6.7 %collective-permute-start.15 = (bf16[384,128]{1,0:T(8,128)(2,1)S(1)}, bf16[384,128]{1,0:T(8,128)(2,1)S(1)}, u32[]{:S(2)}, u32[]{:S(2)}) collective-permute-start(bf16[384,128]{1,0:T(8,128)(2,1)S(1)} %get-tuple-element.46), channel_id=1, source_target_pairs={{0,1},{1,0},{2,3},{3,2},{4,5},{5,4},{6,7},{7,6},{8,9},{9,8},{10,11... | collective-permute-start | bytes 294920 | tf_op jit(solution)/shard_map/ppermute | solution.py:23
  65.4 11.3 %collective-permute-start.16 = (bf16[384,128]{1,0:T(8,128)(2,1)S(1)}, bf16[384,128]{1,0:T(8,128)(2,1)S(1)}, u32[]{:S(2)}, u32[]{:S(2)}) collective-permute-start(bf16[384,128]{1,0:T(8,128)(2,1)S(1)} %get-tuple-element.47), channel_id=1, source_target_pairs={{0,2},{1,3},{2,0},{3,1},{4,6},{5,7},{6,4},{7,5},{8,10},{9,11},{10,... | collective-permute-start | bytes 294920 | tf_op jit(solution)/shard_map/ppermute | solution.py:23
  67.4 9.4 %collective-permute-start.17 = (bf16[384,128]{1,0:T(8,128)(2,1)S(1)}, bf16[384,128]{1,0:T(8,128)(2,1)S(1)}, u32[]{:S(2)}, u32[]{:S(2)}) collective-permute-start(bf16[384,128]{1,0:T(8,128)(2,1)S(1)} %get-tuple-element.48), channel_id=1, source_target_pairs={{0,3},{1,2},{2,1},{3,0},{4,7},{5,6},{6,5},{7,4},{8,11},{9,10},{10,... | collective-permute-start | bytes 294920 | tf_op jit(solution)/shard_map/ppermute | solution.py:23

commit v4 on v3

--- a/solution.py
+++ b/solution.py
@@ -78,8 +78,8 @@
     table = np.zeros((8, row_tiles), np.int32)
     for away in range(8):
         side, way = away & 1, away >> 1
-        group = (0, 1, 1, 2)[way]
-        start = (side, 2 * side, 2 * side + 1, side)[way] * row_tiles
+        group = (0, 1, 1, 2 + side)[way]
+        start = (side, 2 * side, 2 * side + 1, 0)[way] * row_tiles
         table[away] = group * 1024 + start + np.arange(row_tiles)
     return table.reshape(-1)
 
@@ -88,7 +88,7 @@
     steps = counts.shape[0]
     slots = rows.shape[0] // steps
     where = place[0]
-    for group in range(3):
+    for group in range(4):
         found[group] = 0
 
     def offset_loop(offset, carry):
@@ -108,7 +108,7 @@
         return lax.fori_loop(0, counts[offset], slot_loop, carry)
 
     lax.fori_loop(0, steps, offset_loop, 0)
-    for group in range(3):
+    for group in range(4):
         at = found[group]
         for u in range(UNROLL):
             order[group, 0, at + u] = 0
@@ -121,10 +121,10 @@
     room = rows.shape[0] + UNROLL
     return pl.pallas_call(
         functools.partial(plan_kernel, row_tiles),
-        out_shape=jax.ShapeDtypeStruct((3, 4, room), jnp.int32),
+        out_shape=jax.ShapeDtypeStruct((4, 4, room), jnp.int32),
         in_specs=[pl.BlockSpec(memory_space=pltpu.SMEM)] * 5,
         out_specs=pl.BlockSpec(memory_space=pltpu.SMEM),
-        scratch_shapes=[pltpu.SMEM((3,), jnp.int32)],
+        scratch_shapes=[pltpu.SMEM((4,), jnp.int32)],
         cost_estimate=pl.CostEstimate(flops=10**9, bytes_accessed=1000, transcendentals=0),
         name="plan",
     )(rows, cols, counts, place, jnp.asarray(spots(row_tiles)))
@@ -180,7 +180,7 @@
     pieces = [piece.reshape(-1, tile, piece.shape[-1]) for piece in pieces]
     width = pieces[0].shape[-1]
     room = sum(piece.shape[0] for piece in pieces)
-    first, last = group == 0, group == 2
+    first, last = group == 0, group == 3
     vmem = pl.BlockSpec(memory_space=pltpu.VMEM)
     smem = pl.BlockSpec(memory_space=pltpu.SMEM)
     any_space = pl.BlockSpec(memory_space=pl.ANY)
@@ -202,7 +202,7 @@
         ],
         input_output_aliases={} if first else {len(operands) - 1: len(shapes) - 1},
         compiler_params=pltpu.CompilerParams(vmem_limit_bytes=24 << 20),
-        cost_estimate=pl.CostEstimate(flops=1000, bytes_accessed=1000, transcendentals=0),
+        cost_estimate=pl.CostEstimate(flops=10**9, bytes_accessed=1000, transcendentals=0),
         name="add_tiles",
     )(*operands)
 
@@ -283,8 +283,9 @@
     near = [beside, above, flipped(beside, "blk", 1), flipped(above, "blk", 1)]
     (totals,) = add_group(1, row_tiles, order, member, tile_values, near, totals)
     *corner, totals = tie(*corner, totals)
-    corner += [flipped(piece, "blk", 1) for piece in corner]
-    *parts, totals = add_group(2, row_tiles, order, member, tile_values, corner, totals)
+    (totals,) = add_group(2, row_tiles, order, member, tile_values, corner, totals)
+    corner = [flipped(piece, "blk", 1) for piece in corner]
+    *parts, totals = add_group(3, row_tiles, order, member, tile_values, corner, totals)
     every_bias = jnp.concatenate(biases)
     parts = [part.reshape(-1, width) for part in parts]
     done = []

time: 78.1 us -> 77.6 us (level)
  waiting for transfers between devices: 26.6 us -> 22.3 us
  Pallas kernels: 10.6 us -> 13.1 us
  starting transfers between devices: 37.4 us -> 38.9 us
    ppermute x24, waiting for transfers between devices: 26.6 us -> 22.3 us  [flipped(): return lax.ppermute(shard, axis, [(i, i ^ bits) for i in range(count)])]
    pallas_call x3 -> x4, Pallas kernels: 5.41 us -> 7.1 us  [add_group(): pl.pallas_call(functools.partial(add_kernel, group, first, last, len(piec...]
    ppermute x24, starting transfers between devices: 37.4 us -> 38.9 us  [flipped(): return lax.ppermute(shard, axis, [(i, i ^ bits) for i in range(count)])]
  transfers between devices with their start and end apart: 24 -> 24, of which waited for: 10 -> 9; matrix products, arithmetic and copies ran while one was open for 0% -> 0% of each run, Pallas kernels for 10% -> 14%
where the time goes in v4:
time: 77.6 us; the launch traced here: 77.4 us
  starting transfers between devices  38.9 us (50%)
  waiting for transfers between devices  22.3 us (29%)
  Pallas kernels  13.1 us (17%)
  local copies, waits for them, and re-layouts  2.96 us (4%)
    ppermute x24, starting transfers between devices, flipped(): return lax.ppermute(shard, axis, [(i, i ^ bits) for i in range(count)])  38.9 us
    ppermute x24, waiting for transfers between devices, flipped(): return lax.ppermute(shard, axis, [(i, i ^ bits) for i in range(count)])  22.3 us
    pallas_call x4, Pallas kernels, add_group(): pl.pallas_call(functools.partial(add_kernel, group, first, last, len(piec...  7.1 us
    pallas_call x1, Pallas kernels, plan(): pl.pallas_call(functools.partial(plan_kernel, row_tiles), out_shape=jax.S...  3.85 us
    unnamed x10, local copies, waits for them, and re-layouts  2.91 us
  transfers between devices with their start and end apart: 24, of which 9 were waited for; matrix products, arithmetic and copies ran while one was open for 0% of the time, Pallas kernels for 14%

profile of v4, /device:TPU:0, one launch (start us, length us, event | category | flops | bytes accessed | tf_op | source)
XLA Modules:
  0.0 77.4 jit_solution(17305548190346640039)
XLA Ops:
  0.5 2.5 %collective-permute-start = (bf16[3072,128]{1,0:T(8,128)(2,1)}, bf16[3072,128]{1,0:T(8,128)(2,1)S(1)}, u32[]{:S(2)}, u32[]{:S(2)}) collective-permute-start(bf16[3072,128]{1,0:T(8,128)(2,1)} %param.8), channel_id=1, source_target_pairs={{0,8},{4,12},{8,0},{12,4},{16,24},{20,28},{24,16},{28,20},{1,9},{5... | collective-permute-start | bytes 2359304 | tf_op jit(solution)/shard_map/ppermute | solution.py:23
  2.9 1.5 %collective-permute-start.1 = (bf16[3072,128]{1,0:T(8,128)(2,1)}, bf16[3072,128]{1,0:T(8,128)(2,1)S(1)}, u32[]{:S(2)}, u32[]{:S(2)}) collective-permute-start(bf16[3072,128]{1,0:T(8,128)(2,1)} %param.8), channel_id=1, source_target_pairs={{0,16},{4,20},{8,24},{12,28},{16,0},{20,4},{24,8},{28,12},{1,17},{... | collective-permute-start | bytes 2359304 | tf_op jit(solution)/shard_map/ppermute | solution.py:23
  4.5 3.9 %plan.1.order = s32[4,4,144]{2,1,0:T(4,128)} custom-call(s32[128]{0:T(128)} %rows.1, s32[128]{0:T(128)} %cols.1, s32[8]{0:T(128)} %counts.1, s32[1]{0:T(128)} %bitcast.1.place, s32[192]{0:T(256)} %constant.11.clone.table), custom_call_target="tpu_custom_call" | custom-call | flops 1000000000 | bytes 1000 | tf_op jit(solution)/shard_map/plan/pallas_call | solution.py:122
  8.4 2.2 %copy-done = bf16[128,128,128]{2,1,0:T(8,128)(2,1)S(1)} copy-done((bf16[128,128,128]{2,1,0:T(8,128)(2,1)S(1)}, bf16[128,128,128]{2,1,0:T(8,128)(2,1)}, u32[]{:S(2)}) %copy-start) | copy-done | bytes 4194328
  10.5 0.7 copy-done.3
  11.3 1.7 %add_tiles.4.rest_4_ = f32[25,128,128]{2,1,0:T(8,128)S(1)} custom-call(s32[4,4,144]{2,1,0:T(4,128)S(1)} %copy-done.3, s32[1]{0:T(128)} %bitcast.member, bf16[128,128,128]{2,1,0:T(8,128)(2,1)S(1)} %copy-done, bf16[24,128,128]{2,1,0:T(8,128)(2,1)S(1)} %bitcast.23, bf16[24,128,128]{2,1,0:T(8,128)(2,1)S(1)} %bitcast.24), custom_call_target="tpu_custom_call" | custom-call | flops 1000000000 | bytes 1000 | tf_op jit(solution)/shard_map/add_tiles/pallas_call | solution.py:194
  12.9 1.6 %collective-permute-start.3 = (f32[1,128]{1,0:T(1,128)S(1)}, f32[1,128]{1,0:T(1,128)S(1)}, u32[]{:S(2)}, u32[]{:S(2)}) collective-permute-start(f32[1,128]{1,0:T(1,128)S(1)} %bitcast.39), channel_id=1, source_target_pairs={{0,1},{1,0},{2,3},{3,2},{4,5},{5,4},{6,7},{7,6},{8,9},{9,8},{10,11... | collective-permute-start | bytes 1544 | tf_op jit(solution)/shard_map/ppermute | solution.py:23
  14.6 2.6 %collective-permute-start.4 = (f32[1,128]{1,0:T(1,128)S(1)}, f32[1,128]{1,0:T(1,128)S(1)}, u32[]{:S(2)}, u32[]{:S(2)}) collective-permute-start(f32[1,128]{1,0:T(1,128)S(1)} %bitcast.40), channel_id=1, source_target_pairs={{0,2},{1,3},{2,0},{3,1},{4,6},{5,7},{6,4},{7,5},{8,10},{9,11},{10,... | collective-permute-start | bytes 1544 | tf_op jit(solution)/shard_map/ppermute | solution.py:23
  17.4 4.0 %collective-permute-done = bf16[3072,128]{1,0:T(8,128)(2,1)S(1)} collective-permute-done((bf16[3072,128]{1,0:T(8,128)(2,1)}, bf16[3072,128]{1,0:T(8,128)(2,1)S(1)}, u32[]{:S(2)}, u32[]{:S(2)}) %collective-permute-start) | collective-permute-done | bytes 786464 | tf_op jit(solution)/shard_map/ppermute | solution.py:23
  21.4 1.5 %collective-permute-done.1 = bf16[3072,128]{1,0:T(8,128)(2,1)S(1)} collective-permute-done((bf16[3072,128]{1,0:T(8,128)(2,1)}, bf16[3072,128]{1,0:T(8,128)(2,1)S(1)}, u32[]{:S(2)}, u32[]{:S(2)}) %collective-permute-start.1) | collective-permute-done | bytes 786464 | tf_op jit(solution)/shard_map/ppermute | solution.py:23
  23.9 1.7 %collective-permute-start.7 = (bf16[1536,128]{1,0:T(8,128)(2,1)S(1)}, bf16[1536,128]{1,0:T(8,128)(2,1)S(1)}, u32[]{:S(2)}, u32[]{:S(2)}) collective-permute-start(bf16[1536,128]{1,0:T(8,128)(2,1)S(1)} %slice.7), channel_id=1, source_target_pairs={{0,16},{4,20},{8,24},{12,28},{16,0},{20,4},{24,8},{28,12},{1,17},{... | collective-permute-start | bytes 1179656 | tf_op jit(solution)/shard_map/ppermute | solution.py:23
  25.6 0.7 collective-permute-done.9
  26.3 2.3 %add_tiles.5.rest_2_ = f32[25,128,128]{2,1,0:T(8,128)S(1)} custom-call(s32[4,4,144]{2,1,0:T(4,128)S(1)} %copy-done.3, s32[1]{0:T(128)} %bitcast.member, bf16[128,128,128]{2,1,0:T(8,128)(2,1)S(1)} %copy-done, bf16[24,128,128]{2,1,0:T(8,128)(2,1)S(1)} %bitcast.21, bf16[24,128,128]{2,1,0:T(8,128)(2,1)S(1)} %bitcast.22, ...), custom_call_target="tpu_custom_call", output_to_operand_aliasing={{}: (7, {})} | custom-call | flops 1000000000 | bytes 1000 | tf_op jit(solution)/shard_map/add_tiles/pallas_call | solution.py:194
  28.7 6.0 %collective-permute-done.6 = bf16[1536,128]{1,0:T(8,128)(2,1)S(1)} collective-permute-done((bf16[1536,128]{1,0:T(8,128)(2,1)S(1)}, bf16[1536,128]{1,0:T(8,128)(2,1)S(1)}, u32[]{:S(2)}, u32[]{:S(2)}) %collective-permute-start.6) | collective-permute-done | bytes 393248 | tf_op jit(solution)/shard_map/ppermute | solution.py:23
  35.2 1.5 %add_tiles.6.rest_2_ = f32[25,128,128]{2,1,0:T(8,128)S(1)} custom-call(s32[4,4,144]{2,1,0:T(4,128)S(1)} %copy-done.3, s32[1]{0:T(128)} %bitcast.member, bf16[128,128,128]{2,1,0:T(8,128)(2,1)S(1)} %copy-done, bf16[12,128,128]{2,1,0:T(8,128)(2,1)S(1)} %bitcast.27, bf16[12,128,128]{2,1,0:T(8,128)(2,1)S(1)} %bitcast.28, ...), custom_call_target="tpu_custom_call", output_to_operand_aliasing={{}: (5, {})} | custom-call | flops 1000000000 | bytes 1000 | tf_op jit(solution)/shard_map/add_tiles/pallas_call | solution.py:194
  37.0 1.6 %add_tiles.7 = (bf16[3,128,128]{2,1,0:T(8,128)(2,1)S(1)}, bf16[3,128,128]{2,1,0:T(8,128)(2,1)S(1)}, bf16[3,128,128]{2,1,0:T(8,128)(2,1)S(1)}, bf16[3,128,128]{2,...) custom-call(s32[4,4,144]{2,1,0:T(4,128)S(1)} %copy-done.3, ...), custom_call_target="tpu_custom_call", output_to_operand_aliasing={{8}: (5, {})} | custom-call | flops 1000000000 | bytes 1000 | tf_op jit(solution)/shard_map/add_tiles/pallas_call | solution.py:194
  38.6 1.8 %collective-permute-start.18 = (bf16[384,128]{1,0:T(8,128)(2,1)S(1)}, bf16[384,128]{1,0:T(8,128)(2,1)S(1)}, u32[]{:S(2)}, u32[]{:S(2)}) collective-permute-start(bf16[384,128]{1,0:T(8,128)(2,1)S(1)} %bitcast.38), channel_id=1, source_target_pairs={{0,1},{1,0},{2,3},{3,2},{4,5},{5,4},{6,7},{7,6},{8,9},{9,8},{10,11... | collective-permute-start | bytes 294920 | tf_op jit(solution)/shard_map/ppermute | solution.py:23
  40.4 2.6 %collective-permute-start.19 = (bf16[384,128]{1,0:T(8,128)(2,1)S(1)}, bf16[384,128]{1,0:T(8,128)(2,1)S(1)}, u32[]{:S(2)}, u32[]{:S(2)}) collective-permute-start(bf16[384,128]{1,0:T(8,128)(2,1)S(1)} %bitcast.37), channel_id=1, source_target_pairs={{0,2},{1,3},{2,0},{3,1},{4,6},{5,7},{6,4},{7,5},{8,10},{9,11},{10,... | collective-permute-start | bytes 294920 | tf_op jit(solution)/shard_map/ppermute | solution.py:23
  43.1 0.9 %collective-permute-start.12 = (bf16[384,128]{1,0:T(8,128)(2,1)S(1)}, bf16[384,128]{1,0:T(8,128)(2,1)S(1)}, u32[]{:S(2)}, u32[]{:S(2)}) collective-permute-start(bf16[384,128]{1,0:T(8,128)(2,1)S(1)} %bitcast.35), channel_id=1, source_target_pairs={{0,1},{1,0},{2,3},{3,2},{4,5},{5,4},{6,7},{7,6},{8,9},{9,8},{10,11... | collective-permute-start | bytes 294920 | tf_op jit(solution)/shard_map/ppermute | solution.py:23
  44.0 3.5 %collective-permute-start.13 = (bf16[384,128]{1,0:T(8,128)(2,1)S(1)}, bf16[384,128]{1,0:T(8,128)(2,1)S(1)}, u32[]{:S(2)}, u32[]{:S(2)}) collective-permute-start(bf16[384,128]{1,0:T(8,128)(2,1)S(1)} %bitcast.34), channel_id=1, source_target_pairs={{0,2},{1,3},{2,0},{3,1},{4,6},{5,7},{6,4},{7,5},{8,10},{9,11},{10,... | collective-permute-start | bytes 294920 | tf_op jit(solution)/shard_map/ppermute | solution.py:23
  47.5 0.9 %collective-permute-start.14 = (bf16[384,128]{1,0:T(8,128)(2,1)S(1)}, bf16[384,128]{1,0:T(8,128)(2,1)S(1)}, u32[]{:S(2)}, u32[]{:S(2)}) collective-permute-start(bf16[384,128]{1,0:T(8,128)(2,1)S(1)} %bitcast.33), channel_id=1, source_target_pairs={{0,3},{1,2},{2,1},{3,0},{4,7},{5,6},{6,5},{7,4},{8,11},{9,10},{10,... | collective-permute-start | bytes 294920 | tf_op jit(solution)/shard_map/ppermute | solution.py:23
  48.3 2.8 %collective-permute-done.19.rest_2_ = bf16[384,128]{1,0:T(8,128)(2,1)S(1)} collective-permute-done((bf16[384,128]{1,0:T(8,128)(2,1)S(1)}, bf16[384,128]{1,0:T(8,128)(2,1)S(1)}, u32[]{:S(2)}, u32[]{:S(2)}) %collective-permute-start.19) | collective-permute-done | bytes 98336 | tf_op jit(solution)/shard_map/ppermute | solution.py:23
  51.1 0.6 mix.3
  51.7 7.0 %collective-permute-start.21 = (bf16[384,128]{1,0:T(8,128)(2,1)S(1)}, bf16[384,128]{1,0:T(8,128)(2,1)S(1)}, u32[]{:S(2)}, u32[]{:S(2)}) collective-permute-start(bf16[384,128]{1,0:T(8,128)(2,1)S(1)} %get-tuple-element.54), channel_id=1, source_target_pairs={{0,1},{1,0},{2,3},{3,2},{4,5},{5,4},{6,7},{7,6},{8,9},{9,8},{10,11... | collective-permute-start | bytes 294920 | tf_op jit(solution)/shard_map/ppermute | solution.py:23
  58.7 1.1 %collective-permute-start.22 = (bf16[384,128]{1,0:T(8,128)(2,1)S(1)}, bf16[384,128]{1,0:T(8,128)(2,1)S(1)}, u32[]{:S(2)}, u32[]{:S(2)}) collective-permute-start(bf16[384,128]{1,0:T(8,128)(2,1)S(1)} %get-tuple-element.55), channel_id=1, source_target_pairs={{0,2},{1,3},{2,0},{3,1},{4,6},{5,7},{6,4},{7,5},{8,10},{9,11},{10,... | collective-permute-start | bytes 294920 | tf_op jit(solution)/shard_map/ppermute | solution.py:23
  59.8 1.4 %collective-permute-start.23 = (bf16[384,128]{1,0:T(8,128)(2,1)S(1)}, bf16[384,128]{1,0:T(8,128)(2,1)S(1)}, u32[]{:S(2)}, u32[]{:S(2)}) collective-permute-start(bf16[384,128]{1,0:T(8,128)(2,1)S(1)} %get-tuple-element.56), channel_id=1, source_target_pairs={{0,3},{1,2},{2,1},{3,0},{4,7},{5,6},{6,5},{7,4},{8,11},{9,10},{10,... | collective-permute-start | bytes 294920 | tf_op jit(solution)/shard_map/ppermute | solution.py:23
  61.8 3.7 %collective-permute-start.15 = (bf16[384,128]{1,0:T(8,128)(2,1)S(1)}, bf16[384,128]{1,0:T(8,128)(2,1)S(1)}, u32[]{:S(2)}, u32[]{:S(2)}) collective-permute-start(bf16[384,128]{1,0:T(8,128)(2,1)S(1)} %get-tuple-element.46), channel_id=1, source_target_pairs={{0,1},{1,0},{2,3},{3,2},{4,5},{5,4},{6,7},{7,6},{8,9},{9,8},{10,11... | collective-permute-start | bytes 294920 | tf_op jit(solution)/shard_map/ppermute | solution.py:23
  65.5 2.5 %collective-permute-start.16 = (bf16[384,128]{1,0:T(8,128)(2,1)S(1)}, bf16[384,128]{1,0:T(8,128)(2,1)S(1)}, u32[]{:S(2)}, u32[]{:S(2)}) collective-permute-start(bf16[384,128]{1,0:T(8,128)(2,1)S(1)} %get-tuple-element.47), channel_id=1, source_target_pairs={{0,2},{1,3},{2,0},{3,1},{4,6},{5,7},{6,4},{7,5},{8,10},{9,11},{10,... | collective-permute-start | bytes 294920 | tf_op jit(solution)/shard_map/ppermute | solution.py:23
  68.0 1.4 %collective-permute-start.17 = (bf16[384,128]{1,0:T(8,128)(2,1)S(1)}, bf16[384,128]{1,0:T(8,128)(2,1)S(1)}, u32[]{:S(2)}, u32[]{:S(2)}) collective-permute-start(bf16[384,128]{1,0:T(8,128)(2,1)S(1)} %get-tuple-element.48), channel_id=1, source_target_pairs={{0,3},{1,2},{2,1},{3,0},{4,7},{5,6},{6,5},{7,4},{8,11},{9,10},{10,... | collective-permute-start | bytes 294920 | tf_op jit(solution)/shard_map/ppermute | solution.py:23
  69.4 0.8 collective-permute-done.22.rest_6_
  70.2 6.3 %collective-permute-done.16.rest_2_ = bf16[384,128]{1,0:T(8,128)(2,1)S(1)} collective-permute-done((bf16[384,128]{1,0:T(8,128)(2,1)S(1)}, bf16[384,128]{1,0:T(8,128)(2,1)S(1)}, u32[]{:S(2)}, u32[]{:S(2)}) %collective-permute-start.16) | collective-permute-done | bytes 98336 | tf_op jit(solution)/shard_map/ppermute | solution.py:23
  76.5 0.9 %join.1 = bf16[3072,128]{1,0:T(8,128)(2,1)} custom-call(s32[1]{0:T(128)} %bitcast.member, bf16[384,128]{1,0:T(8,128)(2,1)S(1)} %get-tuple-element.45.rest_0_, bf16[384,128]{1,0:T(8,128)(2,1)S(1)} %collective-permute-done.15.rest_1_, bf16[384,128]{1,0:T(8,128)(2,1)S(1)} %collective-permute-done.16.rest_2_, ...), custom_call_target="tpu_custom_call" | custom-call | flops 1000 | bytes 1000 | tf_op jit(solution)/shard_map/join/pallas_call | solution.py:255
  (37 shorter events, 3.2 us)
Async XLA Ops:
  0.0 8.3 %collective-permute-start.2 = (bf16[3072,128]{1,0:T(8,128)(2,1)}, bf16[3072,128]{1,0:T(8,128)(2,1)S(1)}, u32[]{:S(2)}, u32[]{:S(2)}) collective-permute-start(bf16[3072,128]{1,0:T(8,128)(2,1)} %param.8), channel_id=1, source_target_pairs={{0,4},{4,0},{8,12},{12,8},{16,20},{20,16},{24,28},{28,24},{1,5},{5... | collective-permute-start | bytes 2359304 | tf_op jit(solution)/shard_map/ppermute | solution.py:23
  0.5 20.9 %collective-permute-start = (bf16[3072,128]{1,0:T(8,128)(2,1)}, bf16[3072,128]{1,0:T(8,128)(2,1)S(1)}, u32[]{:S(2)}, u32[]{:S(2)}) collective-permute-start(bf16[3072,128]{1,0:T(8,128)(2,1)} %param.8), channel_id=1, source_target_pairs={{0,8},{4,12},{8,0},{12,4},{16,24},{20,28},{24,16},{28,20},{1,9},{5... | collective-permute-start | bytes 2359304 | tf_op jit(solution)/shard_map/ppermute | solution.py:23
  2.9 19.9 %collective-permute-start.1 = (bf16[3072,128]{1,0:T(8,128)(2,1)}, bf16[3072,128]{1,0:T(8,128)(2,1)S(1)}, u32[]{:S(2)}, u32[]{:S(2)}) collective-permute-start(bf16[3072,128]{1,0:T(8,128)(2,1)} %param.8), channel_id=1, source_target_pairs={{0,16},{4,20},{8,24},{12,28},{16,0},{20,4},{24,8},{28,12},{1,17},{... | collective-permute-start | bytes 2359304 | tf_op jit(solution)/shard_map/ppermute | solution.py:23
  4.5 3.9 %copy-start.2 = (bf16[3072,128]{1,0:T(8,128)(2,1)S(1)}, bf16[3072,128]{1,0:T(8,128)(2,1)}, u32[]{:S(2)}) copy-start(bf16[3072,128]{1,0:T(8,128)(2,1)} %param.8) | copy-start | bytes 2359300
  8.3 2.2 %copy-start = (bf16[128,128,128]{2,1,0:T(8,128)(2,1)S(1)}, bf16[128,128,128]{2,1,0:T(8,128)(2,1)}, u32[]{:S(2)}) copy-start(bf16[128,128,128]{2,1,0:T(8,128)(2,1)} %values.7) | copy-start | bytes 12582916
  10.5 0.7 copy-start.3
  11.3 1.7 %copy-start.4 = (f32[128]{0:T(128)S(1)}, f32[128]{0:T(128)}, u32[]{:S(2)}) copy-start(f32[128]{0:T(128)} %param.14) | copy-start | bytes 1540
  12.9 9.9 %collective-permute-start.3 = (f32[1,128]{1,0:T(1,128)S(1)}, f32[1,128]{1,0:T(1,128)S(1)}, u32[]{:S(2)}, u32[]{:S(2)}) collective-permute-start(f32[1,128]{1,0:T(1,128)S(1)} %bitcast.39), channel_id=1, source_target_pairs={{0,1},{1,0},{2,3},{3,2},{4,5},{5,4},{6,7},{7,6},{8,9},{9,8},{10,11... | collective-permute-start | bytes 1544 | tf_op jit(solution)/shard_map/ppermute | solution.py:23
  14.6 8.3 %collective-permute-start.4 = (f32[1,128]{1,0:T(1,128)S(1)}, f32[1,128]{1,0:T(1,128)S(1)}, u32[]{:S(2)}, u32[]{:S(2)}) collective-permute-start(f32[1,128]{1,0:T(1,128)S(1)} %bitcast.40), channel_id=1, source_target_pairs={{0,2},{1,3},{2,0},{3,1},{4,6},{5,7},{6,4},{7,5},{8,10},{9,11},{10,... | collective-permute-start | bytes 1544 | tf_op jit(solution)/shard_map/ppermute | solution.py:23
  17.2 5.7 %collective-permute-start.5 = (f32[1,128]{1,0:T(1,128)S(1)}, f32[1,128]{1,0:T(1,128)S(1)}, u32[]{:S(2)}, u32[]{:S(2)}) collective-permute-start(f32[1,128]{1,0:T(1,128)S(1)} %bitcast.41), channel_id=1, source_target_pairs={{0,3},{1,2},{2,1},{3,0},{4,7},{5,6},{6,5},{7,4},{8,11},{9,10},{10,... | collective-permute-start | bytes 1544 | tf_op jit(solution)/shard_map/ppermute | solution.py:23
  22.8 2.8 %collective-permute-start.8 = (bf16[3072,128]{1,0:T(8,128)(2,1)S(1)}, bf16[3072,128]{1,0:T(8,128)(2,1)S(1)}, u32[]{:S(2)}, u32[]{:S(2)}) collective-permute-start(bf16[3072,128]{1,0:T(8,128)(2,1)S(1)} %collective-permute-done), channel_id=1, source_target_pairs={{0,4},{4,0},{8,12},{12,8},{16,20},{20,16},{24,28},{28,24},{1,5},{5... | collective-permute-start | bytes 2359304 | tf_op jit(solution)/shard_map/ppermute | solution.py:23
  22.9 3.4 %collective-permute-start.9 = (bf16[3072,128]{1,0:T(8,128)(2,1)S(1)}, bf16[3072,128]{1,0:T(8,128)(2,1)S(1)}, u32[]{:S(2)}, u32[]{:S(2)}) collective-permute-start(bf16[3072,128]{1,0:T(8,128)(2,1)S(1)} %collective-permute-done.1), channel_id=1, source_target_pairs={{0,4},{4,0},{8,12},{12,8},{16,20},{20,16},{24,28},{28,24},{1,5},{5... | collective-permute-start | bytes 2359304 | tf_op jit(solution)/shard_map/ppermute | solution.py:23
  23.5 11.2 %collective-permute-start.6 = (bf16[1536,128]{1,0:T(8,128)(2,1)S(1)}, bf16[1536,128]{1,0:T(8,128)(2,1)S(1)}, u32[]{:S(2)}, u32[]{:S(2)}) collective-permute-start(bf16[1536,128]{1,0:T(8,128)(2,1)S(1)} %slice.6), channel_id=1, source_target_pairs={{0,8},{4,12},{8,0},{12,4},{16,24},{20,28},{24,16},{28,20},{1,9},{5... | collective-permute-start | bytes 1179656 | tf_op jit(solution)/shard_map/ppermute | solution.py:23
  23.9 10.8 %collective-permute-start.7 = (bf16[1536,128]{1,0:T(8,128)(2,1)S(1)}, bf16[1536,128]{1,0:T(8,128)(2,1)S(1)}, u32[]{:S(2)}, u32[]{:S(2)}) collective-permute-start(bf16[1536,128]{1,0:T(8,128)(2,1)S(1)} %slice.7), channel_id=1, source_target_pairs={{0,16},{4,20},{8,24},{12,28},{16,0},{20,4},{24,8},{28,12},{1,17},{... | collective-permute-start | bytes 1179656 | tf_op jit(solution)/shard_map/ppermute | solution.py:23
  34.7 2.0 %collective-permute-start.11 = (bf16[1536,128]{1,0:T(8,128)(2,1)S(1)}, bf16[1536,128]{1,0:T(8,128)(2,1)S(1)}, u32[]{:S(2)}, u32[]{:S(2)}) collective-permute-start(bf16[1536,128]{1,0:T(8,128)(2,1)S(1)} %collective-permute-done.7), channel_id=1, source_target_pairs={{0,4},{4,0},{8,12},{12,8},{16,20},{20,16},{24,28},{28,24},{1,5},{5... | collective-permute-start | bytes 1179656 | tf_op jit(solution)/shard_map/ppermute | solution.py:23
  34.7 2.3 %collective-permute-start.10 = (bf16[1536,128]{1,0:T(8,128)(2,1)S(1)}, bf16[1536,128]{1,0:T(8,128)(2,1)S(1)}, u32[]{:S(2)}, u32[]{:S(2)}) collective-permute-start(bf16[1536,128]{1,0:T(8,128)(2,1)S(1)} %collective-permute-done.6), channel_id=1, source_target_pairs={{0,4},{4,0},{8,12},{12,8},{16,20},{20,16},{24,28},{28,24},{1,5},{5... | collective-permute-start | bytes 1179656 | tf_op jit(solution)/shard_map/ppermute | solution.py:23
  37.0 14.1 %copy-start.1 = (bf16[512,512]{1,0:T(8,128)(2,1)S(1)}, bf16[512,512]{1,0:T(8,128)(2,1)}, u32[]{:S(2)}) copy-start(bf16[512,512]{1,0:T(8,128)(2,1)} %rest_4_.3) | copy-start | bytes 1572868
  38.6 8.9 %collective-permute-start.18 = (bf16[384,128]{1,0:T(8,128)(2,1)S(1)}, bf16[384,128]{1,0:T(8,128)(2,1)S(1)}, u32[]{:S(2)}, u32[]{:S(2)}) collective-permute-start(bf16[384,128]{1,0:T(8,128)(2,1)S(1)} %bitcast.38), channel_id=1, source_target_pairs={{0,1},{1,0},{2,3},{3,2},{4,5},{5,4},{6,7},{7,6},{8,9},{9,8},{10,11... | collective-permute-start | bytes 294920 | tf_op jit(solution)/shard_map/ppermute | solution.py:23
  40.4 10.7 %collective-permute-start.19 = (bf16[384,128]{1,0:T(8,128)(2,1)S(1)}, bf16[384,128]{1,0:T(8,128)(2,1)S(1)}, u32[]{:S(2)}, u32[]{:S(2)}) collective-permute-start(bf16[384,128]{1,0:T(8,128)(2,1)S(1)} %bitcast.37), channel_id=1, source_target_pairs={{0,2},{1,3},{2,0},{3,1},{4,6},{5,7},{6,4},{7,5},{8,10},{9,11},{10,... | collective-permute-start | bytes 294920 | tf_op jit(solution)/shard_map/ppermute | solution.py:23
  43.0 8.1 %collective-permute-start.20 = (bf16[384,128]{1,0:T(8,128)(2,1)S(1)}, bf16[384,128]{1,0:T(8,128)(2,1)S(1)}, u32[]{:S(2)}, u32[]{:S(2)}) collective-permute-start(bf16[384,128]{1,0:T(8,128)(2,1)S(1)} %bitcast.36), channel_id=1, source_target_pairs={{0,3},{1,2},{2,1},{3,0},{4,7},{5,6},{6,5},{7,4},{8,11},{9,10},{10,... | collective-permute-start | bytes 294920 | tf_op jit(solution)/shard_map/ppermute | solution.py:23
  43.1 16.8 %collective-permute-start.12 = (bf16[384,128]{1,0:T(8,128)(2,1)S(1)}, bf16[384,128]{1,0:T(8,128)(2,1)S(1)}, u32[]{:S(2)}, u32[]{:S(2)}) collective-permute-start(bf16[384,128]{1,0:T(8,128)(2,1)S(1)} %bitcast.35), channel_id=1, source_target_pairs={{0,1},{1,0},{2,3},{3,2},{4,5},{5,4},{6,7},{7,6},{8,9},{9,8},{10,11... | collective-permute-start | bytes 294920 | tf_op jit(solution)/shard_map/ppermute | solution.py:23
  44.0 17.2 %collective-permute-start.13 = (bf16[384,128]{1,0:T(8,128)(2,1)S(1)}, bf16[384,128]{1,0:T(8,128)(2,1)S(1)}, u32[]{:S(2)}, u32[]{:S(2)}) collective-permute-start(bf16[384,128]{1,0:T(8,128)(2,1)S(1)} %bitcast.34), channel_id=1, source_target_pairs={{0,2},{1,3},{2,0},{3,1},{4,6},{5,7},{6,4},{7,5},{8,10},{9,11},{10,... | collective-permute-start | bytes 294920 | tf_op jit(solution)/shard_map/ppermute | solution.py:23
  47.5 13.7 %collective-permute-start.14 = (bf16[384,128]{1,0:T(8,128)(2,1)S(1)}, bf16[384,128]{1,0:T(8,128)(2,1)S(1)}, u32[]{:S(2)}, u32[]{:S(2)}) collective-permute-start(bf16[384,128]{1,0:T(8,128)(2,1)S(1)} %bitcast.33), channel_id=1, source_target_pairs={{0,3},{1,2},{2,1},{3,0},{4,7},{5,6},{6,5},{7,4},{8,11},{9,10},{10,... | collective-permute-start | bytes 294920 | tf_op jit(solution)/shard_map/ppermute | solution.py:23
  51.7 16.3 %collective-permute-start.21 = (bf16[384,128]{1,0:T(8,128)(2,1)S(1)}, bf16[384,128]{1,0:T(8,128)(2,1)S(1)}, u32[]{:S(2)}, u32[]{:S(2)}) collective-permute-start(bf16[384,128]{1,0:T(8,128)(2,1)S(1)} %get-tuple-element.54), channel_id=1, source_target_pairs={{0,1},{1,0},{2,3},{3,2},{4,5},{5,4},{6,7},{7,6},{8,9},{9,8},{10,11... | collective-permute-start | bytes 294920 | tf_op jit(solution)/shard_map/ppermute | solution.py:23
  58.7 11.5 %collective-permute-start.22 = (bf16[384,128]{1,0:T(8,128)(2,1)S(1)}, bf16[384,128]{1,0:T(8,128)(2,1)S(1)}, u32[]{:S(2)}, u32[]{:S(2)}) collective-permute-start(bf16[384,128]{1,0:T(8,128)(2,1)S(1)} %get-tuple-element.55), channel_id=1, source_target_pairs={{0,2},{1,3},{2,0},{3,1},{4,6},{5,7},{6,4},{7,5},{8,10},{9,11},{10,... | collective-permute-start | bytes 294920 | tf_op jit(solution)/shard_map/ppermute | solution.py:23
  59.8 10.3 %collective-permute-start.23 = (bf16[384,128]{1,0:T(8,128)(2,1)S(1)}, bf16[384,128]{1,0:T(8,128)(2,1)S(1)}, u32[]{:S(2)}, u32[]{:S(2)}) collective-permute-start(bf16[384,128]{1,0:T(8,128)(2,1)S(1)} %get-tuple-element.56), channel_id=1, source_target_pairs={{0,3},{1,2},{2,1},{3,0},{4,7},{5,6},{6,5},{7,4},{8,11},{9,10},{10,... | collective-permute-start | bytes 294920 | tf_op jit(solution)/shard_map/ppermute | solution.py:23
  61.8 8.3 %collective-permute-start.15 = (bf16[384,128]{1,0:T(8,128)(2,1)S(1)}, bf16[384,128]{1,0:T(8,128)(2,1)S(1)}, u32[]{:S(2)}, u32[]{:S(2)}) collective-permute-start(bf16[384,128]{1,0:T(8,128)(2,1)S(1)} %get-tuple-element.46), channel_id=1, source_target_pairs={{0,1},{1,0},{2,3},{3,2},{4,5},{5,4},{6,7},{7,6},{8,9},{9,8},{10,11... | collective-permute-start | bytes 294920 | tf_op jit(solution)/shard_map/ppermute | solution.py:23
  65.5 11.0 %collective-permute-start.16 = (bf16[384,128]{1,0:T(8,128)(2,1)S(1)}, bf16[384,128]{1,0:T(8,128)(2,1)S(1)}, u32[]{:S(2)}, u32[]{:S(2)}) collective-permute-start(bf16[384,128]{1,0:T(8,128)(2,1)S(1)} %get-tuple-element.47), channel_id=1, source_target_pairs={{0,2},{1,3},{2,0},{3,1},{4,6},{5,7},{6,4},{7,5},{8,10},{9,11},{10,... | collective-permute-start | bytes 294920 | tf_op jit(solution)/shard_map/ppermute | solution.py:23
  68.0 8.5 %collective-permute-start.17 = (bf16[384,128]{1,0:T(8,128)(2,1)S(1)}, bf16[384,128]{1,0:T(8,128)(2,1)S(1)}, u32[]{:S(2)}, u32[]{:S(2)}) collective-permute-start(bf16[384,128]{1,0:T(8,128)(2,1)S(1)} %get-tuple-element.48), channel_id=1, source_target_pairs={{0,3},{1,2},{2,1},{3,0},{4,7},{5,6},{6,5},{7,4},{8,11},{9,10},{10,... | collective-permute-start | bytes 294920 | tf_op jit(solution)/shard_map/ppermute | solution.py:23

commit v5 on v4

--- a/solution.py
+++ b/solution.py
@@ -279,7 +279,9 @@
     biases = [flipped(own_bias, "feat", turn) for turn in (1, 2, 3)]
     beside, above, *biases = tie(beside, above, *biases)
     biases = [own_bias, *biases]
-    corner = [flipped(above[:half], "blk", 2), flipped(beside[half:], "blk", 4)]
+    low, high = above[:half], beside[half:]
+    beside, above, low, high = tie(beside, above, low, high)
+    corner = [flipped(low, "blk", 2), flipped(high, "blk", 4)]
     near = [beside, above, flipped(beside, "blk", 1), flipped(above, "blk", 1)]
     (totals,) = add_group(1, row_tiles, order, member, tile_values, near, totals)
     *corner, totals = tie(*corner, totals)

time: 77.6 us -> 77.6 us (level)
  transfers between devices with their start and end apart: 24 -> 24, of which waited for: 9 -> 9; matrix products, arithmetic and copies ran while one was open for 0% -> 0% of each run, Pallas kernels for 14% -> 13%
where the time goes in v5:
time: 77.6 us; the launch traced here: 77.4 us
  starting transfers between devices  38.9 us (50%)
  waiting for transfers between devices  22.8 us (29%)
  Pallas kernels  12.5 us (16%)
  local copies, waits for them, and re-layouts  2.97 us (4%)
    ppermute x24, starting transfers between devices, flipped(): return lax.ppermute(shard, axis, [(i, i ^ bits) for i in range(count)])  38.9 us
    ppermute x24, waiting for transfers between devices, flipped(): return lax.ppermute(shard, axis, [(i, i ^ bits) for i in range(count)])  22.8 us
    pallas_call x4, Pallas kernels, add_group(): pl.pallas_call(functools.partial(add_kernel, group, first, last, len(piec...  6.78 us
    pallas_call x1, Pallas kernels, plan(): pl.pallas_call(functools.partial(plan_kernel, row_tiles), out_shape=jax.S...  3.66 us
    unnamed x10, local copies, waits for them, and re-layouts  2.91 us
  transfers between devices with their start and end apart: 24, of which 9 were waited for; matrix products, arithmetic and copies ran while one was open for 0% of the time, Pallas kernels for 13%

profile of v5, /device:TPU:0, one launch (start us, length us, event | category | flops | bytes accessed | tf_op | source)
XLA Modules:
  0.0 77.4 jit_solution(199134835757775072)
XLA Ops:
  0.5 2.5 %collective-permute-start = (bf16[3072,128]{1,0:T(8,128)(2,1)}, bf16[3072,128]{1,0:T(8,128)(2,1)S(1)}, u32[]{:S(2)}, u32[]{:S(2)}) collective-permute-start(bf16[3072,128]{1,0:T(8,128)(2,1)} %param.8), channel_id=1, source_target_pairs={{0,8},{4,12},{8,0},{12,4},{16,24},{20,28},{24,16},{28,20},{1,9},{5... | collective-permute-start | bytes 2359304 | tf_op jit(solution)/shard_map/ppermute | solution.py:23
  2.9 1.5 %collective-permute-start.1 = (bf16[3072,128]{1,0:T(8,128)(2,1)}, bf16[3072,128]{1,0:T(8,128)(2,1)S(1)}, u32[]{:S(2)}, u32[]{:S(2)}) collective-permute-start(bf16[3072,128]{1,0:T(8,128)(2,1)} %param.8), channel_id=1, source_target_pairs={{0,16},{4,20},{8,24},{12,28},{16,0},{20,4},{24,8},{28,12},{1,17},{... | collective-permute-start | bytes 2359304 | tf_op jit(solution)/shard_map/ppermute | solution.py:23
  4.5 3.7 %plan.1.order = s32[4,4,144]{2,1,0:T(4,128)} custom-call(s32[128]{0:T(128)} %rows.1, s32[128]{0:T(128)} %cols.1, s32[8]{0:T(128)} %counts.1, s32[1]{0:T(128)} %bitcast.1.place, s32[192]{0:T(256)} %constant.11.clone.table), custom_call_target="tpu_custom_call" | custom-call | flops 1000000000 | bytes 1000 | tf_op jit(solution)/shard_map/plan/pallas_call | solution.py:122
  8.2 2.2 %copy-done = bf16[128,128,128]{2,1,0:T(8,128)(2,1)S(1)} copy-done((bf16[128,128,128]{2,1,0:T(8,128)(2,1)S(1)}, bf16[128,128,128]{2,1,0:T(8,128)(2,1)}, u32[]{:S(2)}) %copy-start) | copy-done | bytes 4194328
  10.4 0.7 copy-done.3
  11.1 1.3 %add_tiles.4.rest_4_ = f32[25,128,128]{2,1,0:T(8,128)S(1)} custom-call(s32[4,4,144]{2,1,0:T(4,128)S(1)} %copy-done.3, s32[1]{0:T(128)} %bitcast.member, bf16[128,128,128]{2,1,0:T(8,128)(2,1)S(1)} %copy-done, bf16[24,128,128]{2,1,0:T(8,128)(2,1)S(1)} %bitcast.23, bf16[24,128,128]{2,1,0:T(8,128)(2,1)S(1)} %bitcast.24), custom_call_target="tpu_custom_call" | custom-call | flops 1000000000 | bytes 1000 | tf_op jit(solution)/shard_map/add_tiles/pallas_call | solution.py:194
  12.4 1.6 %collective-permute-start.3 = (f32[1,128]{1,0:T(1,128)S(1)}, f32[1,128]{1,0:T(1,128)S(1)}, u32[]{:S(2)}, u32[]{:S(2)}) collective-permute-start(f32[1,128]{1,0:T(1,128)S(1)} %bitcast.39), channel_id=1, source_target_pairs={{0,1},{1,0},{2,3},{3,2},{4,5},{5,4},{6,7},{7,6},{8,9},{9,8},{10,11... | collective-permute-start | bytes 1544 | tf_op jit(solution)/shard_map/ppermute | solution.py:23
  14.1 2.6 %collective-permute-start.4 = (f32[1,128]{1,0:T(1,128)S(1)}, f32[1,128]{1,0:T(1,128)S(1)}, u32[]{:S(2)}, u32[]{:S(2)}) collective-permute-start(f32[1,128]{1,0:T(1,128)S(1)} %bitcast.40), channel_id=1, source_target_pairs={{0,2},{1,3},{2,0},{3,1},{4,6},{5,7},{6,4},{7,5},{8,10},{9,11},{10,... | collective-permute-start | bytes 1544 | tf_op jit(solution)/shard_map/ppermute | solution.py:23
  16.9 4.5 %collective-permute-done = bf16[3072,128]{1,0:T(8,128)(2,1)S(1)} collective-permute-done((bf16[3072,128]{1,0:T(8,128)(2,1)}, bf16[3072,128]{1,0:T(8,128)(2,1)S(1)}, u32[]{:S(2)}, u32[]{:S(2)}) %collective-permute-start) | collective-permute-done | bytes 786464 | tf_op jit(solution)/shard_map/ppermute | solution.py:23
  21.4 1.5 %collective-permute-done.1 = bf16[3072,128]{1,0:T(8,128)(2,1)S(1)} collective-permute-done((bf16[3072,128]{1,0:T(8,128)(2,1)}, bf16[3072,128]{1,0:T(8,128)(2,1)S(1)}, u32[]{:S(2)}, u32[]{:S(2)}) %collective-permute-start.1) | collective-permute-done | bytes 786464 | tf_op jit(solution)/shard_map/ppermute | solution.py:23
  23.8 1.7 %collective-permute-start.7 = (bf16[1536,128]{1,0:T(8,128)(2,1)S(1)}, bf16[1536,128]{1,0:T(8,128)(2,1)S(1)}, u32[]{:S(2)}, u32[]{:S(2)}) collective-permute-start(bf16[1536,128]{1,0:T(8,128)(2,1)S(1)} %slice.7), channel_id=1, source_target_pairs={{0,16},{4,20},{8,24},{12,28},{16,0},{20,4},{24,8},{28,12},{1,17},{... | collective-permute-start | bytes 1179656 | tf_op jit(solution)/shard_map/ppermute | solution.py:23
  25.5 0.8 %collective-permute-done.9 = bf16[3072,128]{1,0:T(8,128)(2,1)S(1)} collective-permute-done((bf16[3072,128]{1,0:T(8,128)(2,1)S(1)}, bf16[3072,128]{1,0:T(8,128)(2,1)S(1)}, u32[]{:S(2)}, u32[]{:S(2)}) %collective-permute-start.9) | collective-permute-done | bytes 786464 | tf_op jit(solution)/shard_map/ppermute | solution.py:23
  26.4 2.3 %add_tiles.5.rest_2_ = f32[25,128,128]{2,1,0:T(8,128)S(1)} custom-call(s32[4,4,144]{2,1,0:T(4,128)S(1)} %copy-done.3, s32[1]{0:T(128)} %bitcast.member, bf16[128,128,128]{2,1,0:T(8,128)(2,1)S(1)} %copy-done, bf16[24,128,128]{2,1,0:T(8,128)(2,1)S(1)} %bitcast.21, bf16[24,128,128]{2,1,0:T(8,128)(2,1)S(1)} %bitcast.22, ...), custom_call_target="tpu_custom_call", output_to_operand_aliasing={{}: (7, {})} | custom-call | flops 1000000000 | bytes 1000 | tf_op jit(solution)/shard_map/add_tiles/pallas_call | solution.py:194
  28.7 5.9 %collective-permute-done.6 = bf16[1536,128]{1,0:T(8,128)(2,1)S(1)} collective-permute-done((bf16[1536,128]{1,0:T(8,128)(2,1)S(1)}, bf16[1536,128]{1,0:T(8,128)(2,1)S(1)}, u32[]{:S(2)}, u32[]{:S(2)}) %collective-permute-start.6) | collective-permute-done | bytes 393248 | tf_op jit(solution)/shard_map/ppermute | solution.py:23
  35.2 1.5 %add_tiles.6.rest_2_ = f32[25,128,128]{2,1,0:T(8,128)S(1)} custom-call(s32[4,4,144]{2,1,0:T(4,128)S(1)} %copy-done.3, s32[1]{0:T(128)} %bitcast.member, bf16[128,128,128]{2,1,0:T(8,128)(2,1)S(1)} %copy-done, bf16[12,128,128]{2,1,0:T(8,128)(2,1)S(1)} %bitcast.27, bf16[12,128,128]{2,1,0:T(8,128)(2,1)S(1)} %bitcast.28, ...), custom_call_target="tpu_custom_call", output_to_operand_aliasing={{}: (5, {})} | custom-call | flops 1000000000 | bytes 1000 | tf_op jit(solution)/shard_map/add_tiles/pallas_call | solution.py:194
  36.9 1.6 %add_tiles.7 = (bf16[3,128,128]{2,1,0:T(8,128)(2,1)S(1)}, bf16[3,128,128]{2,1,0:T(8,128)(2,1)S(1)}, bf16[3,128,128]{2,1,0:T(8,128)(2,1)S(1)}, bf16[3,128,128]{2,...) custom-call(s32[4,4,144]{2,1,0:T(4,128)S(1)} %copy-done.3, ...), custom_call_target="tpu_custom_call", output_to_operand_aliasing={{8}: (5, {})} | custom-call | flops 1000000000 | bytes 1000 | tf_op jit(solution)/shard_map/add_tiles/pallas_call | solution.py:194
  38.5 1.8 %collective-permute-start.12 = (bf16[384,128]{1,0:T(8,128)(2,1)S(1)}, bf16[384,128]{1,0:T(8,128)(2,1)S(1)}, u32[]{:S(2)}, u32[]{:S(2)}) collective-permute-start(bf16[384,128]{1,0:T(8,128)(2,1)S(1)} %bitcast.38), channel_id=1, source_target_pairs={{0,1},{1,0},{2,3},{3,2},{4,5},{5,4},{6,7},{7,6},{8,9},{9,8},{10,11... | collective-permute-start | bytes 294920 | tf_op jit(solution)/shard_map/ppermute | solution.py:23
  40.4 2.6 %collective-permute-start.13 = (bf16[384,128]{1,0:T(8,128)(2,1)S(1)}, bf16[384,128]{1,0:T(8,128)(2,1)S(1)}, u32[]{:S(2)}, u32[]{:S(2)}) collective-permute-start(bf16[384,128]{1,0:T(8,128)(2,1)S(1)} %bitcast.37), channel_id=1, source_target_pairs={{0,2},{1,3},{2,0},{3,1},{4,6},{5,7},{6,4},{7,5},{8,10},{9,11},{10,... | collective-permute-start | bytes 294920 | tf_op jit(solution)/shard_map/ppermute | solution.py:23
  43.0 0.9 %collective-permute-start.18 = (bf16[384,128]{1,0:T(8,128)(2,1)S(1)}, bf16[384,128]{1,0:T(8,128)(2,1)S(1)}, u32[]{:S(2)}, u32[]{:S(2)}) collective-permute-start(bf16[384,128]{1,0:T(8,128)(2,1)S(1)} %bitcast.35), channel_id=1, source_target_pairs={{0,1},{1,0},{2,3},{3,2},{4,5},{5,4},{6,7},{7,6},{8,9},{9,8},{10,11... | collective-permute-start | bytes 294920 | tf_op jit(solution)/shard_map/ppermute | solution.py:23
  43.9 3.5 %collective-permute-start.19 = (bf16[384,128]{1,0:T(8,128)(2,1)S(1)}, bf16[384,128]{1,0:T(8,128)(2,1)S(1)}, u32[]{:S(2)}, u32[]{:S(2)}) collective-permute-start(bf16[384,128]{1,0:T(8,128)(2,1)S(1)} %bitcast.34), channel_id=1, source_target_pairs={{0,2},{1,3},{2,0},{3,1},{4,6},{5,7},{6,4},{7,5},{8,10},{9,11},{10,... | collective-permute-start | bytes 294920 | tf_op jit(solution)/shard_map/ppermute | solution.py:23
  47.4 0.9 %collective-permute-start.20 = (bf16[384,128]{1,0:T(8,128)(2,1)S(1)}, bf16[384,128]{1,0:T(8,128)(2,1)S(1)}, u32[]{:S(2)}, u32[]{:S(2)}) collective-permute-start(bf16[384,128]{1,0:T(8,128)(2,1)S(1)} %bitcast.33), channel_id=1, source_target_pairs={{0,3},{1,2},{2,1},{3,0},{4,7},{5,6},{6,5},{7,4},{8,11},{9,10},{10,... | collective-permute-start | bytes 294920 | tf_op jit(solution)/shard_map/ppermute | solution.py:23
  48.3 2.8 %collective-permute-done.13.rest_2_ = bf16[384,128]{1,0:T(8,128)(2,1)S(1)} collective-permute-done((bf16[384,128]{1,0:T(8,128)(2,1)S(1)}, bf16[384,128]{1,0:T(8,128)(2,1)S(1)}, u32[]{:S(2)}, u32[]{:S(2)}) %collective-permute-start.13) | collective-permute-done | bytes 98336 | tf_op jit(solution)/shard_map/ppermute | solution.py:23
  51.1 0.6 mix.2
  51.6 7.0 %collective-permute-start.15 = (bf16[384,128]{1,0:T(8,128)(2,1)S(1)}, bf16[384,128]{1,0:T(8,128)(2,1)S(1)}, u32[]{:S(2)}, u32[]{:S(2)}) collective-permute-start(bf16[384,128]{1,0:T(8,128)(2,1)S(1)} %get-tuple-element.54), channel_id=1, source_target_pairs={{0,1},{1,0},{2,3},{3,2},{4,5},{5,4},{6,7},{7,6},{8,9},{9,8},{10,11... | collective-permute-start | bytes 294920 | tf_op jit(solution)/shard_map/ppermute | solution.py:23
  58.6 1.1 %collective-permute-start.16 = (bf16[384,128]{1,0:T(8,128)(2,1)S(1)}, bf16[384,128]{1,0:T(8,128)(2,1)S(1)}, u32[]{:S(2)}, u32[]{:S(2)}) collective-permute-start(bf16[384,128]{1,0:T(8,128)(2,1)S(1)} %get-tuple-element.55), channel_id=1, source_target_pairs={{0,2},{1,3},{2,0},{3,1},{4,6},{5,7},{6,4},{7,5},{8,10},{9,11},{10,... | collective-permute-start | bytes 294920 | tf_op jit(solution)/shard_map/ppermute | solution.py:23
  59.8 1.4 %collective-permute-start.17 = (bf16[384,128]{1,0:T(8,128)(2,1)S(1)}, bf16[384,128]{1,0:T(8,128)(2,1)S(1)}, u32[]{:S(2)}, u32[]{:S(2)}) collective-permute-start(bf16[384,128]{1,0:T(8,128)(2,1)S(1)} %get-tuple-element.56), channel_id=1, source_target_pairs={{0,3},{1,2},{2,1},{3,0},{4,7},{5,6},{6,5},{7,4},{8,11},{9,10},{10,... | collective-permute-start | bytes 294920 | tf_op jit(solution)/shard_map/ppermute | solution.py:23
  61.8 3.7 %collective-permute-start.21 = (bf16[384,128]{1,0:T(8,128)(2,1)S(1)}, bf16[384,128]{1,0:T(8,128)(2,1)S(1)}, u32[]{:S(2)}, u32[]{:S(2)}) collective-permute-start(bf16[384,128]{1,0:T(8,128)(2,1)S(1)} %get-tuple-element.62), channel_id=1, source_target_pairs={{0,1},{1,0},{2,3},{3,2},{4,5},{5,4},{6,7},{7,6},{8,9},{9,8},{10,11... | collective-permute-start | bytes 294920 | tf_op jit(solution)/shard_map/ppermute | solution.py:23
  65.4 2.5 %collective-permute-start.22 = (bf16[384,128]{1,0:T(8,128)(2,1)S(1)}, bf16[384,128]{1,0:T(8,128)(2,1)S(1)}, u32[]{:S(2)}, u32[]{:S(2)}) collective-permute-start(bf16[384,128]{1,0:T(8,128)(2,1)S(1)} %get-tuple-element.63), channel_id=1, source_target_pairs={{0,2},{1,3},{2,0},{3,1},{4,6},{5,7},{6,4},{7,5},{8,10},{9,11},{10,... | collective-permute-start | bytes 294920 | tf_op jit(solution)/shard_map/ppermute | solution.py:23
  67.9 1.4 %collective-permute-start.23 = (bf16[384,128]{1,0:T(8,128)(2,1)S(1)}, bf16[384,128]{1,0:T(8,128)(2,1)S(1)}, u32[]{:S(2)}, u32[]{:S(2)}) collective-permute-start(bf16[384,128]{1,0:T(8,128)(2,1)S(1)} %get-tuple-element.64), channel_id=1, source_target_pairs={{0,3},{1,2},{2,1},{3,0},{4,7},{5,6},{6,5},{7,4},{8,11},{9,10},{10,... | collective-permute-start | bytes 294920 | tf_op jit(solution)/shard_map/ppermute | solution.py:23
  69.3 0.8 collective-permute-done.16.rest_2_
  70.1 6.3 %collective-permute-done.22.rest_6_ = bf16[384,128]{1,0:T(8,128)(2,1)S(1)} collective-permute-done((bf16[384,128]{1,0:T(8,128)(2,1)S(1)}, bf16[384,128]{1,0:T(8,128)(2,1)S(1)}, u32[]{:S(2)}, u32[]{:S(2)}) %collective-permute-start.22) | collective-permute-done | bytes 98336 | tf_op jit(solution)/shard_map/ppermute | solution.py:23
  76.4 0.9 %join.1 = bf16[3072,128]{1,0:T(8,128)(2,1)} custom-call(s32[1]{0:T(128)} %bitcast.member, bf16[384,128]{1,0:T(8,128)(2,1)S(1)} %get-tuple-element.53.rest_0_, bf16[384,128]{1,0:T(8,128)(2,1)S(1)} %collective-permute-done.15.rest_1_, bf16[384,128]{1,0:T(8,128)(2,1)S(1)} %collective-permute-done.16.rest_2_, ...), custom_call_target="tpu_custom_call" | custom-call | flops 1000 | bytes 1000 | tf_op jit(solution)/shard_map/join/pallas_call | solution.py:255
  (37 shorter events, 3.1 us)
Async XLA Ops:
  0.0 8.1 %collective-permute-start.2 = (bf16[3072,128]{1,0:T(8,128)(2,1)}, bf16[3072,128]{1,0:T(8,128)(2,1)S(1)}, u32[]{:S(2)}, u32[]{:S(2)}) collective-permute-start(bf16[3072,128]{1,0:T(8,128)(2,1)} %param.8), channel_id=1, source_target_pairs={{0,4},{4,0},{8,12},{12,8},{16,20},{20,16},{24,28},{28,24},{1,5},{5... | collective-permute-start | bytes 2359304 | tf_op jit(solution)/shard_map/ppermute | solution.py:23
  0.5 20.9 %collective-permute-start = (bf16[3072,128]{1,0:T(8,128)(2,1)}, bf16[3072,128]{1,0:T(8,128)(2,1)S(1)}, u32[]{:S(2)}, u32[]{:S(2)}) collective-permute-start(bf16[3072,128]{1,0:T(8,128)(2,1)} %param.8), channel_id=1, source_target_pairs={{0,8},{4,12},{8,0},{12,4},{16,24},{20,28},{24,16},{28,20},{1,9},{5... | collective-permute-start | bytes 2359304 | tf_op jit(solution)/shard_map/ppermute | solution.py:23
  2.9 19.9 %collective-permute-start.1 = (bf16[3072,128]{1,0:T(8,128)(2,1)}, bf16[3072,128]{1,0:T(8,128)(2,1)S(1)}, u32[]{:S(2)}, u32[]{:S(2)}) collective-permute-start(bf16[3072,128]{1,0:T(8,128)(2,1)} %param.8), channel_id=1, source_target_pairs={{0,16},{4,20},{8,24},{12,28},{16,0},{20,4},{24,8},{28,12},{1,17},{... | collective-permute-start | bytes 2359304 | tf_op jit(solution)/shard_map/ppermute | solution.py:23
  4.5 3.7 %copy-start.2 = (bf16[3072,128]{1,0:T(8,128)(2,1)S(1)}, bf16[3072,128]{1,0:T(8,128)(2,1)}, u32[]{:S(2)}) copy-start(bf16[3072,128]{1,0:T(8,128)(2,1)} %param.8) | copy-start | bytes 2359300
  8.2 2.2 %copy-start = (bf16[128,128,128]{2,1,0:T(8,128)(2,1)S(1)}, bf16[128,128,128]{2,1,0:T(8,128)(2,1)}, u32[]{:S(2)}) copy-start(bf16[128,128,128]{2,1,0:T(8,128)(2,1)} %values.7) | copy-start | bytes 12582916
  10.3 0.7 copy-start.3
  11.1 1.4 %copy-start.4 = (f32[128]{0:T(128)S(1)}, f32[128]{0:T(128)}, u32[]{:S(2)}) copy-start(f32[128]{0:T(128)} %param.14) | copy-start | bytes 1540
  12.4 10.4 %collective-permute-start.3 = (f32[1,128]{1,0:T(1,128)S(1)}, f32[1,128]{1,0:T(1,128)S(1)}, u32[]{:S(2)}, u32[]{:S(2)}) collective-permute-start(f32[1,128]{1,0:T(1,128)S(1)} %bitcast.39), channel_id=1, source_target_pairs={{0,1},{1,0},{2,3},{3,2},{4,5},{5,4},{6,7},{7,6},{8,9},{9,8},{10,11... | collective-permute-start | bytes 1544 | tf_op jit(solution)/shard_map/ppermute | solution.py:23
  14.1 8.8 %collective-permute-start.4 = (f32[1,128]{1,0:T(1,128)S(1)}, f32[1,128]{1,0:T(1,128)S(1)}, u32[]{:S(2)}, u32[]{:S(2)}) collective-permute-start(f32[1,128]{1,0:T(1,128)S(1)} %bitcast.40), channel_id=1, source_target_pairs={{0,2},{1,3},{2,0},{3,1},{4,6},{5,7},{6,4},{7,5},{8,10},{9,11},{10,... | collective-permute-start | bytes 1544 | tf_op jit(solution)/shard_map/ppermute | solution.py:23
  16.7 6.2 %collective-permute-start.5 = (f32[1,128]{1,0:T(1,128)S(1)}, f32[1,128]{1,0:T(1,128)S(1)}, u32[]{:S(2)}, u32[]{:S(2)}) collective-permute-start(f32[1,128]{1,0:T(1,128)S(1)} %bitcast.41), channel_id=1, source_target_pairs={{0,3},{1,2},{2,1},{3,0},{4,7},{5,6},{6,5},{7,4},{8,11},{9,10},{10,... | collective-permute-start | bytes 1544 | tf_op jit(solution)/shard_map/ppermute | solution.py:23
  22.9 2.6 %collective-permute-start.8 = (bf16[3072,128]{1,0:T(8,128)(2,1)S(1)}, bf16[3072,128]{1,0:T(8,128)(2,1)S(1)}, u32[]{:S(2)}, u32[]{:S(2)}) collective-permute-start(bf16[3072,128]{1,0:T(8,128)(2,1)S(1)} %collective-permute-done), channel_id=1, source_target_pairs={{0,4},{4,0},{8,12},{12,8},{16,20},{20,16},{24,28},{28,24},{1,5},{5... | collective-permute-start | bytes 2359304 | tf_op jit(solution)/shard_map/ppermute | solution.py:23
  23.0 3.4 %collective-permute-start.9 = (bf16[3072,128]{1,0:T(8,128)(2,1)S(1)}, bf16[3072,128]{1,0:T(8,128)(2,1)S(1)}, u32[]{:S(2)}, u32[]{:S(2)}) collective-permute-start(bf16[3072,128]{1,0:T(8,128)(2,1)S(1)} %collective-permute-done.1), channel_id=1, source_target_pairs={{0,4},{4,0},{8,12},{12,8},{16,20},{20,16},{24,28},{28,24},{1,5},{5... | collective-permute-start | bytes 2359304 | tf_op jit(solution)/shard_map/ppermute | solution.py:23
  23.5 11.1 %collective-permute-start.6 = (bf16[1536,128]{1,0:T(8,128)(2,1)S(1)}, bf16[1536,128]{1,0:T(8,128)(2,1)S(1)}, u32[]{:S(2)}, u32[]{:S(2)}) collective-permute-start(bf16[1536,128]{1,0:T(8,128)(2,1)S(1)} %slice.6), channel_id=1, source_target_pairs={{0,8},{4,12},{8,0},{12,4},{16,24},{20,28},{24,16},{28,20},{1,9},{5... | collective-permute-start | bytes 1179656 | tf_op jit(solution)/shard_map/ppermute | solution.py:23
  23.8 10.8 %collective-permute-start.7 = (bf16[1536,128]{1,0:T(8,128)(2,1)S(1)}, bf16[1536,128]{1,0:T(8,128)(2,1)S(1)}, u32[]{:S(2)}, u32[]{:S(2)}) collective-permute-start(bf16[1536,128]{1,0:T(8,128)(2,1)S(1)} %slice.7), channel_id=1, source_target_pairs={{0,16},{4,20},{8,24},{12,28},{16,0},{20,4},{24,8},{28,12},{1,17},{... | collective-permute-start | bytes 1179656 | tf_op jit(solution)/shard_map/ppermute | solution.py:23
  34.6 2.0 %collective-permute-start.10 = (bf16[1536,128]{1,0:T(8,128)(2,1)S(1)}, bf16[1536,128]{1,0:T(8,128)(2,1)S(1)}, u32[]{:S(2)}, u32[]{:S(2)}) collective-permute-start(bf16[1536,128]{1,0:T(8,128)(2,1)S(1)} %collective-permute-done.6), channel_id=1, source_target_pairs={{0,4},{4,0},{8,12},{12,8},{16,20},{20,16},{24,28},{28,24},{1,5},{5... | collective-permute-start | bytes 1179656 | tf_op jit(solution)/shard_map/ppermute | solution.py:23
  34.7 2.3 %collective-permute-start.11 = (bf16[1536,128]{1,0:T(8,128)(2,1)S(1)}, bf16[1536,128]{1,0:T(8,128)(2,1)S(1)}, u32[]{:S(2)}, u32[]{:S(2)}) collective-permute-start(bf16[1536,128]{1,0:T(8,128)(2,1)S(1)} %collective-permute-done.7), channel_id=1, source_target_pairs={{0,4},{4,0},{8,12},{12,8},{16,20},{20,16},{24,28},{28,24},{1,5},{5... | collective-permute-start | bytes 1179656 | tf_op jit(solution)/shard_map/ppermute | solution.py:23
  36.9 14.1 %copy-start.1 = (bf16[512,512]{1,0:T(8,128)(2,1)S(1)}, bf16[512,512]{1,0:T(8,128)(2,1)}, u32[]{:S(2)}) copy-start(bf16[512,512]{1,0:T(8,128)(2,1)} %rest_4_.3) | copy-start | bytes 1572868
  38.5 8.9 %collective-permute-start.12 = (bf16[384,128]{1,0:T(8,128)(2,1)S(1)}, bf16[384,128]{1,0:T(8,128)(2,1)S(1)}, u32[]{:S(2)}, u32[]{:S(2)}) collective-permute-start(bf16[384,128]{1,0:T(8,128)(2,1)S(1)} %bitcast.38), channel_id=1, source_target_pairs={{0,1},{1,0},{2,3},{3,2},{4,5},{5,4},{6,7},{7,6},{8,9},{9,8},{10,11... | collective-permute-start | bytes 294920 | tf_op jit(solution)/shard_map/ppermute | solution.py:23
  40.4 10.7 %collective-permute-start.13 = (bf16[384,128]{1,0:T(8,128)(2,1)S(1)}, bf16[384,128]{1,0:T(8,128)(2,1)S(1)}, u32[]{:S(2)}, u32[]{:S(2)}) collective-permute-start(bf16[384,128]{1,0:T(8,128)(2,1)S(1)} %bitcast.37), channel_id=1, source_target_pairs={{0,2},{1,3},{2,0},{3,1},{4,6},{5,7},{6,4},{7,5},{8,10},{9,11},{10,... | collective-permute-start | bytes 294920 | tf_op jit(solution)/shard_map/ppermute | solution.py:23
  43.0 8.1 %collective-permute-start.14 = (bf16[384,128]{1,0:T(8,128)(2,1)S(1)}, bf16[384,128]{1,0:T(8,128)(2,1)S(1)}, u32[]{:S(2)}, u32[]{:S(2)}) collective-permute-start(bf16[384,128]{1,0:T(8,128)(2,1)S(1)} %bitcast.36), channel_id=1, source_target_pairs={{0,3},{1,2},{2,1},{3,0},{4,7},{5,6},{6,5},{7,4},{8,11},{9,10},{10,... | collective-permute-start | bytes 294920 | tf_op jit(solution)/shard_map/ppermute | solution.py:23
  43.0 16.8 %collective-permute-start.18 = (bf16[384,128]{1,0:T(8,128)(2,1)S(1)}, bf16[384,128]{1,0:T(8,128)(2,1)S(1)}, u32[]{:S(2)}, u32[]{:S(2)}) collective-permute-start(bf16[384,128]{1,0:T(8,128)(2,1)S(1)} %bitcast.35), channel_id=1, source_target_pairs={{0,1},{1,0},{2,3},{3,2},{4,5},{5,4},{6,7},{7,6},{8,9},{9,8},{10,11... | collective-permute-start | bytes 294920 | tf_op jit(solution)/shard_map/ppermute | solution.py:23
  43.9 17.2 %collective-permute-start.19 = (bf16[384,128]{1,0:T(8,128)(2,1)S(1)}, bf16[384,128]{1,0:T(8,128)(2,1)S(1)}, u32[]{:S(2)}, u32[]{:S(2)}) collective-permute-start(bf16[384,128]{1,0:T(8,128)(2,1)S(1)} %bitcast.34), channel_id=1, source_target_pairs={{0,2},{1,3},{2,0},{3,1},{4,6},{5,7},{6,4},{7,5},{8,10},{9,11},{10,... | collective-permute-start | bytes 294920 | tf_op jit(solution)/shard_map/ppermute | solution.py:23
  47.4 13.8 %collective-permute-start.20 = (bf16[384,128]{1,0:T(8,128)(2,1)S(1)}, bf16[384,128]{1,0:T(8,128)(2,1)S(1)}, u32[]{:S(2)}, u32[]{:S(2)}) collective-permute-start(bf16[384,128]{1,0:T(8,128)(2,1)S(1)} %bitcast.33), channel_id=1, source_target_pairs={{0,3},{1,2},{2,1},{3,0},{4,7},{5,6},{6,5},{7,4},{8,11},{9,10},{10,... | collective-permute-start | bytes 294920 | tf_op jit(solution)/shard_map/ppermute | solution.py:23
  51.6 16.3 %collective-permute-start.15 = (bf16[384,128]{1,0:T(8,128)(2,1)S(1)}, bf16[384,128]{1,0:T(8,128)(2,1)S(1)}, u32[]{:S(2)}, u32[]{:S(2)}) collective-permute-start(bf16[384,128]{1,0:T(8,128)(2,1)S(1)} %get-tuple-element.54), channel_id=1, source_target_pairs={{0,1},{1,0},{2,3},{3,2},{4,5},{5,4},{6,7},{7,6},{8,9},{9,8},{10,11... | collective-permute-start | bytes 294920 | tf_op jit(solution)/shard_map/ppermute | solution.py:23
  58.6 11.5 %collective-permute-start.16 = (bf16[384,128]{1,0:T(8,128)(2,1)S(1)}, bf16[384,128]{1,0:T(8,128)(2,1)S(1)}, u32[]{:S(2)}, u32[]{:S(2)}) collective-permute-start(bf16[384,128]{1,0:T(8,128)(2,1)S(1)} %get-tuple-element.55), channel_id=1, source_target_pairs={{0,2},{1,3},{2,0},{3,1},{4,6},{5,7},{6,4},{7,5},{8,10},{9,11},{10,... | collective-permute-start | bytes 294920 | tf_op jit(solution)/shard_map/ppermute | solution.py:23
  59.8 10.3 %collective-permute-start.17 = (bf16[384,128]{1,0:T(8,128)(2,1)S(1)}, bf16[384,128]{1,0:T(8,128)(2,1)S(1)}, u32[]{:S(2)}, u32[]{:S(2)}) collective-permute-start(bf16[384,128]{1,0:T(8,128)(2,1)S(1)} %get-tuple-element.56), channel_id=1, source_target_pairs={{0,3},{1,2},{2,1},{3,0},{4,7},{5,6},{6,5},{7,4},{8,11},{9,10},{10,... | collective-permute-start | bytes 294920 | tf_op jit(solution)/shard_map/ppermute | solution.py:23
  61.8 8.3 %collective-permute-start.21 = (bf16[384,128]{1,0:T(8,128)(2,1)S(1)}, bf16[384,128]{1,0:T(8,128)(2,1)S(1)}, u32[]{:S(2)}, u32[]{:S(2)}) collective-permute-start(bf16[384,128]{1,0:T(8,128)(2,1)S(1)} %get-tuple-element.62), channel_id=1, source_target_pairs={{0,1},{1,0},{2,3},{3,2},{4,5},{5,4},{6,7},{7,6},{8,9},{9,8},{10,11... | collective-permute-start | bytes 294920 | tf_op jit(solution)/shard_map/ppermute | solution.py:23
  65.4 11.0 %collective-permute-start.22 = (bf16[384,128]{1,0:T(8,128)(2,1)S(1)}, bf16[384,128]{1,0:T(8,128)(2,1)S(1)}, u32[]{:S(2)}, u32[]{:S(2)}) collective-permute-start(bf16[384,128]{1,0:T(8,128)(2,1)S(1)} %get-tuple-element.63), channel_id=1, source_target_pairs={{0,2},{1,3},{2,0},{3,1},{4,6},{5,7},{6,4},{7,5},{8,10},{9,11},{10,... | collective-permute-start | bytes 294920 | tf_op jit(solution)/shard_map/ppermute | solution.py:23
  67.9 8.5 %collective-permute-start.23 = (bf16[384,128]{1,0:T(8,128)(2,1)S(1)}, bf16[384,128]{1,0:T(8,128)(2,1)S(1)}, u32[]{:S(2)}, u32[]{:S(2)}) collective-permute-start(bf16[384,128]{1,0:T(8,128)(2,1)S(1)} %get-tuple-element.64), channel_id=1, source_target_pairs={{0,3},{1,2},{2,1},{3,0},{4,7},{5,6},{6,5},{7,4},{8,11},{9,10},{10,... | collective-permute-start | bytes 294920 | tf_op jit(solution)/shard_map/ppermute | solution.py:23
